TPU v7x, 32 devices: a whole 2x2x4 slice. The times are simulated.
32 devices in a mesh: row: 8 (over z, core), col: 4 (over y, x).
Axes of the slice: x: 2, y: 2, z: 4, core: 2. Of those that a mesh axis runs over, the one named last changes fastest.
Arguments:
- queries: bfloat16 [256, 32, 1536], P('row', 'col'), may hold values from -24 to 24
- keys: bfloat16 [256, 32, 1536], P('row', 'col'), may hold values from -24 to 24
- values: bfloat16 [256, 32, 1536], P('row', 'col'), may hold values from -12 to 12
- memory_bias: float32 [12], replicated, may hold values from 1 to 6
Outputs:
- attended: bfloat16 [256, 32, 1536], P('row', 'col')
All inputs are finite; a program needn't handle non-finite values.
Results may differ from a plain program's by a relative error of at most 0.0048.
Values may be sent and summed in bfloat16 or wider, within the bound.
No kernel may reach another device: no remote copies, remote signals or barrier semaphores. Data moves between devices by JAX's collectives and lax.ppermute only.
A program may use at most 64 MiB of HBM per device.

v0:
```python
import math

import jax
import jax.numpy as jnp
from jax import lax
from jax.sharding import PartitionSpec as P


def per_device(queries, keys, values, memory_bias):
    row_dev, col_dev, model_width = queries.shape
    n_row = lax.axis_size("row")
    n_col = lax.axis_size("col")
    head_count = memory_bias.shape[0]
    head_dim = model_width // head_count
    pair_count = col_dev * head_count // n_row
    total_rows = row_dev * n_row
    score_scale = 1.0 / math.sqrt(head_dim)

    def to_pairs(tokens_in):
        split_heads = tokens_in.reshape(row_dev, col_dev, head_count, head_dim)
        return jnp.transpose(split_heads, (1, 2, 0, 3)).reshape(
            col_dev * head_count, row_dev, head_dim
        )

    own_keys = jnp.mean(keys, axis=(0, 1), dtype=jnp.float32).astype(jnp.bfloat16)
    own_values = jnp.mean(values, axis=(0, 1), dtype=jnp.float32).astype(jnp.bfloat16)
    summary = jnp.stack([own_keys, own_values])[None]
    pair_ids = lax.axis_index("row") * pair_count + jnp.arange(pair_count, dtype=jnp.int32)
    selector = (
        pair_ids[:, None] % head_count == jnp.arange(head_count, dtype=jnp.int32)[None, :]
    ).astype(jnp.float32)
    bias_pairs = jnp.sum(selector * memory_bias[None, :], axis=1)
    all_slots = lax.all_gather(summary, ("row", "col"), axis=0, tiled=True).reshape(
        n_row, n_col, 2, head_count, head_dim
    )
    query_cols, key_rows, value_rows = (
        lax.all_to_all(to_pairs(queries), "row", split_axis=0, concat_axis=1, tiled=True),
        lax.all_to_all(to_pairs(keys), "row", split_axis=0, concat_axis=1, tiled=True),
        lax.all_to_all(to_pairs(values), "row", split_axis=0, concat_axis=1, tiled=True),
    )
    picker = selector.astype(jnp.bfloat16)
    mem_keys = jnp.einsum(
        "ph,bnhe->pbne", picker, all_slots[:, :, 0], preferred_element_type=jnp.float32
    ).astype(jnp.bfloat16)
    mem_values = jnp.einsum(
        "ph,bnhe->pbne", picker, all_slots[:, :, 1], preferred_element_type=jnp.float32
    ).astype(jnp.bfloat16)

    def attend(item):
        query_one, key_one, value_one, mem_key_one, mem_value_one, bias_one = item
        col_scores = (
            jnp.einsum("re,se->rs", query_one, key_one, preferred_element_type=jnp.float32)
            * score_scale
        )
        query_band = query_one.reshape(n_row, row_dev, head_dim)
        mem_scores = jnp.einsum(
            "bre,bne->brn", query_band, mem_key_one, preferred_element_type=jnp.float32
        )
        mem_scores = mem_scores.reshape(total_rows, n_col) * score_scale + bias_one
        peak_score = jnp.maximum(
            jnp.max(col_scores, axis=-1, keepdims=True), jnp.max(mem_scores, axis=-1, keepdims=True)
        )
        col_exp = jnp.exp(col_scores - peak_score)
        mem_exp = jnp.exp(mem_scores - peak_score)
        total_weight = jnp.sum(col_exp, axis=-1, keepdims=True) + jnp.sum(
            mem_exp, axis=-1, keepdims=True
        )
        col_weights = (col_exp / total_weight).astype(jnp.bfloat16)
        mem_weights = (mem_exp / total_weight).astype(jnp.bfloat16).reshape(n_row, row_dev, n_col)
        mixed = jnp.dot(col_weights, value_one, preferred_element_type=jnp.float32)
        mixed = mixed + jnp.einsum(
            "brn,bne->bre", mem_weights, mem_value_one, preferred_element_type=jnp.float32
        ).reshape(total_rows, head_dim)
        return mixed.astype(jnp.bfloat16)

    attended_cols = lax.map(
        attend, (query_cols, key_rows, value_rows, mem_keys, mem_values, bias_pairs)
    )
    returned = lax.all_to_all(attended_cols, "row", split_axis=1, concat_axis=0, tiled=True)
    returned = returned.reshape(col_dev, head_count, row_dev, head_dim)
    return jnp.transpose(returned, (2, 0, 1, 3)).reshape(row_dev, col_dev, model_width)


def solution(mesh):
    return jax.shard_map(
        per_device,
        mesh=mesh,
        in_specs=(P("row", "col", None), P("row", "col", None), P("row", "col", None), P()),
        out_specs=P("row", "col", None),
        check_vma=False,
    )
```

profile of v0, /device:TPU:0, one launch (start us, length us, event | category | flops | bytes accessed | tf_op | source)
XLA Modules:
  0.0 220.4 jit_solution(9912349975866750605)
XLA Ops:
  0.0 2.3 %copy.22 = bf16[8,12,32,128]{3,2,1,0:T(8,128)(2,1)} copy(bf16[8,12,32,128]{3,0,1,2:T(8,128)(2,1)} %bitcast.106) | data formatting | bytes 1572864 | tf_op jit(solution)/shard_map/transpose | solution.py:21
  2.3 6.5 %all-to-all-start = ((bf16[96,32,128]{2,1,0:T(8,128)(2,1)}), bf16[96,32,128]{2,1,0:T(8,128)(2,1)S(1)}, u32[]{:S(2)}, u32[]{:S(2)}) async-start(bf16[96,32,128]{2,1,0:T(8,128)(2,1)} %bitcast.11), calls=%async_computation | async-start | bytes 1572864 | tf_op jit(solution)/shard_map/all_to_all | solution.py:37
  8.8 1.2 copy.24
  10.0 19.8 %all-to-all-done = bf16[96,32,128]{2,1,0:T(8,128)(2,1)S(1)} async-done(((bf16[96,32,128]{2,1,0:T(8,128)(2,1)}), bf16[96,32,128]{2,1,0:T(8,128)(2,1)S(1)}, u32[]{:S(2)}, u32[]{:S(2)}) %all-to-all-start) | async-done | bytes 786464 | tf_op jit(solution)/shard_map/all_to_all | solution.py:37
  29.8 3.7 %all-to-all-start.1 = ((bf16[96,32,128]{2,1,0:T(8,128)(2,1)}), bf16[96,32,128]{2,1,0:T(8,128)(2,1)S(1)}, u32[]{:S(2)}, u32[]{:S(2)}) async-start(bf16[96,32,128]{2,1,0:T(8,128)(2,1)} %bitcast.103), calls=%async_computation.1 | async-start | bytes 1572864 | tf_op jit(solution)/shard_map/all_to_all | solution.py:38
  33.6 1.2 copy.27
  34.8 19.5 %all-to-all-done.1 = bf16[96,32,128]{2,1,0:T(8,128)(2,1)S(1)} async-done(((bf16[96,32,128]{2,1,0:T(8,128)(2,1)}), bf16[96,32,128]{2,1,0:T(8,128)(2,1)S(1)}, u32[]{:S(2)}, u32[]{:S(2)}) %all-to-all-start.1) | async-done | bytes 786464 | tf_op jit(solution)/shard_map/all_to_all | solution.py:38
  54.3 3.5 %all-to-all-start.2 = ((bf16[96,32,128]{2,1,0:T(8,128)(2,1)}), bf16[96,32,128]{2,1,0:T(8,128)(2,1)S(1)}, u32[]{:S(2)}, u32[]{:S(2)}) async-start(bf16[96,32,128]{2,1,0:T(8,128)(2,1)} %bitcast.27), calls=%async_computation.2 | async-start | bytes 1572864 | tf_op jit(solution)/shard_map/all_to_all | solution.py:39
  58.1 76.3 %all-gather.1 = bf16[32,2,1536]{2,1,0:T(2,128)(2,1)S(1)} all-gather(bf16[1,2,1536]{2,1,0:T(2,128)(2,1)S(1)} %maximum_bitcast_fusion), channel_id=2, replica_groups=mesh['row'=8,'col'=4] {'row','col'}, dimensions={0}, use_global_device_ids=true | all-gather | bytes 202752 | tf_op jit(solution)/shard_map/all_gather | solution.py:33
  135.4 1.0 copy.25
  136.4 1.0 copy.28
  137.4 0.4 copy-done.2
  137.8 51.3 %while.10 = (s32[]{:T(128)}, bf16[12,256,128]{2,1,0:T(8,128)(2,1)S(1)}, bf16[12,256,128]{2,1,0:T(8,128)(2,1)S(1)}, bf16[12,256,128]{2,1,0:T(8,128)(2,1)}, bf16[1...) while((s32[]{:T(128)}, ...), condition=%wide.region_8.9_spmd, body=%wide.region_3.8_spmd.sunk | while | flops 34611200 | bytes 1587321 | solution.py:76
  137.8 0.6 dynamic_slice.60
  138.4 0.8 fusion.44
  139.2 1.1 fusion.45
  140.9 1.1 fusion.49
  142.1 0.6 dynamic_slice.60
  142.7 0.8 fusion.44
  143.5 1.1 fusion.45
  145.2 1.1 fusion.49
  146.3 0.6 dynamic_slice.60
  146.9 0.8 fusion.44
  147.7 1.1 fusion.45
  149.5 1.1 fusion.49
  150.6 0.6 dynamic_slice.60
  151.2 0.8 fusion.44
  152.0 1.1 fusion.45
  153.8 1.1 fusion.49
  154.9 0.6 dynamic_slice.60
  155.5 0.8 fusion.44
  156.3 1.1 fusion.45
  158.0 1.1 fusion.49
  159.2 0.6 dynamic_slice.60
  159.8 0.8 fusion.44
  160.6 1.1 fusion.45
  162.3 1.1 fusion.49
  163.4 0.6 dynamic_slice.60
  164.0 0.8 fusion.44
  164.8 1.1 fusion.45
  166.6 1.1 fusion.49
  167.7 0.6 dynamic_slice.60
  168.3 0.8 fusion.44
  169.1 1.1 fusion.45
  170.9 1.1 fusion.49
  172.0 0.6 dynamic_slice.60
  172.6 0.8 fusion.44
  173.4 1.1 fusion.45
  175.1 1.1 fusion.49
  176.3 0.6 dynamic_slice.60
  176.9 0.8 fusion.44
  177.7 1.1 fusion.45
  179.4 1.1 fusion.49
  180.6 0.6 dynamic_slice.60
  181.1 0.8 fusion.44
  182.0 1.1 fusion.45
  183.7 1.1 fusion.49
  184.8 0.6 dynamic_slice.60
  185.4 0.8 fusion.44
  186.2 1.1 fusion.45
  188.0 1.1 fusion.49
  189.1 0.5 copy.31
  189.6 29.0 %all_to_all.66 = bf16[12,256,128]{2,0,1:T(8,128)(2,1)S(1)} all-to-all(bf16[12,256,128]{2,0,1:T(8,128)(2,1)S(1)} %copy.31), channel_id=1, replica_groups=mesh['row'=8,'col'=4] {'row'}, dimensions={1} | all-to-all | bytes 1572864 | tf_op jit(solution)/shard_map/all_to_all | solution.py:79
  218.6 1.8 copy.35
  (169 shorter events, 9.3 us)
Async XLA Ops:
  2.3 6.5 %copy-start = (bf16[32,8,1536]{2,1,0:T(8,128)(2,1)S(1)}, bf16[32,8,1536]{2,1,0:T(8,128)(2,1)}, u32[]{:S(2)}) copy-start(bf16[32,8,1536]{2,1,0:T(8,128)(2,1)} %param.7) | copy-start | bytes 2359300
  2.3 27.4 %all-to-all-start = ((bf16[96,32,128]{2,1,0:T(8,128)(2,1)}), bf16[96,32,128]{2,1,0:T(8,128)(2,1)S(1)}, u32[]{:S(2)}, u32[]{:S(2)}) async-start(bf16[96,32,128]{2,1,0:T(8,128)(2,1)} %bitcast.11), calls=%async_computation | async-start | bytes 1572864 | tf_op jit(solution)/shard_map/all_to_all | solution.py:37
  29.8 3.9 %copy-start.1 = (bf16[32,8,1536]{2,1,0:T(8,128)(2,1)S(1)}, bf16[32,8,1536]{2,1,0:T(8,128)(2,1)}, u32[]{:S(2)}) copy-start(bf16[32,8,1536]{2,1,0:T(8,128)(2,1)} %param.8) | copy-start | bytes 2359300
  29.8 24.6 %all-to-all-start.1 = ((bf16[96,32,128]{2,1,0:T(8,128)(2,1)}), bf16[96,32,128]{2,1,0:T(8,128)(2,1)S(1)}, u32[]{:S(2)}, u32[]{:S(2)}) async-start(bf16[96,32,128]{2,1,0:T(8,128)(2,1)} %bitcast.103), calls=%async_computation.1 | async-start | bytes 1572864 | tf_op jit(solution)/shard_map/all_to_all | solution.py:38
  54.3 82.0 %all-to-all-start.2 = ((bf16[96,32,128]{2,1,0:T(8,128)(2,1)}), bf16[96,32,128]{2,1,0:T(8,128)(2,1)S(1)}, u32[]{:S(2)}, u32[]{:S(2)}) async-start(bf16[96,32,128]{2,1,0:T(8,128)(2,1)} %bitcast.27), calls=%async_computation.2 | async-start | bytes 1572864 | tf_op jit(solution)/shard_map/all_to_all | solution.py:39
  58.0 77.1 %copy-start.3 = (f32[12]{0:T(128)S(1)}, f32[12]{0:T(128)}, u32[]{:S(2)}) copy-start(f32[12]{0:T(128)} %param.9) | copy-start | bytes 148
  136.4 1.4 copy-start.2
where the time goes:
time: 222 us; the launch traced here: 220 us
  blocking collectives  105 us (47%)
  waiting for transfers between devices  39.3 us (18%)
  matrix products  38.6 us (17%)
  local copies, waits for them, and re-layouts  20.6 us (9%)
  starting transfers between devices  13.7 us (6%)
    all_gather x1, blocking collectives, per_device(): lax.all_gather(summary, ('row', 'col'), axis=0, tiled=True)  76.3 us
    all_to_all x1, blocking collectives, per_device(): lax.all_to_all(attended_cols, 'row', split_axis=1, concat_axis=0, tiled=T...  29 us
    all_to_all x1, waiting for transfers between devices, per_device(): lax.all_to_all(to_pairs(queries), 'row', split_axis=0, concat_axis=1, til...  19.8 us
    all_to_all x1, waiting for transfers between devices, per_device(): lax.all_to_all(to_pairs(keys), 'row', split_axis=0, concat_axis=1, tiled=...  19.5 us
    dot_general x12, matrix products, attend(): mixed = jnp.dot(col_weights, value_one, preferred_element_type=jnp.float32)  13.2 us
    dot_general x12, matrix products, attend(): jnp.einsum('re,se->rs', query_one, key_one, preferred_element_type=jnp.fl...  12.8 us
    dot_general x12, matrix products, attend(): jnp.einsum('bre,bne->brn', query_band, mem_key_one, preferred_element_typ...  9.59 us
    dynamic_slice x24, local copies, waits for them, and re-layouts, per_device(): lax.map(attend, (query_cols, key_rows, value_rows, mem_keys, mem_values,...  7.19 us
  transfers between devices with their start and end apart: 3, of which 2 were waited for; matrix products, arithmetic and copies ran while one was open for 2% of the time, Pallas kernels for 0%

commit v1 on v0

v1 whole, which is shorter than its diff:
```python
import functools
import math

import jax
import jax.numpy as jnp
from jax import lax
from jax.experimental import pallas as pl
from jax.experimental.pallas import tpu as pltpu
from jax.sharding import PartitionSpec as P

LOG2E = 1.4426950408889634
VMEM_LIMIT = 48 * 1024 * 1024


def spread_kernel(dims, head_ids, me_ref, q_ref, k_ref, v_ref, *rest):
    n_row, col_groups, cols_g, heads_g, row_dev, col_dev, head_dim = dims
    out_refs = rest[:n_row]
    wide, blocks, sems = rest[n_row:]
    me = me_ref[0]
    slot = 0
    for t, ref in enumerate((q_ref, k_ref, v_ref)):
        for g in range(n_row // col_groups):
            for j, local in enumerate(head_ids):
                start = (g * heads_g + local) * head_dim
                wide[slot] = (
                    ref[:, :, start : start + head_dim]
                    .astype(jnp.float32)
                    .reshape(row_dev * col_dev, head_dim)
                )
                for c in range(col_dev):
                    dest = g * col_groups + c // cols_g
                    pair = j * cols_g + c % cols_g
                    blocks[dest, t, pair] = wide[slot, pl.ds(c, row_dev, stride=col_dev), :].astype(
                        jnp.bfloat16
                    )
                slot = (slot + 1) % wide.shape[0]
    copies = [
        pltpu.make_async_copy(blocks.at[me ^ k], out_refs[k], sems.at[k]) for k in range(n_row)
    ]
    for copy in copies:
        copy.start()
    for copy in copies:
        copy.wait()


def spread(dims, head_ids, me, q, k, v):
    n_row, col_groups, cols_g, heads_g, row_dev, col_dev, head_dim = dims
    block = (3, len(head_ids) * cols_g, row_dev, head_dim)
    return pl.pallas_call(
        functools.partial(spread_kernel, dims, head_ids),
        out_shape=[jax.ShapeDtypeStruct(block, jnp.bfloat16)] * n_row,
        in_specs=[pl.BlockSpec(memory_space=pltpu.SMEM)]
        + [pl.BlockSpec(memory_space=pltpu.VMEM)] * 3,
        out_specs=[pl.BlockSpec(memory_space=pl.ANY)] * n_row,
        scratch_shapes=[
            pltpu.VMEM((4, row_dev * col_dev, head_dim), jnp.float32),
            pltpu.VMEM((n_row,) + block, jnp.bfloat16),
            pltpu.SemaphoreType.DMA((n_row,)),
        ],
        compiler_params=pltpu.CompilerParams(vmem_limit_bytes=VMEM_LIMIT),
        name="spread",
    )(me, q, k, v)


def attend_kernel(dims, n_col, head_ids, me_ref, bias_ref, mem_ref, *rest):
    n_row, col_groups, cols_g, heads_g, row_dev, col_dev, head_dim = dims
    in_refs, out_refs = rest[:n_row], rest[n_row:]
    rows, slots = n_row * row_dev, n_row * n_col
    me = me_ref[0]
    scale = LOG2E / math.sqrt(head_dim)
    band = (lax.broadcasted_iota(jnp.int32, (rows, slots), 0) // row_dev) ^ me
    owner = lax.broadcasted_iota(jnp.int32, (rows, slots), 1) // n_col
    hidden = jnp.where(band == owner, 0.0, -1e30)
    ones = jnp.ones((rows, head_dim), jnp.bfloat16)
    slot_ones = jnp.ones((slots, head_dim), jnp.bfloat16)
    nt = (((1,), (1,)), ((), ()))
    group = me // col_groups
    for j, local in enumerate(head_ids):
        bias = bias_ref[group * heads_g + local] * LOG2E
        shift = hidden + bias
        mem_key = mem_ref[0, local]
        mem_value = jnp.concatenate([mem_ref[1, local], slot_ones], axis=1)
        for c in range(cols_g):
            pair = j * cols_g + c
            query = jnp.concatenate([ref[0, pair] for ref in in_refs], axis=0)
            key = jnp.concatenate([ref[1, pair] for ref in in_refs], axis=0)
            value = jnp.concatenate([ref[2, pair] for ref in in_refs], axis=0)
            value = jnp.concatenate([value, ones], axis=1)
            col = lax.dot_general(query, key, nt, preferred_element_type=jnp.float32) * scale
            mem = lax.dot_general(query, mem_key, nt, preferred_element_type=jnp.float32) * scale
            mem = mem + shift
            peak = jnp.maximum(
                jnp.max(col, axis=1, keepdims=True), jnp.max(mem, axis=1, keepdims=True)
            )
            col = jnp.exp2(col - peak).astype(jnp.bfloat16)
            mem = jnp.exp2(mem - peak).astype(jnp.bfloat16)
            mixed = jnp.dot(col, value, preferred_element_type=jnp.float32)
            mixed = mixed + jnp.dot(mem, mem_value, preferred_element_type=jnp.float32)
            out = (mixed[:, :head_dim] / mixed[:, head_dim:]).astype(jnp.bfloat16)
            for k in range(n_row):
                out_refs[k][pair] = out[k * row_dev : (k + 1) * row_dev]


def attend(dims, n_col, head_ids, me, bias, mem, blocks):
    n_row, col_groups, cols_g, heads_g, row_dev, col_dev, head_dim = dims
    block = (len(head_ids) * cols_g, row_dev, head_dim)
    return pl.pallas_call(
        functools.partial(attend_kernel, dims, n_col, head_ids),
        out_shape=[jax.ShapeDtypeStruct(block, jnp.bfloat16)] * n_row,
        in_specs=[pl.BlockSpec(memory_space=pltpu.SMEM)] * 2
        + [pl.BlockSpec(memory_space=pltpu.VMEM)] * (1 + n_row),
        out_specs=[pl.BlockSpec(memory_space=pltpu.VMEM)] * n_row,
        compiler_params=pltpu.CompilerParams(vmem_limit_bytes=VMEM_LIMIT),
        name="attend",
    )(me, bias, mem, *blocks)


def collect_kernel(dims, chunks, me_ref, *rest):
    n_row, col_groups, cols_g, heads_g, row_dev, col_dev, head_dim = dims
    in_refs = rest[: n_row * len(chunks)]
    out_ref, *held, wide = rest[n_row * len(chunks) :]
    me = me_ref[0]
    for i in range(len(chunks)):
        for k in range(n_row):
            held[i][me ^ k] = in_refs[i * n_row + k][...]
    slot = 0
    for i, head_ids in enumerate(chunks):
        for g in range(n_row // col_groups):
            for j, local in enumerate(head_ids):
                for c in range(col_dev):
                    dest = g * col_groups + c // cols_g
                    pair = j * cols_g + c % cols_g
                    wide[slot, pl.ds(c, row_dev, stride=col_dev), :] = held[i][dest, pair].astype(
                        jnp.float32
                    )
                start = (g * heads_g + local) * head_dim
                out_ref[:, :, start : start + head_dim] = (
                    wide[slot].astype(jnp.bfloat16).reshape(row_dev, col_dev, head_dim)
                )
                slot = (slot + 1) % wide.shape[0]


def collect(dims, chunks, me, blocks):
    n_row, col_groups, cols_g, heads_g, row_dev, col_dev, head_dim = dims
    width = n_row // col_groups * heads_g * head_dim
    return pl.pallas_call(
        functools.partial(collect_kernel, dims, chunks),
        out_shape=jax.ShapeDtypeStruct((row_dev, col_dev, width), jnp.bfloat16),
        in_specs=[pl.BlockSpec(memory_space=pltpu.SMEM)]
        + [pl.BlockSpec(memory_space=pltpu.VMEM)] * len(blocks),
        out_specs=pl.BlockSpec(memory_space=pltpu.VMEM),
        scratch_shapes=[
            pltpu.VMEM((n_row, len(ids) * cols_g, row_dev, head_dim), jnp.bfloat16)
            for ids in chunks
        ]
        + [pltpu.VMEM((4, row_dev * col_dev, head_dim), jnp.float32)],
        compiler_params=pltpu.CompilerParams(vmem_limit_bytes=VMEM_LIMIT),
        name="collect",
    )(me, *blocks)


def exchange(blocks):
    n_row = len(blocks)
    return [blocks[0]] + [
        lax.ppermute(blocks[k], "row", [(i, i ^ k) for i in range(n_row)]) for k in range(1, n_row)
    ]


def per_device(queries, keys, values, memory_bias):
    row_dev, col_dev, model_width = queries.shape
    n_row = lax.axis_size("row")
    n_col = lax.axis_size("col")
    head_count = memory_bias.shape[0]
    head_dim = model_width // head_count
    head_groups = math.gcd(head_count, n_row)
    col_groups = n_row // head_groups
    heads_g = head_count // head_groups
    cols_g = col_dev // col_groups
    dims = (n_row, col_groups, cols_g, heads_g, row_dev, col_dev, head_dim)
    split = max(1, heads_g * 2 // 3)
    chunks = [tuple(range(split)), tuple(range(split, heads_g))]
    me = lax.axis_index("row").astype(jnp.int32).reshape(1)

    sent = [spread(dims, ids, me, queries, keys, values) for ids in chunks]
    arrived = [exchange(blocks) for blocks in sent]

    own_keys = jnp.mean(keys, axis=(0, 1), dtype=jnp.float32).astype(jnp.bfloat16)
    own_values = jnp.mean(values, axis=(0, 1), dtype=jnp.float32).astype(jnp.bfloat16)
    own = jnp.stack([own_keys, own_values])[None]
    band = lax.all_gather(own, "col", axis=0, tiled=True)
    band = band.reshape(n_col, 2, head_groups, 1, heads_g, head_dim)
    band = jnp.transpose(band, (2, 3, 1, 4, 0, 5))
    band = jnp.broadcast_to(band, (head_groups, col_groups, 2, heads_g, n_col, head_dim))
    band = band.reshape(n_row, 2 * heads_g * n_col, head_dim)
    mem = lax.all_to_all(band, "row", split_axis=0, concat_axis=0, tiled=True)
    mem = mem.reshape(n_row, 2, heads_g, n_col, head_dim)
    mem = jnp.transpose(mem, (1, 2, 0, 3, 4)).reshape(2, heads_g, n_row * n_col, head_dim)

    returned = []
    for ids, blocks in zip(chunks, arrived):
        returned += exchange(attend(dims, n_col, ids, me, memory_bias, mem, blocks))
    return collect(dims, chunks, me, returned)


def solution(mesh):
    return jax.shard_map(
        per_device,
        mesh=mesh,
        in_specs=(P("row", "col", None), P("row", "col", None), P("row", "col", None), P()),
        out_specs=P("row", "col", None),
        check_vma=False,
    )
```

time: 222 us -> 98.2 us (0.44)
  blocking collectives: 105 us -> 30.3 us
  matrix products: 38.6 us -> 0 us
  waiting for transfers between devices: 39.3 us -> 15.1 us
  starting transfers between devices: 13.7 us -> 37.8 us
  local copies, waits for them, and re-layouts: 20.6 us -> 3.5 us
  Pallas kernels: 0 us -> 10 us
    all_gather x1, blocking collectives: 76.3 us -> 8.17 us  [per_device(): band = lax.all_gather(own, 'col', axis=0, tiled=True)]
    all_to_all x3 -> x0, waiting for transfers between devices: 39.3 us -> none  [the longest x1 19.8 us: per_device(): lax.all_to_all(to_pairs(queries), 'row', split_axis=0, concat_axis=1, til...]
    dot_general x50 -> x0, matrix products: 38.6 us -> none  [the longest x12 13.2 us: attend(): mixed = jnp.dot(col_weights, value_one, preferred_element_type=jnp.float32)]
    ppermute x0 -> x28, starting transfers between devices: none -> 37.8 us  [exchange(): lax.ppermute(blocks[k], 'row', [(i, i ^ k) for i in range(n_row)])]
    ppermute x0 -> x28, waiting for transfers between devices: none -> 15.1 us  [exchange(): lax.ppermute(blocks[k], 'row', [(i, i ^ k) for i in range(n_row)])]
    all_to_all x3 -> x0, starting transfers between devices: 13.7 us -> none  [the longest x1 6.46 us: per_device(): lax.all_to_all(to_pairs(queries), 'row', split_axis=0, concat_axis=1, til...]
    pallas_call x0 -> x5, Pallas kernels: none -> 10 us  [the longest x2 4.54 us: attend(): pl.pallas_call(functools.partial(attend_kernel, dims, n_col, head_ids), o...]
    dynamic_slice x24 -> x0, local copies, waits for them, and re-layouts: 7.19 us -> none  [per_device(): lax.map(attend, (query_cols, key_rows, value_rows, mem_keys, mem_values,...]
  transfers between devices with their start and end apart: 3 -> 28, of which waited for: 2 -> 8; matrix products, arithmetic and copies ran while one was open for 2% -> 0% of each run, Pallas kernels for 0% -> 6%
where the time goes in v1:
time: 98.2 us; the launch traced here: 97.2 us
  starting transfers between devices  37.8 us (38%)
  blocking collectives  30.3 us (31%)
  waiting for transfers between devices  15.1 us (15%)
  Pallas kernels  10 us (10%)
  local copies, waits for them, and re-layouts  3.5 us (4%)
    ppermute x28, starting transfers between devices, exchange(): lax.ppermute(blocks[k], 'row', [(i, i ^ k) for i in range(n_row)])  37.8 us
    all_to_all x1, blocking collectives, per_device(): mem = lax.all_to_all(band, 'row', split_axis=0, concat_axis=0, tiled=True)  22.2 us
    ppermute x28, waiting for transfers between devices, exchange(): lax.ppermute(blocks[k], 'row', [(i, i ^ k) for i in range(n_row)])  15.1 us
    all_gather x1, blocking collectives, per_device(): band = lax.all_gather(own, 'col', axis=0, tiled=True)  8.17 us
    pallas_call x2, Pallas kernels, attend(): pl.pallas_call(functools.partial(attend_kernel, dims, n_col, head_ids), o...  4.54 us
    pallas_call x2, Pallas kernels, spread(): pl.pallas_call(functools.partial(spread_kernel, dims, head_ids), out_shap...  4.19 us
    unnamed x8, local copies, waits for them, and re-layouts  3.4 us
  transfers between devices with their start and end apart: 28, of which 8 were waited for; matrix products, arithmetic and copies ran while one was open for 0% of the time, Pallas kernels for 6%

profile of v1, /device:TPU:0, one launch (start us, length us, event | category | flops | bytes accessed | tf_op | source)
XLA Modules:
  0.0 97.2 jit_solution(13661021952170391237)
XLA Ops:
  0.0 1.1 %copy-done = bf16[32,8,1536]{2,1,0:T(8,128)(2,1)S(1)} copy-done((bf16[32,8,1536]{2,1,0:T(8,128)(2,1)S(1)}, bf16[32,8,1536]{2,1,0:T(8,128)(2,1)}, u32[]{:S(2)}) %copy-start) | copy-done | bytes 786456
  1.1 1.1 %copy-done.1 = bf16[32,8,1536]{2,1,0:T(8,128)(2,1)S(1)} copy-done((bf16[32,8,1536]{2,1,0:T(8,128)(2,1)S(1)}, bf16[32,8,1536]{2,1,0:T(8,128)(2,1)}, u32[]{:S(2)}) %copy-start.1) | copy-done | bytes 786456
  2.3 1.1 %copy-done.2 = bf16[32,8,1536]{2,1,0:T(8,128)(2,1)S(1)} copy-done((bf16[32,8,1536]{2,1,0:T(8,128)(2,1)S(1)}, bf16[32,8,1536]{2,1,0:T(8,128)(2,1)}, u32[]{:S(2)}) %copy-start.2) | copy-done | bytes 786456
  3.4 2.8 %spread.2 = (bf16[3,8,32,128]{3,2,1,0:T(8,128)(2,1)S(1)}, bf16[3,8,32,128]{3,2,1,0:T(8,128)(2,1)S(1)}, bf16[3,8,32,128]{3,2,1,0:T(8,128)(2,1)S(1)}, bf16[3,8,32,...) custom-call(s32[1]{0:T(128)} %bitcast.me_ref, ...), custom_call_target="tpu_custom_call" | custom-call | tf_op jit(solution)/shard_map/spread/pallas_call | solution.py:49
  6.2 0.5 collective-permute-start
  6.7 1.4 %spread.3 = (bf16[3,4,32,128]{3,2,1,0:T(8,128)(2,1)S(1)}, bf16[3,4,32,128]{3,2,1,0:T(8,128)(2,1)S(1)}, bf16[3,4,32,128]{3,2,1,0:T(8,128)(2,1)S(1)}, bf16[3,4,32,...) custom-call(s32[1]{0:T(128)} %bitcast.me_ref, ...), custom_call_target="tpu_custom_call" | custom-call | tf_op jit(solution)/shard_map/spread/pallas_call | solution.py:49
  8.1 0.1 collective-permute-start.14
  8.2 3.0 %collective-permute-start.15 = (bf16[3,4,32,128]{3,2,1,0:T(8,128)(2,1)S(1)}, bf16[3,4,32,128]{3,2,1,0:T(8,128)(2,1)S(1)}, u32[]{:S(2)}, u32[]{:S(2)}) collective-permute-start(bf16[3,4,32,128]{3,2,1,0:T(8,128)(2,1)S(1)} %get-tuple-element.55), channel_id=1, source_target_pairs={{0,8},{4,12},{8,0},{12,4},{16,24},{20,28},{24,16},{28,20},{1,9},{5... | collective-permute-start | bytes 294920 | tf_op jit(solution)/shard_map/ppermute | solution.py:165
  11.3 0.0 collective-permute-start.16
  11.3 2.6 %collective-permute-start.17 = (bf16[3,4,32,128]{3,2,1,0:T(8,128)(2,1)S(1)}, bf16[3,4,32,128]{3,2,1,0:T(8,128)(2,1)S(1)}, u32[]{:S(2)}, u32[]{:S(2)}) collective-permute-start(bf16[3,4,32,128]{3,2,1,0:T(8,128)(2,1)S(1)} %get-tuple-element.57), channel_id=1, source_target_pairs={{0,16},{4,20},{8,24},{12,28},{16,0},{20,4},{24,8},{28,12},{1,17},{... | collective-permute-start | bytes 294920 | tf_op jit(solution)/shard_map/ppermute | solution.py:165
  13.9 0.1 convert_reduce_fusion
  14.0 0.1 convert_reduce_fusion.1
  14.1 0.0 collective-permute-done.14.rest_1_
  14.2 1.5 %collective-permute-start.1 = (bf16[3,8,32,128]{3,2,1,0:T(8,128)(2,1)S(1)}, bf16[3,8,32,128]{3,2,1,0:T(8,128)(2,1)S(1)}, u32[]{:S(2)}, u32[]{:S(2)}) collective-permute-start(bf16[3,8,32,128]{3,2,1,0:T(8,128)(2,1)S(1)} %get-tuple-element.39), channel_id=1, source_target_pairs={{0,8},{4,12},{8,0},{12,4},{16,24},{20,28},{24,16},{28,20},{1,9},{5... | collective-permute-start | bytes 589832 | tf_op jit(solution)/shard_map/ppermute | solution.py:165
  15.6 0.0 collective-permute-done.15.rest_2_
  15.6 0.3 collective-permute-start.18
  15.9 2.6 %collective-permute-done.16.rest_3_ = bf16[3,4,32,128]{3,2,1,0:T(8,128)(2,1)S(1)} collective-permute-done((bf16[3,4,32,128]{3,2,1,0:T(8,128)(2,1)S(1)}, bf16[3,4,32,128]{3,2,1,0:T(8,128)(2,1)S(1)}, u32[]{:S(2)}, u32[]{:S(2)}) %collective-permute-start.16) | collective-permute-done | bytes 98336 | tf_op jit(solution)/shard_map/ppermute | solution.py:165
  18.5 1.3 %collective-permute-start.19 = (bf16[3,4,32,128]{3,2,1,0:T(8,128)(2,1)S(1)}, bf16[3,4,32,128]{3,2,1,0:T(8,128)(2,1)S(1)}, u32[]{:S(2)}, u32[]{:S(2)}) collective-permute-start(bf16[3,4,32,128]{3,2,1,0:T(8,128)(2,1)S(1)} %get-tuple-element.59), channel_id=1, source_target_pairs={{0,24},{4,28},{8,16},{12,20},{16,8},{20,12},{24,0},{28,4},{1,25},{... | collective-permute-start | bytes 294920 | tf_op jit(solution)/shard_map/ppermute | solution.py:165
  19.8 0.0 collective-permute-done.17.rest_4_
  19.8 3.0 %collective-permute-start.20 = (bf16[3,4,32,128]{3,2,1,0:T(8,128)(2,1)S(1)}, bf16[3,4,32,128]{3,2,1,0:T(8,128)(2,1)S(1)}, u32[]{:S(2)}, u32[]{:S(2)}) collective-permute-start(bf16[3,4,32,128]{3,2,1,0:T(8,128)(2,1)S(1)} %get-tuple-element.60), channel_id=1, source_target_pairs={{0,28},{4,24},{8,20},{12,16},{16,12},{20,8},{24,4},{28,0},{1,29},{... | collective-permute-start | bytes 294920 | tf_op jit(solution)/shard_map/ppermute | solution.py:165
  22.8 2.1 %collective-permute-done.18.rest_5_ = bf16[3,4,32,128]{3,2,1,0:T(8,128)(2,1)S(1)} collective-permute-done((bf16[3,4,32,128]{3,2,1,0:T(8,128)(2,1)S(1)}, bf16[3,4,32,128]{3,2,1,0:T(8,128)(2,1)S(1)}, u32[]{:S(2)}, u32[]{:S(2)}) %collective-permute-start.18) | collective-permute-done | bytes 98336 | tf_op jit(solution)/shard_map/ppermute | solution.py:165
  24.9 2.4 %collective-permute-start.2 = (bf16[3,8,32,128]{3,2,1,0:T(8,128)(2,1)S(1)}, bf16[3,8,32,128]{3,2,1,0:T(8,128)(2,1)S(1)}, u32[]{:S(2)}, u32[]{:S(2)}) collective-permute-start(bf16[3,8,32,128]{3,2,1,0:T(8,128)(2,1)S(1)} %get-tuple-element.40), channel_id=1, source_target_pairs={{0,12},{4,8},{8,4},{12,0},{16,28},{20,24},{24,20},{28,16},{1,13},{... | collective-permute-start | bytes 589832 | tf_op jit(solution)/shard_map/ppermute | solution.py:165
  27.3 2.2 %collective-permute-done.19.rest_6_ = bf16[3,4,32,128]{3,2,1,0:T(8,128)(2,1)S(1)} collective-permute-done((bf16[3,4,32,128]{3,2,1,0:T(8,128)(2,1)S(1)}, bf16[3,4,32,128]{3,2,1,0:T(8,128)(2,1)S(1)}, u32[]{:S(2)}, u32[]{:S(2)}) %collective-permute-start.19) | collective-permute-done | bytes 98336 | tf_op jit(solution)/shard_map/ppermute | solution.py:165
  29.5 3.4 %collective-permute-start.3 = (bf16[3,8,32,128]{3,2,1,0:T(8,128)(2,1)S(1)}, bf16[3,8,32,128]{3,2,1,0:T(8,128)(2,1)S(1)}, u32[]{:S(2)}, u32[]{:S(2)}) collective-permute-start(bf16[3,8,32,128]{3,2,1,0:T(8,128)(2,1)S(1)} %get-tuple-element.41), channel_id=1, source_target_pairs={{0,16},{4,20},{8,24},{12,28},{16,0},{20,4},{24,8},{28,12},{1,17},{... | collective-permute-start | bytes 589832 | tf_op jit(solution)/shard_map/ppermute | solution.py:165
  33.0 0.0 collective-permute-done.20.rest_7_
  33.0 1.8 %collective-permute-start.4 = (bf16[3,8,32,128]{3,2,1,0:T(8,128)(2,1)S(1)}, bf16[3,8,32,128]{3,2,1,0:T(8,128)(2,1)S(1)}, u32[]{:S(2)}, u32[]{:S(2)}) collective-permute-start(bf16[3,8,32,128]{3,2,1,0:T(8,128)(2,1)S(1)} %get-tuple-element.42), channel_id=1, source_target_pairs={{0,20},{4,16},{8,28},{12,24},{16,4},{20,0},{24,12},{28,8},{1,21},{... | collective-permute-start | bytes 589832 | tf_op jit(solution)/shard_map/ppermute | solution.py:165
  34.8 0.0 collective-permute-done.rest_1_
  34.8 1.3 %collective-permute-start.5 = (bf16[3,8,32,128]{3,2,1,0:T(8,128)(2,1)S(1)}, bf16[3,8,32,128]{3,2,1,0:T(8,128)(2,1)S(1)}, u32[]{:S(2)}, u32[]{:S(2)}) collective-permute-start(bf16[3,8,32,128]{3,2,1,0:T(8,128)(2,1)S(1)} %get-tuple-element.43), channel_id=1, source_target_pairs={{0,24},{4,28},{8,16},{12,20},{16,8},{20,12},{24,0},{28,4},{1,25},{... | collective-permute-start | bytes 589832 | tf_op jit(solution)/shard_map/ppermute | solution.py:165
  36.1 0.0 collective-permute-done.1.rest_2_
  36.1 1.9 %collective-permute-start.6 = (bf16[3,8,32,128]{3,2,1,0:T(8,128)(2,1)S(1)}, bf16[3,8,32,128]{3,2,1,0:T(8,128)(2,1)S(1)}, u32[]{:S(2)}, u32[]{:S(2)}) collective-permute-start(bf16[3,8,32,128]{3,2,1,0:T(8,128)(2,1)S(1)} %get-tuple-element.44), channel_id=1, source_target_pairs={{0,28},{4,24},{8,20},{12,16},{16,12},{20,8},{24,4},{28,0},{1,29},{... | collective-permute-start | bytes 589832 | tf_op jit(solution)/shard_map/ppermute | solution.py:165
  38.0 8.2 %all-gather.1 = bf16[4,2,1536]{2,1,0:T(2,128)(2,1)S(1)} all-gather(bf16[1,2,1536]{2,1,0:T(2,128)(2,1)S(1)} %maximum_bitcast_fusion), channel_id=2, replica_groups=mesh['row'=8,'col'=4] {'col'}, dimensions={0}, use_global_device_ids=true | all-gather | bytes 30720 | tf_op jit(solution)/shard_map/all_gather | solution.py:190
  46.2 22.2 %all_to_all.5 = bf16[8,24,128]{2,1,0:T(8,128)(2,1)S(1)} all-to-all(bf16[8,24,128]{2,1,0:T(8,128)(2,1)S(1)} %bitcast.13), channel_id=1, replica_groups=mesh['row'=8,'col'=4] {'row'}, dimensions={0} | all-to-all | bytes 98304 | tf_op jit(solution)/shard_map/all_to_all | solution.py:195
  68.4 1.8 %attend.3 = (bf16[4,32,128]{2,1,0:T(8,128)(2,1)S(1)}, bf16[4,32,128]{2,1,0:T(8,128)(2,1)S(1)}, bf16[4,32,128]{2,1,0:T(8,128)(2,1)S(1)}, bf16[4,32,128]{2,1,0:T(8...) custom-call(s32[1]{0:T(128)} %bitcast.me_ref, ...), custom_call_target="tpu_custom_call" | custom-call | tf_op jit(solution)/shard_map/attend/pallas_call | solution.py:107
  70.3 0.0 collective-permute-done.2.rest_3_
  70.3 0.1 collective-permute-start.21
  70.3 0.0 collective-permute-done.3.rest_4_
  70.4 0.5 collective-permute-start.22
  70.8 0.0 collective-permute-done.4.rest_5_
  70.9 1.4 %collective-permute-start.23 = (bf16[4,32,128]{2,1,0:T(8,128)(2,1)S(1)}, bf16[4,32,128]{2,1,0:T(8,128)(2,1)S(1)}, u32[]{:S(2)}, u32[]{:S(2)}) collective-permute-start(bf16[4,32,128]{2,1,0:T(8,128)(2,1)S(1)} %get-tuple-element.64), channel_id=1, source_target_pairs={{0,12},{4,8},{8,4},{12,0},{16,28},{20,24},{24,20},{28,16},{1,13},{... | collective-permute-start | bytes 98312 | tf_op jit(solution)/shard_map/ppermute | solution.py:165
  72.2 0.0 collective-permute-done.5.rest_6_
  72.2 1.2 %collective-permute-start.24 = (bf16[4,32,128]{2,1,0:T(8,128)(2,1)S(1)}, bf16[4,32,128]{2,1,0:T(8,128)(2,1)S(1)}, u32[]{:S(2)}, u32[]{:S(2)}) collective-permute-start(bf16[4,32,128]{2,1,0:T(8,128)(2,1)S(1)} %get-tuple-element.65), channel_id=1, source_target_pairs={{0,16},{4,20},{8,24},{12,28},{16,0},{20,4},{24,8},{28,12},{1,17},{... | collective-permute-start | bytes 98312 | tf_op jit(solution)/shard_map/ppermute | solution.py:165
  73.4 0.0 collective-permute-done.6.rest_7_
  73.4 2.7 %attend.2 = (bf16[8,32,128]{2,1,0:T(8,128)(2,1)S(1)}, bf16[8,32,128]{2,1,0:T(8,128)(2,1)S(1)}, bf16[8,32,128]{2,1,0:T(8,128)(2,1)S(1)}, bf16[8,32,128]{2,1,0:T(8...) custom-call(s32[1]{0:T(128)} %bitcast.me_ref, ...), custom_call_target="tpu_custom_call" | custom-call | tf_op jit(solution)/shard_map/attend/pallas_call | solution.py:107
  76.1 0.1 collective-permute-start.7
  76.3 0.0 collective-permute-done.21.rest_9_
  76.3 1.6 %collective-permute-start.8 = (bf16[8,32,128]{2,1,0:T(8,128)(2,1)S(1)}, bf16[8,32,128]{2,1,0:T(8,128)(2,1)S(1)}, u32[]{:S(2)}, u32[]{:S(2)}) collective-permute-start(bf16[8,32,128]{2,1,0:T(8,128)(2,1)S(1)} %get-tuple-element.47), channel_id=1, source_target_pairs={{0,8},{4,12},{8,0},{12,4},{16,24},{20,28},{24,16},{28,20},{1,9},{5... | collective-permute-start | bytes 196616 | tf_op jit(solution)/shard_map/ppermute | solution.py:165
  77.9 0.0 collective-permute-done.22.rest_10_
  77.9 0.3 collective-permute-start.25
  78.2 0.0 collective-permute-done.23.rest_11_
  78.2 2.2 %collective-permute-start.26 = (bf16[4,32,128]{2,1,0:T(8,128)(2,1)S(1)}, bf16[4,32,128]{2,1,0:T(8,128)(2,1)S(1)}, u32[]{:S(2)}, u32[]{:S(2)}) collective-permute-start(bf16[4,32,128]{2,1,0:T(8,128)(2,1)S(1)} %get-tuple-element.67), channel_id=1, source_target_pairs={{0,24},{4,28},{8,16},{12,20},{16,8},{20,12},{24,0},{28,4},{1,25},{... | collective-permute-start | bytes 98312 | tf_op jit(solution)/shard_map/ppermute | solution.py:165
  80.5 1.3 %collective-permute-start.27 = (bf16[4,32,128]{2,1,0:T(8,128)(2,1)S(1)}, bf16[4,32,128]{2,1,0:T(8,128)(2,1)S(1)}, u32[]{:S(2)}, u32[]{:S(2)}) collective-permute-start(bf16[4,32,128]{2,1,0:T(8,128)(2,1)S(1)} %get-tuple-element.68), channel_id=1, source_target_pairs={{0,28},{4,24},{8,20},{12,16},{16,12},{20,8},{24,4},{28,0},{1,29},{... | collective-permute-start | bytes 98312 | tf_op jit(solution)/shard_map/ppermute | solution.py:165
  81.7 1.2 %collective-permute-done.25.rest_13_ = bf16[4,32,128]{2,1,0:T(8,128)(2,1)S(1)} collective-permute-done((bf16[4,32,128]{2,1,0:T(8,128)(2,1)S(1)}, bf16[4,32,128]{2,1,0:T(8,128)(2,1)S(1)}, u32[]{:S(2)}, u32[]{:S(2)}) %collective-permute-start.25) | collective-permute-done | bytes 32800 | tf_op jit(solution)/shard_map/ppermute | solution.py:165
  82.9 1.0 %collective-permute-done.26.rest_14_ = bf16[4,32,128]{2,1,0:T(8,128)(2,1)S(1)} collective-permute-done((bf16[4,32,128]{2,1,0:T(8,128)(2,1)S(1)}, bf16[4,32,128]{2,1,0:T(8,128)(2,1)S(1)}, u32[]{:S(2)}, u32[]{:S(2)}) %collective-permute-start.26) | collective-permute-done | bytes 32800 | tf_op jit(solution)/shard_map/ppermute | solution.py:165
  83.9 1.6 %collective-permute-start.10 = (bf16[8,32,128]{2,1,0:T(8,128)(2,1)S(1)}, bf16[8,32,128]{2,1,0:T(8,128)(2,1)S(1)}, u32[]{:S(2)}, u32[]{:S(2)}) collective-permute-start(bf16[8,32,128]{2,1,0:T(8,128)(2,1)S(1)} %get-tuple-element.49), channel_id=1, source_target_pairs={{0,16},{4,20},{8,24},{12,28},{16,0},{20,4},{24,8},{28,12},{1,17},{... | collective-permute-start | bytes 196616 | tf_op jit(solution)/shard_map/ppermute | solution.py:165
  85.6 0.1 collective-permute-done.27.rest_15_
  85.7 0.6 collective-permute-start.11
  86.3 1.8 %collective-permute-start.12 = (bf16[8,32,128]{2,1,0:T(8,128)(2,1)S(1)}, bf16[8,32,128]{2,1,0:T(8,128)(2,1)S(1)}, u32[]{:S(2)}, u32[]{:S(2)}) collective-permute-start(bf16[8,32,128]{2,1,0:T(8,128)(2,1)S(1)} %get-tuple-element.51), channel_id=1, source_target_pairs={{0,24},{4,28},{8,16},{12,20},{16,8},{20,12},{24,0},{28,4},{1,25},{... | collective-permute-start | bytes 196616 | tf_op jit(solution)/shard_map/ppermute | solution.py:165
  88.1 2.0 %collective-permute-start.13 = (bf16[8,32,128]{2,1,0:T(8,128)(2,1)S(1)}, bf16[8,32,128]{2,1,0:T(8,128)(2,1)S(1)}, u32[]{:S(2)}, u32[]{:S(2)}) collective-permute-start(bf16[8,32,128]{2,1,0:T(8,128)(2,1)S(1)} %get-tuple-element.52), channel_id=1, source_target_pairs={{0,28},{4,24},{8,20},{12,16},{16,12},{20,8},{24,4},{28,0},{1,29},{... | collective-permute-start | bytes 196616 | tf_op jit(solution)/shard_map/ppermute | solution.py:165
  90.2 0.0 collective-permute-done.9.rest_3_
  90.2 3.8 %collective-permute-done.10.rest_4_ = bf16[8,32,128]{2,1,0:T(8,128)(2,1)S(1)} collective-permute-done((bf16[8,32,128]{2,1,0:T(8,128)(2,1)S(1)}, bf16[8,32,128]{2,1,0:T(8,128)(2,1)S(1)}, u32[]{:S(2)}, u32[]{:S(2)}) %collective-permute-start.10) | collective-permute-done | bytes 65568 | tf_op jit(solution)/shard_map/ppermute | solution.py:165
  93.9 2.0 %collective-permute-done.11.rest_5_ = bf16[8,32,128]{2,1,0:T(8,128)(2,1)S(1)} collective-permute-done((bf16[8,32,128]{2,1,0:T(8,128)(2,1)S(1)}, bf16[8,32,128]{2,1,0:T(8,128)(2,1)S(1)}, u32[]{:S(2)}, u32[]{:S(2)}) %collective-permute-start.11) | collective-permute-done | bytes 65568 | tf_op jit(solution)/shard_map/ppermute | solution.py:165
  95.9 0.0 collective-permute-done.12.rest_6_
  95.9 0.0 collective-permute-done.13.rest_7_
  95.9 1.3 %collect.1 = bf16[32,8,1536]{2,1,0:T(8,128)(2,1)} custom-call(s32[1]{0:T(128)} %bitcast.me_ref, bf16[8,32,128]{2,1,0:T(8,128)(2,1)S(1)} %get-tuple-element.45.rest_0_, bf16[8,32,128]{2,1,0:T(8,128)(2,1)S(1)} %collective-permute-done.7.rest_1_, bf16[8,32,128]{2,1,0:T(8,128)(2,1)S(1)} %collective-permute-done.8.rest_2_, ...), custom_call_target="tpu_custom_call" | custom-call | tf_op jit(solution)/shard_map/collect/pallas_call | solution.py:146
  (19 shorter events, 0.1 us)
Async XLA Ops:
  0.0 1.1 %copy-start = (bf16[32,8,1536]{2,1,0:T(8,128)(2,1)S(1)}, bf16[32,8,1536]{2,1,0:T(8,128)(2,1)}, u32[]{:S(2)}) copy-start(bf16[32,8,1536]{2,1,0:T(8,128)(2,1)} %v_ref.3) | copy-start | bytes 2359300
  1.1 1.1 %copy-start.1 = (bf16[32,8,1536]{2,1,0:T(8,128)(2,1)S(1)}, bf16[32,8,1536]{2,1,0:T(8,128)(2,1)}, u32[]{:S(2)}) copy-start(bf16[32,8,1536]{2,1,0:T(8,128)(2,1)} %k_ref.3) | copy-start | bytes 2359300
  2.3 1.1 %copy-start.2 = (bf16[32,8,1536]{2,1,0:T(8,128)(2,1)S(1)}, bf16[32,8,1536]{2,1,0:T(8,128)(2,1)}, u32[]{:S(2)}) copy-start(bf16[32,8,1536]{2,1,0:T(8,128)(2,1)} %q_ref.3) | copy-start | bytes 2359300
  6.2 28.6 %collective-permute-start = (bf16[3,8,32,128]{3,2,1,0:T(8,128)(2,1)S(1)}, bf16[3,8,32,128]{3,2,1,0:T(8,128)(2,1)S(1)}, u32[]{:S(2)}, u32[]{:S(2)}) collective-permute-start(bf16[3,8,32,128]{3,2,1,0:T(8,128)(2,1)S(1)} %get-tuple-element.38), channel_id=1, source_target_pairs={{0,4},{4,0},{8,12},{12,8},{16,20},{20,16},{24,28},{28,24},{1,5},{5... | collective-permute-start | bytes 589832 | tf_op jit(solution)/shard_map/ppermute | solution.py:165
  8.1 6.0 %collective-permute-start.14 = (bf16[3,4,32,128]{3,2,1,0:T(8,128)(2,1)S(1)}, bf16[3,4,32,128]{3,2,1,0:T(8,128)(2,1)S(1)}, u32[]{:S(2)}, u32[]{:S(2)}) collective-permute-start(bf16[3,4,32,128]{3,2,1,0:T(8,128)(2,1)S(1)} %get-tuple-element.54), channel_id=1, source_target_pairs={{0,4},{4,0},{8,12},{12,8},{16,20},{20,16},{24,28},{28,24},{1,5},{5... | collective-permute-start | bytes 294920 | tf_op jit(solution)/shard_map/ppermute | solution.py:165
  8.2 7.4 %collective-permute-start.15 = (bf16[3,4,32,128]{3,2,1,0:T(8,128)(2,1)S(1)}, bf16[3,4,32,128]{3,2,1,0:T(8,128)(2,1)S(1)}, u32[]{:S(2)}, u32[]{:S(2)}) collective-permute-start(bf16[3,4,32,128]{3,2,1,0:T(8,128)(2,1)S(1)} %get-tuple-element.55), channel_id=1, source_target_pairs={{0,8},{4,12},{8,0},{12,4},{16,24},{20,28},{24,16},{28,20},{1,9},{5... | collective-permute-start | bytes 294920 | tf_op jit(solution)/shard_map/ppermute | solution.py:165
  11.3 7.3 %collective-permute-start.16 = (bf16[3,4,32,128]{3,2,1,0:T(8,128)(2,1)S(1)}, bf16[3,4,32,128]{3,2,1,0:T(8,128)(2,1)S(1)}, u32[]{:S(2)}, u32[]{:S(2)}) collective-permute-start(bf16[3,4,32,128]{3,2,1,0:T(8,128)(2,1)S(1)} %get-tuple-element.56), channel_id=1, source_target_pairs={{0,12},{4,8},{8,4},{12,0},{16,28},{20,24},{24,20},{28,16},{1,13},{... | collective-permute-start | bytes 294920 | tf_op jit(solution)/shard_map/ppermute | solution.py:165
  11.3 8.5 %collective-permute-start.17 = (bf16[3,4,32,128]{3,2,1,0:T(8,128)(2,1)S(1)}, bf16[3,4,32,128]{3,2,1,0:T(8,128)(2,1)S(1)}, u32[]{:S(2)}, u32[]{:S(2)}) collective-permute-start(bf16[3,4,32,128]{3,2,1,0:T(8,128)(2,1)S(1)} %get-tuple-element.57), channel_id=1, source_target_pairs={{0,16},{4,20},{8,24},{12,28},{16,0},{20,4},{24,8},{28,12},{1,17},{... | collective-permute-start | bytes 294920 | tf_op jit(solution)/shard_map/ppermute | solution.py:165
  14.0 54.4 %copy-start.3 = (f32[12]{0:T(128)S(1)}, f32[12]{0:T(128)}, u32[]{:S(2)}) copy-start(f32[12]{0:T(128)} %bias_ref.3) | copy-start | bytes 148
  14.2 21.9 %collective-permute-start.1 = (bf16[3,8,32,128]{3,2,1,0:T(8,128)(2,1)S(1)}, bf16[3,8,32,128]{3,2,1,0:T(8,128)(2,1)S(1)}, u32[]{:S(2)}, u32[]{:S(2)}) collective-permute-start(bf16[3,8,32,128]{3,2,1,0:T(8,128)(2,1)S(1)} %get-tuple-element.39), channel_id=1, source_target_pairs={{0,8},{4,12},{8,0},{12,4},{16,24},{20,28},{24,16},{28,20},{1,9},{5... | collective-permute-start | bytes 589832 | tf_op jit(solution)/shard_map/ppermute | solution.py:165
  15.6 9.3 %collective-permute-start.18 = (bf16[3,4,32,128]{3,2,1,0:T(8,128)(2,1)S(1)}, bf16[3,4,32,128]{3,2,1,0:T(8,128)(2,1)S(1)}, u32[]{:S(2)}, u32[]{:S(2)}) collective-permute-start(bf16[3,4,32,128]{3,2,1,0:T(8,128)(2,1)S(1)} %get-tuple-element.58), channel_id=1, source_target_pairs={{0,20},{4,16},{8,28},{12,24},{16,4},{20,0},{24,12},{28,8},{1,21},{... | collective-permute-start | bytes 294920 | tf_op jit(solution)/shard_map/ppermute | solution.py:165
  18.5 11.0 %collective-permute-start.19 = (bf16[3,4,32,128]{3,2,1,0:T(8,128)(2,1)S(1)}, bf16[3,4,32,128]{3,2,1,0:T(8,128)(2,1)S(1)}, u32[]{:S(2)}, u32[]{:S(2)}) collective-permute-start(bf16[3,4,32,128]{3,2,1,0:T(8,128)(2,1)S(1)} %get-tuple-element.59), channel_id=1, source_target_pairs={{0,24},{4,28},{8,16},{12,20},{16,8},{20,12},{24,0},{28,4},{1,25},{... | collective-permute-start | bytes 294920 | tf_op jit(solution)/shard_map/ppermute | solution.py:165
  19.8 13.2 %collective-permute-start.20 = (bf16[3,4,32,128]{3,2,1,0:T(8,128)(2,1)S(1)}, bf16[3,4,32,128]{3,2,1,0:T(8,128)(2,1)S(1)}, u32[]{:S(2)}, u32[]{:S(2)}) collective-permute-start(bf16[3,4,32,128]{3,2,1,0:T(8,128)(2,1)S(1)} %get-tuple-element.60), channel_id=1, source_target_pairs={{0,28},{4,24},{8,20},{12,16},{16,12},{20,8},{24,4},{28,0},{1,29},{... | collective-permute-start | bytes 294920 | tf_op jit(solution)/shard_map/ppermute | solution.py:165
  24.9 45.3 %collective-permute-start.2 = (bf16[3,8,32,128]{3,2,1,0:T(8,128)(2,1)S(1)}, bf16[3,8,32,128]{3,2,1,0:T(8,128)(2,1)S(1)}, u32[]{:S(2)}, u32[]{:S(2)}) collective-permute-start(bf16[3,8,32,128]{3,2,1,0:T(8,128)(2,1)S(1)} %get-tuple-element.40), channel_id=1, source_target_pairs={{0,12},{4,8},{8,4},{12,0},{16,28},{20,24},{24,20},{28,16},{1,13},{... | collective-permute-start | bytes 589832 | tf_op jit(solution)/shard_map/ppermute | solution.py:165
  29.5 40.8 %collective-permute-start.3 = (bf16[3,8,32,128]{3,2,1,0:T(8,128)(2,1)S(1)}, bf16[3,8,32,128]{3,2,1,0:T(8,128)(2,1)S(1)}, u32[]{:S(2)}, u32[]{:S(2)}) collective-permute-start(bf16[3,8,32,128]{3,2,1,0:T(8,128)(2,1)S(1)} %get-tuple-element.41), channel_id=1, source_target_pairs={{0,16},{4,20},{8,24},{12,28},{16,0},{20,4},{24,8},{28,12},{1,17},{... | collective-permute-start | bytes 589832 | tf_op jit(solution)/shard_map/ppermute | solution.py:165
  33.0 37.9 %collective-permute-start.4 = (bf16[3,8,32,128]{3,2,1,0:T(8,128)(2,1)S(1)}, bf16[3,8,32,128]{3,2,1,0:T(8,128)(2,1)S(1)}, u32[]{:S(2)}, u32[]{:S(2)}) collective-permute-start(bf16[3,8,32,128]{3,2,1,0:T(8,128)(2,1)S(1)} %get-tuple-element.42), channel_id=1, source_target_pairs={{0,20},{4,16},{8,28},{12,24},{16,4},{20,0},{24,12},{28,8},{1,21},{... | collective-permute-start | bytes 589832 | tf_op jit(solution)/shard_map/ppermute | solution.py:165
  34.8 37.4 %collective-permute-start.5 = (bf16[3,8,32,128]{3,2,1,0:T(8,128)(2,1)S(1)}, bf16[3,8,32,128]{3,2,1,0:T(8,128)(2,1)S(1)}, u32[]{:S(2)}, u32[]{:S(2)}) collective-permute-start(bf16[3,8,32,128]{3,2,1,0:T(8,128)(2,1)S(1)} %get-tuple-element.43), channel_id=1, source_target_pairs={{0,24},{4,28},{8,16},{12,20},{16,8},{20,12},{24,0},{28,4},{1,25},{... | collective-permute-start | bytes 589832 | tf_op jit(solution)/shard_map/ppermute | solution.py:165
  36.1 37.3 %collective-permute-start.6 = (bf16[3,8,32,128]{3,2,1,0:T(8,128)(2,1)S(1)}, bf16[3,8,32,128]{3,2,1,0:T(8,128)(2,1)S(1)}, u32[]{:S(2)}, u32[]{:S(2)}) collective-permute-start(bf16[3,8,32,128]{3,2,1,0:T(8,128)(2,1)S(1)} %get-tuple-element.44), channel_id=1, source_target_pairs={{0,28},{4,24},{8,20},{12,16},{16,12},{20,8},{24,4},{28,0},{1,29},{... | collective-permute-start | bytes 589832 | tf_op jit(solution)/shard_map/ppermute | solution.py:165
  70.3 6.0 %collective-permute-start.21 = (bf16[4,32,128]{2,1,0:T(8,128)(2,1)S(1)}, bf16[4,32,128]{2,1,0:T(8,128)(2,1)S(1)}, u32[]{:S(2)}, u32[]{:S(2)}) collective-permute-start(bf16[4,32,128]{2,1,0:T(8,128)(2,1)S(1)} %get-tuple-element.62), channel_id=1, source_target_pairs={{0,4},{4,0},{8,12},{12,8},{16,20},{20,16},{24,28},{28,24},{1,5},{5... | collective-permute-start | bytes 98312 | tf_op jit(solution)/shard_map/ppermute | solution.py:165
  70.4 7.5 %collective-permute-start.22 = (bf16[4,32,128]{2,1,0:T(8,128)(2,1)S(1)}, bf16[4,32,128]{2,1,0:T(8,128)(2,1)S(1)}, u32[]{:S(2)}, u32[]{:S(2)}) collective-permute-start(bf16[4,32,128]{2,1,0:T(8,128)(2,1)S(1)} %get-tuple-element.63), channel_id=1, source_target_pairs={{0,8},{4,12},{8,0},{12,4},{16,24},{20,28},{24,16},{28,20},{1,9},{5... | collective-permute-start | bytes 98312 | tf_op jit(solution)/shard_map/ppermute | solution.py:165
  70.9 7.4 %collective-permute-start.23 = (bf16[4,32,128]{2,1,0:T(8,128)(2,1)S(1)}, bf16[4,32,128]{2,1,0:T(8,128)(2,1)S(1)}, u32[]{:S(2)}, u32[]{:S(2)}) collective-permute-start(bf16[4,32,128]{2,1,0:T(8,128)(2,1)S(1)} %get-tuple-element.64), channel_id=1, source_target_pairs={{0,12},{4,8},{8,4},{12,0},{16,28},{20,24},{24,20},{28,16},{1,13},{... | collective-permute-start | bytes 98312 | tf_op jit(solution)/shard_map/ppermute | solution.py:165
  72.2 8.2 %collective-permute-start.24 = (bf16[4,32,128]{2,1,0:T(8,128)(2,1)S(1)}, bf16[4,32,128]{2,1,0:T(8,128)(2,1)S(1)}, u32[]{:S(2)}, u32[]{:S(2)}) collective-permute-start(bf16[4,32,128]{2,1,0:T(8,128)(2,1)S(1)} %get-tuple-element.65), channel_id=1, source_target_pairs={{0,16},{4,20},{8,24},{12,28},{16,0},{20,4},{24,8},{28,12},{1,17},{... | collective-permute-start | bytes 98312 | tf_op jit(solution)/shard_map/ppermute | solution.py:165
  76.1 10.2 %collective-permute-start.7 = (bf16[8,32,128]{2,1,0:T(8,128)(2,1)S(1)}, bf16[8,32,128]{2,1,0:T(8,128)(2,1)S(1)}, u32[]{:S(2)}, u32[]{:S(2)}) collective-permute-start(bf16[8,32,128]{2,1,0:T(8,128)(2,1)S(1)} %get-tuple-element.46), channel_id=1, source_target_pairs={{0,4},{4,0},{8,12},{12,8},{16,20},{20,16},{24,28},{28,24},{1,5},{5... | collective-permute-start | bytes 196616 | tf_op jit(solution)/shard_map/ppermute | solution.py:165
  76.3 11.9 %collective-permute-start.8 = (bf16[8,32,128]{2,1,0:T(8,128)(2,1)S(1)}, bf16[8,32,128]{2,1,0:T(8,128)(2,1)S(1)}, u32[]{:S(2)}, u32[]{:S(2)}) collective-permute-start(bf16[8,32,128]{2,1,0:T(8,128)(2,1)S(1)} %get-tuple-element.47), channel_id=1, source_target_pairs={{0,8},{4,12},{8,0},{12,4},{16,24},{20,28},{24,16},{28,20},{1,9},{5... | collective-permute-start | bytes 196616 | tf_op jit(solution)/shard_map/ppermute | solution.py:165
  77.9 5.0 %collective-permute-start.25 = (bf16[4,32,128]{2,1,0:T(8,128)(2,1)S(1)}, bf16[4,32,128]{2,1,0:T(8,128)(2,1)S(1)}, u32[]{:S(2)}, u32[]{:S(2)}) collective-permute-start(bf16[4,32,128]{2,1,0:T(8,128)(2,1)S(1)} %get-tuple-element.66), channel_id=1, source_target_pairs={{0,20},{4,16},{8,28},{12,24},{16,4},{20,0},{24,12},{28,8},{1,21},{... | collective-permute-start | bytes 98312 | tf_op jit(solution)/shard_map/ppermute | solution.py:165
  78.2 5.7 %collective-permute-start.26 = (bf16[4,32,128]{2,1,0:T(8,128)(2,1)S(1)}, bf16[4,32,128]{2,1,0:T(8,128)(2,1)S(1)}, u32[]{:S(2)}, u32[]{:S(2)}) collective-permute-start(bf16[4,32,128]{2,1,0:T(8,128)(2,1)S(1)} %get-tuple-element.67), channel_id=1, source_target_pairs={{0,24},{4,28},{8,16},{12,20},{16,8},{20,12},{24,0},{28,4},{1,25},{... | collective-permute-start | bytes 98312 | tf_op jit(solution)/shard_map/ppermute | solution.py:165
  80.5 5.2 %collective-permute-start.27 = (bf16[4,32,128]{2,1,0:T(8,128)(2,1)S(1)}, bf16[4,32,128]{2,1,0:T(8,128)(2,1)S(1)}, u32[]{:S(2)}, u32[]{:S(2)}) collective-permute-start(bf16[4,32,128]{2,1,0:T(8,128)(2,1)S(1)} %get-tuple-element.68), channel_id=1, source_target_pairs={{0,28},{4,24},{8,20},{12,16},{16,12},{20,8},{24,4},{28,0},{1,29},{... | collective-permute-start | bytes 98312 | tf_op jit(solution)/shard_map/ppermute | solution.py:165
  82.9 7.2 %collective-permute-start.9 = (bf16[8,32,128]{2,1,0:T(8,128)(2,1)S(1)}, bf16[8,32,128]{2,1,0:T(8,128)(2,1)S(1)}, u32[]{:S(2)}, u32[]{:S(2)}) collective-permute-start(bf16[8,32,128]{2,1,0:T(8,128)(2,1)S(1)} %get-tuple-element.48), channel_id=1, source_target_pairs={{0,12},{4,8},{8,4},{12,0},{16,28},{20,24},{24,20},{28,16},{1,13},{... | collective-permute-start | bytes 196616 | tf_op jit(solution)/shard_map/ppermute | solution.py:165
  83.9 10.0 %collective-permute-start.10 = (bf16[8,32,128]{2,1,0:T(8,128)(2,1)S(1)}, bf16[8,32,128]{2,1,0:T(8,128)(2,1)S(1)}, u32[]{:S(2)}, u32[]{:S(2)}) collective-permute-start(bf16[8,32,128]{2,1,0:T(8,128)(2,1)S(1)} %get-tuple-element.49), channel_id=1, source_target_pairs={{0,16},{4,20},{8,24},{12,28},{16,0},{20,4},{24,8},{28,12},{1,17},{... | collective-permute-start | bytes 196616 | tf_op jit(solution)/shard_map/ppermute | solution.py:165
  85.7 10.2 %collective-permute-start.11 = (bf16[8,32,128]{2,1,0:T(8,128)(2,1)S(1)}, bf16[8,32,128]{2,1,0:T(8,128)(2,1)S(1)}, u32[]{:S(2)}, u32[]{:S(2)}) collective-permute-start(bf16[8,32,128]{2,1,0:T(8,128)(2,1)S(1)} %get-tuple-element.50), channel_id=1, source_target_pairs={{0,20},{4,16},{8,28},{12,24},{16,4},{20,0},{24,12},{28,8},{1,21},{... | collective-permute-start | bytes 196616 | tf_op jit(solution)/shard_map/ppermute | solution.py:165
  86.3 9.6 %collective-permute-start.12 = (bf16[8,32,128]{2,1,0:T(8,128)(2,1)S(1)}, bf16[8,32,128]{2,1,0:T(8,128)(2,1)S(1)}, u32[]{:S(2)}, u32[]{:S(2)}) collective-permute-start(bf16[8,32,128]{2,1,0:T(8,128)(2,1)S(1)} %get-tuple-element.51), channel_id=1, source_target_pairs={{0,24},{4,28},{8,16},{12,20},{16,8},{20,12},{24,0},{28,4},{1,25},{... | collective-permute-start | bytes 196616 | tf_op jit(solution)/shard_map/ppermute | solution.py:165
  88.1 7.8 %collective-permute-start.13 = (bf16[8,32,128]{2,1,0:T(8,128)(2,1)S(1)}, bf16[8,32,128]{2,1,0:T(8,128)(2,1)S(1)}, u32[]{:S(2)}, u32[]{:S(2)}) collective-permute-start(bf16[8,32,128]{2,1,0:T(8,128)(2,1)S(1)} %get-tuple-element.52), channel_id=1, source_target_pairs={{0,28},{4,24},{8,20},{12,16},{16,12},{20,8},{24,4},{28,0},{1,29},{... | collective-permute-start | bytes 196616 | tf_op jit(solution)/shard_map/ppermute | solution.py:165

commit v2 on v0

v2 whole, which is shorter than its diff:
```python
import functools
import math

import jax
import jax.numpy as jnp
from jax import lax
from jax.experimental import pallas as pl
from jax.experimental.pallas import tpu as pltpu
from jax.sharding import PartitionSpec as P


LOG2E = 1.4426950408889634
PARTS = 3
NT = (((1,), (1,)), ((), ()))
PARAMS = pltpu.CompilerParams(vmem_limit_bytes=20 * 1024 * 1024)
SMEM = pl.BlockSpec(memory_space=pltpu.SMEM)
VMEM = pl.BlockSpec(memory_space=pltpu.VMEM)
HBM = pl.BlockSpec(memory_space=pltpu.HBM)


def in_hbm(x):
    return pltpu.with_memory_space_constraint(x, pltpu.HBM)


class Dims:
    def __init__(self, n_row, n_col, heads, head_dim, row_dev, col_dev):
        self.n_row, self.n_col, self.head_dim = n_row, n_col, head_dim
        self.row_dev, self.col_dev, self.heads = row_dev, col_dev, heads
        self.head_groups = math.gcd(heads, n_row)
        self.col_groups = n_row // self.head_groups
        self.heads_g = heads // self.head_groups
        self.cols_g = col_dev // self.col_groups
        self.pairs = self.heads_g * self.cols_g
        self.width = self.heads_g * head_dim
        self.patches = row_dev * col_dev
        self.rows = n_row * row_dev
        self.sent_rows = 3 * self.pairs * row_dev
        self.back_rows = (self.pairs + 1) * row_dev

    def lane(self, me, kg):
        return pl.multiple_of(((me // self.col_groups) ^ kg) * self.width, 128)

    def column(self, me, kl, c):
        return ((me % self.col_groups) ^ kl) * self.cols_g + c


def spread_kernel(dims, kgs, me_ref, *refs):
    args, outs, (raw, wide, sems) = refs[:3], refs[3:-3], refs[-3:]
    me, head_dim, row_dev = me_ref[0], dims.head_dim, dims.row_dev
    loads = {}
    for i, kg in enumerate(kgs):
        for t, arg in enumerate(args):
            loads[i, t] = pltpu.make_async_copy(
                arg.at[:, :, pl.ds(dims.lane(me, kg), dims.width)], raw.at[i, t], sems.at[i, t]
            )
            loads[i, t].start()
    slot = 0
    for i in range(len(kgs)):
        for t in range(3):
            loads[i, t].wait()
            for j in range(dims.heads_g):
                wide[slot] = (
                    raw[i, t, :, :, j * head_dim : (j + 1) * head_dim]
                    .astype(jnp.float32)
                    .reshape(dims.patches, head_dim)
                )
                for kl in range(dims.col_groups):
                    for c in range(dims.cols_g):
                        at = (t * dims.pairs + j * dims.cols_g + c) * row_dev
                        outs[i * dims.col_groups + kl][at : at + row_dev] = wide[
                            slot,
                            pl.ds(dims.column(me, kl, c), row_dev, stride=dims.col_dev),
                            :,
                        ].astype(jnp.bfloat16)
                slot = (slot + 1) % wide.shape[0]


def spread(dims, kgs, me, args):
    block = jax.ShapeDtypeStruct((dims.sent_rows, dims.head_dim), jnp.bfloat16)
    count = len(kgs) * dims.col_groups
    return pl.pallas_call(
        functools.partial(spread_kernel, dims, kgs),
        out_shape=[block] * count,
        in_specs=[SMEM] + [HBM] * 3,
        out_specs=[VMEM] * count,
        scratch_shapes=[
            pltpu.VMEM((len(kgs), 3, dims.row_dev, dims.col_dev, dims.width), jnp.bfloat16),
            pltpu.VMEM((4, dims.patches, dims.head_dim), jnp.float32),
            pltpu.SemaphoreType.DMA((len(kgs), 3)),
        ],
        compiler_params=PARAMS,
        name="spread",
    )(me, *[in_hbm(arg) for arg in args])


def pool_kernel(dims, k_ref, v_ref, out_ref, raw, sems):
    loads = [
        pltpu.make_async_copy(ref, raw.at[i], sems.at[i]) for i, ref in enumerate((k_ref, v_ref))
    ]
    for load in loads:
        load.start()
    for i, load in enumerate(loads):
        load.wait()
        total = jnp.zeros((dims.col_dev, raw.shape[-1]), jnp.float32)
        for r in range(dims.row_dev):
            total = total + raw[i, r].astype(jnp.float32)
        mean = jnp.sum(total, axis=0, keepdims=True) * (1.0 / dims.patches)
        out_ref[i : i + 1] = mean.astype(jnp.bfloat16).astype(jnp.float32)


def pool(dims, keys, values):
    return pl.pallas_call(
        functools.partial(pool_kernel, dims),
        out_shape=jax.ShapeDtypeStruct((2, keys.shape[-1]), jnp.float32),
        in_specs=[HBM] * 2,
        out_specs=VMEM,
        scratch_shapes=[
            pltpu.VMEM((2,) + keys.shape, jnp.bfloat16),
            pltpu.SemaphoreType.DMA((2,)),
        ],
        compiler_params=PARAMS,
        name="pool",
    )(in_hbm(keys), in_hbm(values)).astype(jnp.bfloat16)


def recall_kernel(dims, bias_ref, q_ref, key_ref, value_ref, out_ref, lse_ref, raw, sem):
    load = pltpu.make_async_copy(q_ref, raw, sem)
    load.start()
    load.wait()
    head_dim = dims.head_dim
    scale = LOG2E / math.sqrt(head_dim)
    ones = jnp.ones((dims.n_col, head_dim), jnp.bfloat16)
    for h in range(dims.heads):
        lanes = slice(h * head_dim, (h + 1) * head_dim)
        query = raw[:, :, lanes].reshape(dims.patches, head_dim)
        value = jnp.concatenate([value_ref[:, lanes], ones], axis=1)
        score = lax.dot_general(query, key_ref[:, lanes], NT, preferred_element_type=jnp.float32)
        score = score * scale + bias_ref[h] * LOG2E
        peak = jnp.max(score, axis=1, keepdims=True)
        weight = jnp.exp2(score - peak).astype(jnp.bfloat16)
        mixed = jnp.dot(weight, value, preferred_element_type=jnp.float32)
        total = mixed[:, head_dim:]
        out_ref[:, lanes] = mixed[:, :head_dim] / total
        lse_ref[:, lanes] = peak + jnp.log2(total)


def recall(dims, bias, queries, key, value):
    out = jax.ShapeDtypeStruct((dims.patches, queries.shape[-1]), jnp.float32)
    return pl.pallas_call(
        functools.partial(recall_kernel, dims),
        out_shape=[out] * 2,
        in_specs=[SMEM, HBM] + [VMEM] * 2,
        out_specs=[VMEM] * 2,
        scratch_shapes=[pltpu.VMEM(queries.shape, jnp.bfloat16), pltpu.SemaphoreType.DMA],
        compiler_params=PARAMS,
        name="recall",
    )(bias, in_hbm(queries), key, value)


def attend_kernel(dims, ks, *refs):
    ins, outs = refs[: dims.n_row], refs[dims.n_row :]
    row_dev, head_dim, rows = dims.row_dev, dims.head_dim, dims.rows
    count = len(ks) * row_dev
    scale = LOG2E / math.sqrt(head_dim)
    ones = jnp.ones((rows, head_dim), jnp.bfloat16)
    lane = lax.broadcasted_iota(jnp.int32, (count, head_dim), 1)
    tail = jnp.zeros((count, head_dim), jnp.float32)

    def gather(t, pair, sources):
        at = (t * dims.pairs + pair) * row_dev
        return jnp.concatenate([ins[k][at : at + row_dev] for k in sources], axis=0)

    for pair in range(dims.pairs):
        query = gather(0, pair, ks)
        key = gather(1, pair, range(dims.n_row))
        value = jnp.concatenate([gather(2, pair, range(dims.n_row)), ones], axis=1)
        score = lax.dot_general(query, key, NT, preferred_element_type=jnp.float32) * scale
        peak = jnp.max(score, axis=1, keepdims=True)
        weight = jnp.exp2(score - peak).astype(jnp.bfloat16)
        mixed = jnp.dot(weight, value, preferred_element_type=jnp.float32)
        total = mixed[:, head_dim:]
        out = (mixed[:, :head_dim] / total).astype(jnp.bfloat16)
        rest = peak + jnp.log2(total)
        for part in range(PARTS):
            term = rest.astype(jnp.bfloat16).astype(jnp.float32)
            tail = jnp.where(lane == pair * PARTS + part, term, tail)
            rest = rest - term
        for i in range(len(ks)):
            outs[i][pair * row_dev : (pair + 1) * row_dev] = out[i * row_dev : (i + 1) * row_dev]
    tail = tail.astype(jnp.bfloat16)
    for i in range(len(ks)):
        outs[i][dims.pairs * row_dev :] = tail[i * row_dev : (i + 1) * row_dev]


def attend(dims, ks, blocks):
    block = jax.ShapeDtypeStruct((dims.back_rows, dims.head_dim), jnp.bfloat16)
    return pl.pallas_call(
        functools.partial(attend_kernel, dims, ks),
        out_shape=[block] * len(ks),
        in_specs=[VMEM] * dims.n_row,
        out_specs=[VMEM] * len(ks),
        compiler_params=PARAMS,
        name="attend",
    )(*blocks)


def collect_kernel(dims, kgs, me_ref, mem_ref, lse_ref, *refs):
    blocks = refs[: len(kgs) * dims.col_groups]
    out, wide, wide_lse, done, sems = refs[-5:]
    me, head_dim, row_dev = me_ref[0], dims.head_dim, dims.row_dev
    row = lax.broadcasted_iota(jnp.int32, (head_dim, dims.pairs * head_dim), 0)
    col = lax.broadcasted_iota(jnp.int32, (head_dim, dims.pairs * head_dim), 1)
    pick = jnp.where(row // PARTS == col // head_dim, 1.0, 0.0).astype(jnp.bfloat16)
    stores = []
    slot = 0
    for i, kg in enumerate(kgs):
        mine = blocks[i * dims.col_groups : (i + 1) * dims.col_groups]
        tails = [ref[dims.pairs * row_dev :] for ref in mine]
        tails = jnp.concatenate(tails, axis=0)
        lses = jnp.dot(tails, pick, preferred_element_type=jnp.float32)
        lane = dims.lane(me, kg)
        for j in range(dims.heads_g):
            for kl, ref in enumerate(mine):
                for c in range(dims.cols_g):
                    pair = j * dims.cols_g + c
                    to = pl.ds(dims.column(me, kl, c), row_dev, stride=dims.col_dev)
                    wide[slot, to, :] = ref[pair * row_dev : (pair + 1) * row_dev].astype(
                        jnp.float32
                    )
                    wide_lse[slot, to, :] = lses[
                        kl * row_dev : (kl + 1) * row_dev, pair * head_dim : (pair + 1) * head_dim
                    ]
            at = pl.ds(pl.multiple_of(lane + j * head_dim, 128), head_dim)
            mem = mem_ref[:, at]
            share = 1.0 / (1.0 + jnp.exp2(lse_ref[:, at] - wide_lse[slot]))
            value = mem + share * (wide[slot] - mem)
            done[i, :, :, j * head_dim : (j + 1) * head_dim] = value.astype(jnp.bfloat16).reshape(
                row_dev, dims.col_dev, head_dim
            )
            slot = (slot + 1) % wide.shape[0]
        stores.append(
            pltpu.make_async_copy(
                done.at[i], out.at[:, :, pl.ds(lane, dims.width)], sems.at[i]
            )
        )
        stores[-1].start()
    for store in stores:
        store.wait()


def collect(dims, kgs, me, mem, lse, blocks, out=None):
    shape = (dims.row_dev, dims.col_dev, dims.heads * dims.head_dim)
    operands = (me, mem, lse, *blocks) + (() if out is None else (out,))
    return pl.pallas_call(
        functools.partial(collect_kernel, dims, kgs),
        out_shape=jax.ShapeDtypeStruct(shape, jnp.bfloat16),
        in_specs=[SMEM] + [VMEM] * (2 + len(blocks)) + [HBM] * (out is not None),
        out_specs=HBM,
        scratch_shapes=[
            pltpu.VMEM((4, dims.patches, dims.head_dim), jnp.float32),
            pltpu.VMEM((4, dims.patches, dims.head_dim), jnp.float32),
            pltpu.VMEM((len(kgs),) + shape[:2] + (dims.width,), jnp.bfloat16),
            pltpu.SemaphoreType.DMA((len(kgs),)),
        ],
        input_output_aliases={} if out is None else {len(operands) - 1: 0},
        compiler_params=PARAMS,
        name="collect",
    )(*operands)


def exchange(dims, ks, blocks):
    return [
        lax.ppermute(block, "row", [(i, i ^ k) for i in range(dims.n_row)]) if k else block
        for k, block in zip(ks, blocks)
    ]


def per_device(queries, keys, values, memory_bias):
    row_dev, col_dev, model_width = queries.shape
    n_row, n_col = lax.axis_size("row"), lax.axis_size("col")
    heads = memory_bias.shape[0]
    dims = Dims(n_row, n_col, heads, model_width // heads, row_dev, col_dev)
    me = lax.axis_index("row").astype(jnp.int32).reshape(1)
    args = (queries, keys, values)
    near_kgs, far_kgs = range(dims.head_groups // 2), range(dims.head_groups // 2, dims.head_groups)
    near = range(n_row // 2)
    far = range(n_row // 2, n_row)

    sent_far = list(spread(dims, far_kgs, me, args))
    me, sent_far[0] = lax.optimization_barrier((me, sent_far[0]))
    got_far = exchange(dims, far, sent_far)
    got_near = exchange(dims, near, spread(dims, near_kgs, me, args))

    pooled = pool(dims, keys, values)
    band = lax.all_gather(pooled[None], "col", axis=0, tiled=True)
    mem, lse = recall(dims, memory_bias, queries, band[:, 0], band[:, 1])

    blocks, mem, lse = lax.optimization_barrier((got_near + got_far, mem, lse))
    back_far = attend(dims, far, blocks)
    blocks, back_far = lax.optimization_barrier((blocks, back_far))
    home_far = exchange(dims, far, back_far)
    home_near = exchange(dims, near, attend(dims, near, blocks))
    out = collect(dims, near_kgs, me, mem, lse, home_near)
    return collect(dims, far_kgs, me, mem, lse, home_far, out)


def solution(mesh):
    return jax.shard_map(
        per_device,
        mesh=mesh,
        in_specs=(P("row", "col", None), P("row", "col", None), P("row", "col", None), P()),
        out_specs=P("row", "col", None),
        check_vma=False,
    )
```

time: 222 us -> 81.8 us (0.37)
  the two profiles are of different devices: /device:TPU:0 before, /device:TPU:11 now
where the time goes in v2:
time: 81.8 us; the launch traced here: 81.6 us
  waiting for transfers between devices  47.6 us (58%)
  starting transfers between devices  14.1 us (17%)
  Pallas kernels  13.1 us (16%)
  blocking collectives  6.61 us (8%)
    ppermute x14, waiting for transfers between devices, exchange(): lax.ppermute(block, 'row', [(i, i ^ k) for i in range(dims.n_row)])  47.6 us
    ppermute x14, starting transfers between devices, exchange(): lax.ppermute(block, 'row', [(i, i ^ k) for i in range(dims.n_row)])  14.1 us
    all_gather x1, blocking collectives, per_device(): band = lax.all_gather(pooled[None], 'col', axis=0, tiled=True)  6.61 us
    pallas_call x1, Pallas kernels, recall(): pl.pallas_call(functools.partial(recall_kernel, dims), out_shape=[out] *...  3.62 us
    pallas_call x2, Pallas kernels, spread(): pl.pallas_call(functools.partial(spread_kernel, dims, kgs), out_shape=[bl...  3.15 us
    pallas_call x2, Pallas kernels, collect(): pl.pallas_call(functools.partial(collect_kernel, dims, kgs), out_shape=ja...  2.97 us
    pallas_call x2, Pallas kernels, attend(): pl.pallas_call(functools.partial(attend_kernel, dims, ks), out_shape=[blo...  1.88 us
  transfers between devices with their start and end apart: 14, of which 8 were waited for; matrix products, arithmetic and copies ran while one was open for 0% of the time, Pallas kernels for 10%

profile of v2, /device:TPU:11, one launch (start us, length us, event | category | flops | bytes accessed | tf_op | source)
XLA Modules:
  0.0 81.6 jit_solution(12700650765442417105)
XLA Ops:
  0.0 1.6 %spread.2 = (bf16[1152,128]{1,0:T(8,128)(2,1)S(1)}, bf16[1152,128]{1,0:T(8,128)(2,1)S(1)}, bf16[1152,128]{1,0:T(8,128)(2,1)S(1)}, bf16[1152,128]{1,0:T(8,128)(2,1)S(1)}) custom-call(s32[1]{0:T(128)} %bitcast.me_ref, bf16[32,8,1536]{2,1,0:T(8,128)(2,1)} %q_ref.1, bf16[32,8,1536]{2,1,0:T(8,128)(2,1)} %k_ref.1, bf16[32,8,1536]{2,1,0:T(8,128)(2,1)} %v_ref.1), custom_call_target="tpu_custom_call" | custom-call | tf_op jit(solution)/shard_map/spread/pallas_call | solution.py:81
  1.6 2.4 %collective-permute-start.3 = (bf16[1152,128]{1,0:T(8,128)(2,1)S(1)}, bf16[1152,128]{1,0:T(8,128)(2,1)S(1)}, u32[]{:S(2)}, u32[]{:S(2)}) collective-permute-start(bf16[1152,128]{1,0:T(8,128)(2,1)S(1)} %get-tuple-element.53), channel_id=1, source_target_pairs={{0,16},{4,20},{8,24},{12,28},{16,0},{20,4},{24,8},{28,12},{1,17},{... | collective-permute-start | bytes 884744 | tf_op jit(solution)/shard_map/ppermute | solution.py:273
  4.0 0.9 %collective-permute-start.4 = (bf16[1152,128]{1,0:T(8,128)(2,1)S(1)}, bf16[1152,128]{1,0:T(8,128)(2,1)S(1)}, u32[]{:S(2)}, u32[]{:S(2)}) collective-permute-start(bf16[1152,128]{1,0:T(8,128)(2,1)S(1)} %get-tuple-element.54), channel_id=1, source_target_pairs={{0,20},{4,16},{8,28},{12,24},{16,4},{20,0},{24,12},{28,8},{1,21},{... | collective-permute-start | bytes 884744 | tf_op jit(solution)/shard_map/ppermute | solution.py:273
  4.9 1.3 %collective-permute-start.5 = (bf16[1152,128]{1,0:T(8,128)(2,1)S(1)}, bf16[1152,128]{1,0:T(8,128)(2,1)S(1)}, u32[]{:S(2)}, u32[]{:S(2)}) collective-permute-start(bf16[1152,128]{1,0:T(8,128)(2,1)S(1)} %get-tuple-element.55), channel_id=1, source_target_pairs={{0,24},{4,28},{8,16},{12,20},{16,8},{20,12},{24,0},{28,4},{1,25},{... | collective-permute-start | bytes 884744 | tf_op jit(solution)/shard_map/ppermute | solution.py:273
  6.2 0.0 copy-start
  6.2 0.4 collective-permute-start.6
  6.6 1.6 %spread.3 = (bf16[1152,128]{1,0:T(8,128)(2,1)S(1)}, bf16[1152,128]{1,0:T(8,128)(2,1)S(1)}, bf16[1152,128]{1,0:T(8,128)(2,1)S(1)}, bf16[1152,128]{1,0:T(8,128)(2,1)S(1)}) custom-call(s32[1]{0:T(128)} %bitcast.me_ref, bf16[32,8,1536]{2,1,0:T(8,128)(2,1)} %q_ref.1, bf16[32,8,1536]{2,1,0:T(8,128)(2,1)} %k_ref.1, bf16[32,8,1536]{2,1,0:T(8,128)(2,1)} %v_ref.1), custom_call_target="tpu_custom_call" | custom-call | tf_op jit(solution)/shard_map/spread/pallas_call | solution.py:81
  8.1 0.2 collective-permute-start
  8.4 1.5 %pool.1 = f32[2,1536]{1,0:T(2,128)S(1)} custom-call(bf16[32,8,1536]{2,1,0:T(8,128)(2,1)} %k_ref.1, bf16[32,8,1536]{2,1,0:T(8,128)(2,1)} %v_ref.1), custom_call_target="tpu_custom_call" | custom-call | tf_op jit(solution)/shard_map/pool/pallas_call | solution.py:112
  9.9 6.6 %all-gather.1 = bf16[4,2,1536]{2,1,0:T(2,128)(2,1)S(1)} all-gather(bf16[1,2,1536]{2,1,0:T(2,128)(2,1)S(1)} %convert_bitcast_fusion), channel_id=2, replica_groups=mesh['row'=8,'col'=4] {'col'}, dimensions={0}, use_global_device_ids=true | all-gather | bytes 30720 | tf_op jit(solution)/shard_map/all_gather | solution.py:295
  16.6 19.3 %collective-permute-done.3.refs_4_ = bf16[1152,128]{1,0:T(8,128)(2,1)S(1)} collective-permute-done((bf16[1152,128]{1,0:T(8,128)(2,1)S(1)}, bf16[1152,128]{1,0:T(8,128)(2,1)S(1)}, u32[]{:S(2)}, u32[]{:S(2)}) %collective-permute-start.3) | collective-permute-done | bytes 294944 | tf_op jit(solution)/shard_map/ppermute | solution.py:273
  35.9 0.0 collective-permute-start.1
  35.9 6.3 %collective-permute-done.4.refs_5_ = bf16[1152,128]{1,0:T(8,128)(2,1)S(1)} collective-permute-done((bf16[1152,128]{1,0:T(8,128)(2,1)S(1)}, bf16[1152,128]{1,0:T(8,128)(2,1)S(1)}, u32[]{:S(2)}, u32[]{:S(2)}) %collective-permute-start.4) | collective-permute-done | bytes 294944 | tf_op jit(solution)/shard_map/ppermute | solution.py:273
  42.2 0.4 collective-permute-start.2
  42.6 0.0 copy-done
  42.6 3.6 %recall.1 = (f32[256,1536]{1,0:T(8,128)S(1)}, f32[256,1536]{1,0:T(8,128)S(1)}) custom-call(f32[12]{0:T(128)S(1)} %copy-done, bf16[32,8,1536]{2,1,0:T(8,128)(2,1)} %q_ref.1, bf16[4,1536]{1,0:T(4,128)(2,1)S(1)} %get-tuple-element.92.key_ref, bf16[4,1536]{1,0:T(4,128)(2,1)S(1)} %get-tuple-element.91.value_ref), custom_call_target="tpu_custom_call" | custom-call | tf_op jit(solution)/shard_map/recall/pallas_call | solution.py:149
  46.3 2.3 %collective-permute-done.5.refs_6_ = bf16[1152,128]{1,0:T(8,128)(2,1)S(1)} collective-permute-done((bf16[1152,128]{1,0:T(8,128)(2,1)S(1)}, bf16[1152,128]{1,0:T(8,128)(2,1)S(1)}, u32[]{:S(2)}, u32[]{:S(2)}) %collective-permute-start.5) | collective-permute-done | bytes 294944 | tf_op jit(solution)/shard_map/ppermute | solution.py:273
  48.5 6.3 %collective-permute-done.6.refs_7_ = bf16[1152,128]{1,0:T(8,128)(2,1)S(1)} collective-permute-done((bf16[1152,128]{1,0:T(8,128)(2,1)S(1)}, bf16[1152,128]{1,0:T(8,128)(2,1)S(1)}, u32[]{:S(2)}, u32[]{:S(2)}) %collective-permute-start.6) | collective-permute-done | bytes 294944 | tf_op jit(solution)/shard_map/ppermute | solution.py:273
  54.9 0.0 collective-permute-done.refs_1_
  54.9 0.0 collective-permute-done.1.refs_2_
  54.9 0.0 collective-permute-done.2.refs_3_
  54.9 0.9 %attend.2 = (bf16[416,128]{1,0:T(8,128)(2,1)S(1)}, bf16[416,128]{1,0:T(8,128)(2,1)S(1)}, bf16[416,128]{1,0:T(8,128)(2,1)S(1)}, bf16[416,128]{1,0:T(8,128)(2,1)S(1)}) custom-call(bf16[1152,128]{1,0:T(8,128)(2,1)S(1)} %get-tuple-element.77.refs_0_, bf16[1152,128]{1,0:T(8,128)(2,1)S(1)} %collective-permute-done.refs_1_, ...), custom_call_target="tpu_custom_call" | custom-call | tf_op jit(solution)/shard_map/attend/pallas_call | solution.py:197
  55.8 0.9 %attend.3 = (bf16[416,128]{1,0:T(8,128)(2,1)S(1)}, bf16[416,128]{1,0:T(8,128)(2,1)S(1)}, bf16[416,128]{1,0:T(8,128)(2,1)S(1)}, bf16[416,128]{1,0:T(8,128)(2,1)S(1)}) custom-call(bf16[1152,128]{1,0:T(8,128)(2,1)S(1)} %get-tuple-element.77.refs_0_, bf16[1152,128]{1,0:T(8,128)(2,1)S(1)} %collective-permute-done.refs_1_, ...), custom_call_target="tpu_custom_call" | custom-call | tf_op jit(solution)/shard_map/attend/pallas_call | solution.py:197
  56.8 0.6 collective-permute-start.11
  57.3 0.9 %collective-permute-start.12 = (bf16[416,128]{1,0:T(8,128)(2,1)S(1)}, bf16[416,128]{1,0:T(8,128)(2,1)S(1)}, u32[]{:S(2)}, u32[]{:S(2)}) collective-permute-start(bf16[416,128]{1,0:T(8,128)(2,1)S(1)} %get-tuple-element.87), channel_id=1, source_target_pairs={{0,8},{4,12},{8,0},{12,4},{16,24},{20,28},{24,16},{28,20},{1,9},{5... | collective-permute-start | bytes 319496 | tf_op jit(solution)/shard_map/ppermute | solution.py:273
  58.2 2.4 %collective-permute-start.7 = (bf16[416,128]{1,0:T(8,128)(2,1)S(1)}, bf16[416,128]{1,0:T(8,128)(2,1)S(1)}, u32[]{:S(2)}, u32[]{:S(2)}) collective-permute-start(bf16[416,128]{1,0:T(8,128)(2,1)S(1)} %get-tuple-element.73), channel_id=1, source_target_pairs={{0,16},{4,20},{8,24},{12,28},{16,0},{20,4},{24,8},{28,12},{1,17},{... | collective-permute-start | bytes 319496 | tf_op jit(solution)/shard_map/ppermute | solution.py:273
  60.6 1.7 %collective-permute-start.13 = (bf16[416,128]{1,0:T(8,128)(2,1)S(1)}, bf16[416,128]{1,0:T(8,128)(2,1)S(1)}, u32[]{:S(2)}, u32[]{:S(2)}) collective-permute-start(bf16[416,128]{1,0:T(8,128)(2,1)S(1)} %get-tuple-element.88), channel_id=1, source_target_pairs={{0,12},{4,8},{8,4},{12,0},{16,28},{20,24},{24,20},{28,16},{1,13},{... | collective-permute-start | bytes 319496 | tf_op jit(solution)/shard_map/ppermute | solution.py:273
  62.3 0.0 collective-permute-start.8
  62.3 0.0 collective-permute-done.11.refs_1_
  62.3 1.2 %collective-permute-start.9 = (bf16[416,128]{1,0:T(8,128)(2,1)S(1)}, bf16[416,128]{1,0:T(8,128)(2,1)S(1)}, u32[]{:S(2)}, u32[]{:S(2)}) collective-permute-start(bf16[416,128]{1,0:T(8,128)(2,1)S(1)} %get-tuple-element.75), channel_id=1, source_target_pairs={{0,24},{4,28},{8,16},{12,20},{16,8},{20,12},{24,0},{28,4},{1,25},{... | collective-permute-start | bytes 319496 | tf_op jit(solution)/shard_map/ppermute | solution.py:273
  63.5 0.0 collective-permute-done.12.refs_2_
  63.5 1.7 %collective-permute-start.10 = (bf16[416,128]{1,0:T(8,128)(2,1)S(1)}, bf16[416,128]{1,0:T(8,128)(2,1)S(1)}, u32[]{:S(2)}, u32[]{:S(2)}) collective-permute-start(bf16[416,128]{1,0:T(8,128)(2,1)S(1)} %get-tuple-element.76), channel_id=1, source_target_pairs={{0,28},{4,24},{8,20},{12,16},{16,12},{20,8},{24,4},{28,0},{1,29},{... | collective-permute-start | bytes 319496 | tf_op jit(solution)/shard_map/ppermute | solution.py:273
  65.2 3.2 %collective-permute-done.13.refs_3_ = bf16[416,128]{1,0:T(8,128)(2,1)S(1)} collective-permute-done((bf16[416,128]{1,0:T(8,128)(2,1)S(1)}, bf16[416,128]{1,0:T(8,128)(2,1)S(1)}, u32[]{:S(2)}, u32[]{:S(2)}) %collective-permute-start.13) | collective-permute-done | bytes 106528 | tf_op jit(solution)/shard_map/ppermute | solution.py:273
  68.4 1.5 %collect.2.refs_4_ = bf16[32,8,1536]{2,1,0:T(8,128)(2,1)} custom-call(s32[1]{0:T(128)} %bitcast.me_ref, f32[256,1536]{1,0:T(8,128)S(1)} %get-tuple-element.59.mem_ref, f32[256,1536]{1,0:T(8,128)S(1)} %get-tuple-element.60.lse_ref, bf16[416,128]{1,0:T(8,128)(2,1)S(1)} %get-tuple-element.85.refs_0_, bf16[416,128]{1,0:T(8,128)(2,1)S(1)} %collective-permute-done.11.refs_1_, ...), custom_call_target="tpu_custom_call" | custom-call | tf_op jit(solution)/shard_map/collect/pallas_call | solution.py:254
  69.9 0.0 collective-permute-done.7.refs_0_
  69.9 3.9 %collective-permute-done.8.refs_1_ = bf16[416,128]{1,0:T(8,128)(2,1)S(1)} collective-permute-done((bf16[416,128]{1,0:T(8,128)(2,1)S(1)}, bf16[416,128]{1,0:T(8,128)(2,1)S(1)}, u32[]{:S(2)}, u32[]{:S(2)}) %collective-permute-start.8) | collective-permute-done | bytes 106528 | tf_op jit(solution)/shard_map/ppermute | solution.py:273
  73.8 4.0 %collective-permute-done.9.refs_2_ = bf16[416,128]{1,0:T(8,128)(2,1)S(1)} collective-permute-done((bf16[416,128]{1,0:T(8,128)(2,1)S(1)}, bf16[416,128]{1,0:T(8,128)(2,1)S(1)}, u32[]{:S(2)}, u32[]{:S(2)}) %collective-permute-start.9) | collective-permute-done | bytes 106528 | tf_op jit(solution)/shard_map/ppermute | solution.py:273
  77.8 2.3 %collective-permute-done.10.refs_3_ = bf16[416,128]{1,0:T(8,128)(2,1)S(1)} collective-permute-done((bf16[416,128]{1,0:T(8,128)(2,1)S(1)}, bf16[416,128]{1,0:T(8,128)(2,1)S(1)}, u32[]{:S(2)}, u32[]{:S(2)}) %collective-permute-start.10) | collective-permute-done | bytes 106528 | tf_op jit(solution)/shard_map/ppermute | solution.py:273
  80.1 1.5 %collect.3 = bf16[32,8,1536]{2,1,0:T(8,128)(2,1)} custom-call(s32[1]{0:T(128)} %bitcast.me_ref, f32[256,1536]{1,0:T(8,128)S(1)} %get-tuple-element.59.mem_ref, f32[256,1536]{1,0:T(8,128)S(1)} %get-tuple-element.60.lse_ref, bf16[416,128]{1,0:T(8,128)(2,1)S(1)} %collective-permute-done.7.refs_0_, ...), custom_call_target="tpu_custom_call", output_to_operand_aliasing={{}: (7, {})} | custom-call | tf_op jit(solution)/shard_map/collect/pallas_call | solution.py:254
  (3 shorter events, 0.1 us)
Async XLA Ops:
  1.6 34.3 %collective-permute-start.3 = (bf16[1152,128]{1,0:T(8,128)(2,1)S(1)}, bf16[1152,128]{1,0:T(8,128)(2,1)S(1)}, u32[]{:S(2)}, u32[]{:S(2)}) collective-permute-start(bf16[1152,128]{1,0:T(8,128)(2,1)S(1)} %get-tuple-element.53), channel_id=1, source_target_pairs={{0,16},{4,20},{8,24},{12,28},{16,0},{20,4},{24,8},{28,12},{1,17},{... | collective-permute-start | bytes 884744 | tf_op jit(solution)/shard_map/ppermute | solution.py:273
  4.0 38.3 %collective-permute-start.4 = (bf16[1152,128]{1,0:T(8,128)(2,1)S(1)}, bf16[1152,128]{1,0:T(8,128)(2,1)S(1)}, u32[]{:S(2)}, u32[]{:S(2)}) collective-permute-start(bf16[1152,128]{1,0:T(8,128)(2,1)S(1)} %get-tuple-element.54), channel_id=1, source_target_pairs={{0,20},{4,16},{8,28},{12,24},{16,4},{20,0},{24,12},{28,8},{1,21},{... | collective-permute-start | bytes 884744 | tf_op jit(solution)/shard_map/ppermute | solution.py:273
  4.9 43.7 %collective-permute-start.5 = (bf16[1152,128]{1,0:T(8,128)(2,1)S(1)}, bf16[1152,128]{1,0:T(8,128)(2,1)S(1)}, u32[]{:S(2)}, u32[]{:S(2)}) collective-permute-start(bf16[1152,128]{1,0:T(8,128)(2,1)S(1)} %get-tuple-element.55), channel_id=1, source_target_pairs={{0,24},{4,28},{8,16},{12,20},{16,8},{20,12},{24,0},{28,4},{1,25},{... | collective-permute-start | bytes 884744 | tf_op jit(solution)/shard_map/ppermute | solution.py:273
  6.2 36.5 %copy-start = (f32[12]{0:T(128)S(1)}, f32[12]{0:T(128)}, u32[]{:S(2)}) copy-start(f32[12]{0:T(128)} %bias_ref.1) | copy-start | bytes 148
  6.2 48.7 %collective-permute-start.6 = (bf16[1152,128]{1,0:T(8,128)(2,1)S(1)}, bf16[1152,128]{1,0:T(8,128)(2,1)S(1)}, u32[]{:S(2)}, u32[]{:S(2)}) collective-permute-start(bf16[1152,128]{1,0:T(8,128)(2,1)S(1)} %get-tuple-element.56), channel_id=1, source_target_pairs={{0,28},{4,24},{8,20},{12,16},{16,12},{20,8},{24,4},{28,0},{1,29},{... | collective-permute-start | bytes 884744 | tf_op jit(solution)/shard_map/ppermute | solution.py:273
  8.1 46.7 %collective-permute-start = (bf16[1152,128]{1,0:T(8,128)(2,1)S(1)}, bf16[1152,128]{1,0:T(8,128)(2,1)S(1)}, u32[]{:S(2)}, u32[]{:S(2)}) collective-permute-start(bf16[1152,128]{1,0:T(8,128)(2,1)S(1)} %get-tuple-element.50), channel_id=1, source_target_pairs={{0,4},{4,0},{8,12},{12,8},{16,20},{20,16},{24,28},{28,24},{1,5},{5... | collective-permute-start | bytes 884744 | tf_op jit(solution)/shard_map/ppermute | solution.py:273
  35.9 19.0 %collective-permute-start.1 = (bf16[1152,128]{1,0:T(8,128)(2,1)S(1)}, bf16[1152,128]{1,0:T(8,128)(2,1)S(1)}, u32[]{:S(2)}, u32[]{:S(2)}) collective-permute-start(bf16[1152,128]{1,0:T(8,128)(2,1)S(1)} %get-tuple-element.51), channel_id=1, source_target_pairs={{0,8},{4,12},{8,0},{12,4},{16,24},{20,28},{24,16},{28,20},{1,9},{5... | collective-permute-start | bytes 884744 | tf_op jit(solution)/shard_map/ppermute | solution.py:273
  42.2 12.6 %collective-permute-start.2 = (bf16[1152,128]{1,0:T(8,128)(2,1)S(1)}, bf16[1152,128]{1,0:T(8,128)(2,1)S(1)}, u32[]{:S(2)}, u32[]{:S(2)}) collective-permute-start(bf16[1152,128]{1,0:T(8,128)(2,1)S(1)} %get-tuple-element.52), channel_id=1, source_target_pairs={{0,12},{4,8},{8,4},{12,0},{16,28},{20,24},{24,20},{28,16},{1,13},{... | collective-permute-start | bytes 884744 | tf_op jit(solution)/shard_map/ppermute | solution.py:273
  56.8 5.5 %collective-permute-start.11 = (bf16[416,128]{1,0:T(8,128)(2,1)S(1)}, bf16[416,128]{1,0:T(8,128)(2,1)S(1)}, u32[]{:S(2)}, u32[]{:S(2)}) collective-permute-start(bf16[416,128]{1,0:T(8,128)(2,1)S(1)} %get-tuple-element.86), channel_id=1, source_target_pairs={{0,4},{4,0},{8,12},{12,8},{16,20},{20,16},{24,28},{28,24},{1,5},{5... | collective-permute-start | bytes 319496 | tf_op jit(solution)/shard_map/ppermute | solution.py:273
  57.3 6.2 %collective-permute-start.12 = (bf16[416,128]{1,0:T(8,128)(2,1)S(1)}, bf16[416,128]{1,0:T(8,128)(2,1)S(1)}, u32[]{:S(2)}, u32[]{:S(2)}) collective-permute-start(bf16[416,128]{1,0:T(8,128)(2,1)S(1)} %get-tuple-element.87), channel_id=1, source_target_pairs={{0,8},{4,12},{8,0},{12,4},{16,24},{20,28},{24,16},{28,20},{1,9},{5... | collective-permute-start | bytes 319496 | tf_op jit(solution)/shard_map/ppermute | solution.py:273
  58.2 11.7 %collective-permute-start.7 = (bf16[416,128]{1,0:T(8,128)(2,1)S(1)}, bf16[416,128]{1,0:T(8,128)(2,1)S(1)}, u32[]{:S(2)}, u32[]{:S(2)}) collective-permute-start(bf16[416,128]{1,0:T(8,128)(2,1)S(1)} %get-tuple-element.73), channel_id=1, source_target_pairs={{0,16},{4,20},{8,24},{12,28},{16,0},{20,4},{24,8},{28,12},{1,17},{... | collective-permute-start | bytes 319496 | tf_op jit(solution)/shard_map/ppermute | solution.py:273
  60.6 7.8 %collective-permute-start.13 = (bf16[416,128]{1,0:T(8,128)(2,1)S(1)}, bf16[416,128]{1,0:T(8,128)(2,1)S(1)}, u32[]{:S(2)}, u32[]{:S(2)}) collective-permute-start(bf16[416,128]{1,0:T(8,128)(2,1)S(1)} %get-tuple-element.88), channel_id=1, source_target_pairs={{0,12},{4,8},{8,4},{12,0},{16,28},{20,24},{24,20},{28,16},{1,13},{... | collective-permute-start | bytes 319496 | tf_op jit(solution)/shard_map/ppermute | solution.py:273
  62.3 11.5 %collective-permute-start.8 = (bf16[416,128]{1,0:T(8,128)(2,1)S(1)}, bf16[416,128]{1,0:T(8,128)(2,1)S(1)}, u32[]{:S(2)}, u32[]{:S(2)}) collective-permute-start(bf16[416,128]{1,0:T(8,128)(2,1)S(1)} %get-tuple-element.74), channel_id=1, source_target_pairs={{0,20},{4,16},{8,28},{12,24},{16,4},{20,0},{24,12},{28,8},{1,21},{... | collective-permute-start | bytes 319496 | tf_op jit(solution)/shard_map/ppermute | solution.py:273
  62.3 15.5 %collective-permute-start.9 = (bf16[416,128]{1,0:T(8,128)(2,1)S(1)}, bf16[416,128]{1,0:T(8,128)(2,1)S(1)}, u32[]{:S(2)}, u32[]{:S(2)}) collective-permute-start(bf16[416,128]{1,0:T(8,128)(2,1)S(1)} %get-tuple-element.75), channel_id=1, source_target_pairs={{0,24},{4,28},{8,16},{12,20},{16,8},{20,12},{24,0},{28,4},{1,25},{... | collective-permute-start | bytes 319496 | tf_op jit(solution)/shard_map/ppermute | solution.py:273
  63.5 16.6 %collective-permute-start.10 = (bf16[416,128]{1,0:T(8,128)(2,1)S(1)}, bf16[416,128]{1,0:T(8,128)(2,1)S(1)}, u32[]{:S(2)}, u32[]{:S(2)}) collective-permute-start(bf16[416,128]{1,0:T(8,128)(2,1)S(1)} %get-tuple-element.76), channel_id=1, source_target_pairs={{0,28},{4,24},{8,20},{12,16},{16,12},{20,8},{24,4},{28,0},{1,29},{... | collective-permute-start | bytes 319496 | tf_op jit(solution)/shard_map/ppermute | solution.py:273

commit v3 on v2

--- a/solution.py
+++ b/solution.py
@@ -35,10 +35,19 @@
         self.patches = row_dev * col_dev
         self.rows = n_row * row_dev
         self.sent_rows = 3 * self.pairs * row_dev
-        self.back_rows = (self.pairs + 1) * row_dev
+        self.folds = 2 if 2 * PARTS * self.pairs <= head_dim and row_dev % 32 == 0 else 1
+        self.tail_rows = row_dev // self.folds
+        self.back_rows = self.pairs * row_dev + self.tail_rows
 
     def lane(self, me, kg):
         return pl.multiple_of(((me // self.col_groups) ^ kg) * self.width, 128)
+
+    def partners(self, kg):
+        ks = range(kg * self.col_groups, (kg + 1) * self.col_groups)
+        return sorted(ks, reverse=kg == 0)
+
+    def at(self, k, pair):
+        return (k * self.pairs + pair) * self.row_dev
 
     def column(self, me, kl, c):
         return ((me % self.col_groups) ^ kl) * self.cols_g + c
@@ -64,10 +73,11 @@
                     .astype(jnp.float32)
                     .reshape(dims.patches, head_dim)
                 )
-                for kl in range(dims.col_groups):
+                for n, k in enumerate(dims.partners(kgs[i])):
+                    kl = k % dims.col_groups
                     for c in range(dims.cols_g):
                         at = (t * dims.pairs + j * dims.cols_g + c) * row_dev
-                        outs[i * dims.col_groups + kl][at : at + row_dev] = wide[
+                        outs[i * dims.col_groups + n][at : at + row_dev] = wide[
                             slot,
                             pl.ds(dims.column(me, kl, c), row_dev, stride=dims.col_dev),
                             :,
@@ -123,38 +133,57 @@
     )(in_hbm(keys), in_hbm(values)).astype(jnp.bfloat16)
 
 
-def recall_kernel(dims, bias_ref, q_ref, key_ref, value_ref, out_ref, lse_ref, raw, sem):
+def recall_kernel(
+    dims, me_ref, bias_ref, q_ref, key_ref, value_ref, out_ref, lse_ref, raw, wide, wide_lse, sem
+):
     load = pltpu.make_async_copy(q_ref, raw, sem)
     load.start()
     load.wait()
-    head_dim = dims.head_dim
+    me, head_dim, row_dev = me_ref[0], dims.head_dim, dims.row_dev
     scale = LOG2E / math.sqrt(head_dim)
     ones = jnp.ones((dims.n_col, head_dim), jnp.bfloat16)
-    for h in range(dims.heads):
-        lanes = slice(h * head_dim, (h + 1) * head_dim)
-        query = raw[:, :, lanes].reshape(dims.patches, head_dim)
-        value = jnp.concatenate([value_ref[:, lanes], ones], axis=1)
-        score = lax.dot_general(query, key_ref[:, lanes], NT, preferred_element_type=jnp.float32)
-        score = score * scale + bias_ref[h] * LOG2E
-        peak = jnp.max(score, axis=1, keepdims=True)
-        weight = jnp.exp2(score - peak).astype(jnp.bfloat16)
-        mixed = jnp.dot(weight, value, preferred_element_type=jnp.float32)
-        total = mixed[:, head_dim:]
-        out_ref[:, lanes] = mixed[:, :head_dim] / total
-        lse_ref[:, lanes] = peak + jnp.log2(total)
-
-
-def recall(dims, bias, queries, key, value):
-    out = jax.ShapeDtypeStruct((dims.patches, queries.shape[-1]), jnp.float32)
+    slot = 0
+    for kg in range(dims.head_groups):
+        lane = dims.lane(me, kg)
+        for j in range(dims.heads_g):
+            at = pl.ds(pl.multiple_of(lane + j * head_dim, 128), head_dim)
+            query = raw[:, :, at].reshape(dims.patches, head_dim)
+            key, value = key_ref[:, at], jnp.concatenate([value_ref[:, at], ones], axis=1)
+            bias = bias_ref[((me // dims.col_groups) ^ kg) * dims.heads_g + j] * LOG2E
+            score = lax.dot_general(query, key, NT, preferred_element_type=jnp.float32)
+            score = score * scale + bias
+            peak = jnp.max(score, axis=1, keepdims=True)
+            weight = jnp.exp2(score - peak).astype(jnp.bfloat16)
+            mixed = jnp.dot(weight, value, preferred_element_type=jnp.float32)
+            total = mixed[:, head_dim:]
+            wide[slot] = mixed[:, :head_dim] / total
+            wide_lse[slot] = peak + jnp.log2(total)
+            for kl in range(dims.col_groups):
+                for c in range(dims.cols_g):
+                    to = dims.at(kg * dims.col_groups + kl, j * dims.cols_g + c)
+                    patch = pl.ds(dims.column(me, kl, c), row_dev, stride=dims.col_dev)
+                    out_ref[to : to + row_dev] = wide[slot, patch, :]
+                    lse_ref[to : to + row_dev] = wide_lse[slot, patch, :]
+            slot = (slot + 1) % wide.shape[0]
+
+
+def recall(dims, me, bias, queries, key, value):
+    out = jax.ShapeDtypeStruct((dims.heads * dims.patches, dims.head_dim), jnp.float32)
+    wide = pltpu.VMEM((4, dims.patches, dims.head_dim), jnp.float32)
     return pl.pallas_call(
         functools.partial(recall_kernel, dims),
         out_shape=[out] * 2,
-        in_specs=[SMEM, HBM] + [VMEM] * 2,
+        in_specs=[SMEM] * 2 + [HBM] + [VMEM] * 2,
         out_specs=[VMEM] * 2,
-        scratch_shapes=[pltpu.VMEM(queries.shape, jnp.bfloat16), pltpu.SemaphoreType.DMA],
+        scratch_shapes=[
+            pltpu.VMEM(queries.shape, jnp.bfloat16),
+            wide,
+            wide,
+            pltpu.SemaphoreType.DMA,
+        ],
         compiler_params=PARAMS,
         name="recall",
-    )(bias, in_hbm(queries), key, value)
+    )(me, bias, in_hbm(queries), key, value)
 
 
 def attend_kernel(dims, ks, *refs):
@@ -164,6 +193,8 @@
     scale = LOG2E / math.sqrt(head_dim)
     ones = jnp.ones((rows, head_dim), jnp.bfloat16)
     lane = lax.broadcasted_iota(jnp.int32, (count, head_dim), 1)
+    row = lax.broadcasted_iota(jnp.int32, (count, head_dim), 0) % row_dev
+    lane = lane - row // dims.tail_rows * (head_dim // dims.folds)
     tail = jnp.zeros((count, head_dim), jnp.float32)
 
     def gather(t, pair, sources):
@@ -187,9 +218,12 @@
             rest = rest - term
         for i in range(len(ks)):
             outs[i][pair * row_dev : (pair + 1) * row_dev] = out[i * row_dev : (i + 1) * row_dev]
-    tail = tail.astype(jnp.bfloat16)
     for i in range(len(ks)):
-        outs[i][dims.pairs * row_dev :] = tail[i * row_dev : (i + 1) * row_dev]
+        folded = jnp.zeros((dims.tail_rows, head_dim), jnp.float32)
+        for fold in range(dims.folds):
+            at = i * row_dev + fold * dims.tail_rows
+            folded = folded + tail[at : at + dims.tail_rows]
+        outs[i][dims.pairs * row_dev :] = folded.astype(jnp.bfloat16)
 
 
 def attend(dims, ks, blocks):
@@ -206,44 +240,45 @@
 
 def collect_kernel(dims, kgs, me_ref, mem_ref, lse_ref, *refs):
     blocks = refs[: len(kgs) * dims.col_groups]
-    out, wide, wide_lse, done, sems = refs[-5:]
+    out, wide, done, sems = refs[-4:]
     me, head_dim, row_dev = me_ref[0], dims.head_dim, dims.row_dev
-    row = lax.broadcasted_iota(jnp.int32, (head_dim, dims.pairs * head_dim), 0)
-    col = lax.broadcasted_iota(jnp.int32, (head_dim, dims.pairs * head_dim), 1)
-    pick = jnp.where(row // PARTS == col // head_dim, 1.0, 0.0).astype(jnp.bfloat16)
+    shape = (head_dim, dims.pairs * head_dim)
+    row = lax.broadcasted_iota(jnp.int32, shape, 0)
+    pair_of = lax.broadcasted_iota(jnp.int32, shape, 1) // head_dim
     stores = []
     slot = 0
     for i, kg in enumerate(kgs):
         mine = blocks[i * dims.col_groups : (i + 1) * dims.col_groups]
-        tails = [ref[dims.pairs * row_dev :] for ref in mine]
-        tails = jnp.concatenate(tails, axis=0)
-        lses = jnp.dot(tails, pick, preferred_element_type=jnp.float32)
+        tails = jnp.concatenate([ref[dims.pairs * row_dev :] for ref in mine], axis=0)
+        lses = []
+        for fold in range(dims.folds):
+            first = fold * (head_dim // dims.folds)
+            pick = ((row >= first) & ((row - first) // PARTS == pair_of)).astype(jnp.bfloat16)
+            lses.append(jnp.dot(tails, pick, preferred_element_type=jnp.float32))
         lane = dims.lane(me, kg)
         for j in range(dims.heads_g):
-            for kl, ref in enumerate(mine):
+            for n, ref in enumerate(mine):
+                kl = dims.partners(kg)[n] % dims.col_groups
                 for c in range(dims.cols_g):
                     pair = j * dims.cols_g + c
+                    lanes = slice(pair * head_dim, (pair + 1) * head_dim)
+                    rows = slice(n * dims.tail_rows, (n + 1) * dims.tail_rows)
+                    lse = jnp.concatenate([part[rows, lanes] for part in lses], axis=0)
+                    at = dims.at(kg * dims.col_groups + kl, pair)
+                    mem = mem_ref[at : at + row_dev]
+                    share = 1.0 / (1.0 + jnp.exp2(lse_ref[at : at + row_dev] - lse))
+                    col = ref[pair * row_dev : (pair + 1) * row_dev].astype(jnp.float32)
                     to = pl.ds(dims.column(me, kl, c), row_dev, stride=dims.col_dev)
-                    wide[slot, to, :] = ref[pair * row_dev : (pair + 1) * row_dev].astype(
-                        jnp.float32
-                    )
-                    wide_lse[slot, to, :] = lses[
-                        kl * row_dev : (kl + 1) * row_dev, pair * head_dim : (pair + 1) * head_dim
-                    ]
+                    wide[slot, to, :] = mem + share * (col - mem)
+            done[i, j] = (
+                wide[slot].astype(jnp.bfloat16).reshape(row_dev, dims.col_dev, head_dim)
+            )
             at = pl.ds(pl.multiple_of(lane + j * head_dim, 128), head_dim)
-            mem = mem_ref[:, at]
-            share = 1.0 / (1.0 + jnp.exp2(lse_ref[:, at] - wide_lse[slot]))
-            value = mem + share * (wide[slot] - mem)
-            done[i, :, :, j * head_dim : (j + 1) * head_dim] = value.astype(jnp.bfloat16).reshape(
-                row_dev, dims.col_dev, head_dim
+            stores.append(
+                pltpu.make_async_copy(done.at[i, j], out.at[:, :, at], sems.at[i, j])
             )
+            stores[-1].start()
             slot = (slot + 1) % wide.shape[0]
-        stores.append(
-            pltpu.make_async_copy(
-                done.at[i], out.at[:, :, pl.ds(lane, dims.width)], sems.at[i]
-            )
-        )
-        stores[-1].start()
     for store in stores:
         store.wait()
 
@@ -258,9 +293,8 @@
         out_specs=HBM,
         scratch_shapes=[
             pltpu.VMEM((4, dims.patches, dims.head_dim), jnp.float32),
-            pltpu.VMEM((4, dims.patches, dims.head_dim), jnp.float32),
-            pltpu.VMEM((len(kgs),) + shape[:2] + (dims.width,), jnp.bfloat16),
-            pltpu.SemaphoreType.DMA((len(kgs),)),
+            pltpu.VMEM((len(kgs), dims.heads_g) + shape[:2] + (dims.head_dim,), jnp.bfloat16),
+            pltpu.SemaphoreType.DMA((len(kgs), dims.heads_g)),
         ],
         input_output_aliases={} if out is None else {len(operands) - 1: 0},
         compiler_params=PARAMS,
@@ -282,26 +316,30 @@
     dims = Dims(n_row, n_col, heads, model_width // heads, row_dev, col_dev)
     me = lax.axis_index("row").astype(jnp.int32).reshape(1)
     args = (queries, keys, values)
-    near_kgs, far_kgs = range(dims.head_groups // 2), range(dims.head_groups // 2, dims.head_groups)
-    near = range(n_row // 2)
-    far = range(n_row // 2, n_row)
-
-    sent_far = list(spread(dims, far_kgs, me, args))
-    me, sent_far[0] = lax.optimization_barrier((me, sent_far[0]))
-    got_far = exchange(dims, far, sent_far)
-    got_near = exchange(dims, near, spread(dims, near_kgs, me, args))
+    order = (*range(1, dims.head_groups), 0)
+    flat = [k for kg in order for k in dims.partners(kg)]
+    lead = dims.head_groups // 2
+    waves = [kgs for kgs in ((lead,), tuple(kg for kg in order if kg != lead)) if kgs]
+
+    got, token = {}, me
+    for kgs in waves:
+        ks = [k for kg in kgs for k in dims.partners(kg)]
+        sent = list(spread(dims, kgs, token, args))
+        got.update(zip(ks, exchange(dims, ks, sent)))
+        token, _ = lax.optimization_barrier((me, sent[0]))
 
     pooled = pool(dims, keys, values)
     band = lax.all_gather(pooled[None], "col", axis=0, tiled=True)
-    mem, lse = recall(dims, memory_bias, queries, band[:, 0], band[:, 1])
-
-    blocks, mem, lse = lax.optimization_barrier((got_near + got_far, mem, lse))
-    back_far = attend(dims, far, blocks)
-    blocks, back_far = lax.optimization_barrier((blocks, back_far))
-    home_far = exchange(dims, far, back_far)
-    home_near = exchange(dims, near, attend(dims, near, blocks))
-    out = collect(dims, near_kgs, me, mem, lse, home_near)
-    return collect(dims, far_kgs, me, mem, lse, home_far, out)
+    mem, lse = recall(dims, me, memory_bias, queries, band[:, 0], band[:, 1])
+
+    got, mem, lse = lax.optimization_barrier(([got[k] for k in flat], mem, lse))
+    home = {}
+    for kgs in waves:
+        ks = [k for kg in kgs for k in dims.partners(kg)]
+        back = attend(dims, ks, [got[flat.index(k)] for k in range(n_row)])
+        got, back = lax.optimization_barrier((got, list(back)))
+        home.update(zip(ks, exchange(dims, ks, back)))
+    return collect(dims, order, me, mem, lse, [home[k] for k in flat])
 
 
 def solution(mesh):

time: 81.8 us -> 79.4 us (0.971)
  the two profiles are of different devices: /device:TPU:11 before, /device:TPU:0 now
where the time goes in v3:
time: 79.4 us; the launch traced here: 79 us
  starting transfers between devices  32.9 us (41%)
  waiting for transfers between devices  25 us (31%)
  Pallas kernels  12.9 us (16%)
  blocking collectives  8.17 us (10%)
    ppermute x14, starting transfers between devices, exchange(): lax.ppermute(block, 'row', [(i, i ^ k) for i in range(dims.n_row)])  32.9 us
    ppermute x14, waiting for transfers between devices, exchange(): lax.ppermute(block, 'row', [(i, i ^ k) for i in range(dims.n_row)])  25 us
    all_gather x1, blocking collectives, per_device(): band = lax.all_gather(pooled[None], 'col', axis=0, tiled=True)  8.17 us
    pallas_call x1, Pallas kernels, recall(): pl.pallas_call(functools.partial(recall_kernel, dims), out_shape=[out] *...  4.09 us
    pallas_call x2, Pallas kernels, spread(): pl.pallas_call(functools.partial(spread_kernel, dims, kgs), out_shape=[bl...  3.16 us
    pallas_call x2, Pallas kernels, attend(): pl.pallas_call(functools.partial(attend_kernel, dims, ks), out_shape=[blo...  2.22 us
    pallas_call x1, Pallas kernels, collect(): pl.pallas_call(functools.partial(collect_kernel, dims, kgs), out_shape=ja...  1.88 us
  transfers between devices with their start and end apart: 14, of which 8 were waited for; matrix products, arithmetic and copies ran while one was open for 0% of the time, Pallas kernels for 11%

profile of v3, /device:TPU:0, one launch (start us, length us, event | category | flops | bytes accessed | tf_op | source)
XLA Modules:
  0.0 79.0 jit_solution(14404053158354986292)
XLA Ops:
  0.0 1.2 %spread.2 = (bf16[1152,128]{1,0:T(8,128)(2,1)S(1)}, bf16[1152,128]{1,0:T(8,128)(2,1)S(1)}) custom-call(s32[1]{0:T(128)} %bitcast.me_ref, bf16[32,8,1536]{2,1,0:T(8,128)(2,1)} %q_ref.1, bf16[32,8,1536]{2,1,0:T(8,128)(2,1)} %k_ref.1, bf16[32,8,1536]{2,1,0:T(8,128)(2,1)} %v_ref.1), custom_call_target="tpu_custom_call" | custom-call | tf_op jit(solution)/shard_map/spread/pallas_call | solution.py:91
  1.3 3.5 %collective-permute-start.3 = (bf16[1152,128]{1,0:T(8,128)(2,1)S(1)}, bf16[1152,128]{1,0:T(8,128)(2,1)S(1)}, u32[]{:S(2)}, u32[]{:S(2)}) collective-permute-start(bf16[1152,128]{1,0:T(8,128)(2,1)S(1)} %get-tuple-element.54), channel_id=1, source_target_pairs={{0,20},{4,16},{8,28},{12,24},{16,4},{20,0},{24,12},{28,8},{1,21},{... | collective-permute-start | bytes 884744 | tf_op jit(solution)/shard_map/ppermute | solution.py:307
  4.8 0.0 copy-start
  4.8 0.6 collective-permute-start.2
  5.5 1.9 %spread.3 = (bf16[1152,128]{1,0:T(8,128)(2,1)S(1)}, bf16[1152,128]{1,0:T(8,128)(2,1)S(1)}, bf16[1152,128]{1,0:T(8,128)(2,1)S(1)}, bf16[1152,128]{1,0:T(8,128)(2,...) custom-call(s32[1]{0:T(128)} %bitcast.me_ref, bf16[32,8,1536]{2,1,0:T(8,128)(2,1)} %q_ref.1, ...), custom_call_target="tpu_custom_call" | custom-call | tf_op jit(solution)/shard_map/spread/pallas_call | solution.py:91
  7.4 1.7 %collective-permute-start = (bf16[1152,128]{1,0:T(8,128)(2,1)S(1)}, bf16[1152,128]{1,0:T(8,128)(2,1)S(1)}, u32[]{:S(2)}, u32[]{:S(2)}) collective-permute-start(bf16[1152,128]{1,0:T(8,128)(2,1)S(1)} %get-tuple-element.52), channel_id=1, source_target_pairs={{0,8},{4,12},{8,0},{12,4},{16,24},{20,28},{24,16},{28,20},{1,9},{5... | collective-permute-start | bytes 884744 | tf_op jit(solution)/shard_map/ppermute | solution.py:307
  9.0 0.0 collective-permute-start.1
  9.0 3.5 %collective-permute-start.4 = (bf16[1152,128]{1,0:T(8,128)(2,1)S(1)}, bf16[1152,128]{1,0:T(8,128)(2,1)S(1)}, u32[]{:S(2)}, u32[]{:S(2)}) collective-permute-start(bf16[1152,128]{1,0:T(8,128)(2,1)S(1)} %get-tuple-element.55), channel_id=1, source_target_pairs={{0,24},{4,28},{8,16},{12,20},{16,8},{20,12},{24,0},{28,4},{1,25},{... | collective-permute-start | bytes 884744 | tf_op jit(solution)/shard_map/ppermute | solution.py:307
  12.5 1.5 %pool.1 = f32[2,1536]{1,0:T(2,128)S(1)} custom-call(bf16[32,8,1536]{2,1,0:T(8,128)(2,1)} %k_ref.1, bf16[32,8,1536]{2,1,0:T(8,128)(2,1)} %v_ref.1), custom_call_target="tpu_custom_call" | custom-call | tf_op jit(solution)/shard_map/pool/pallas_call | solution.py:122
  14.0 8.2 %all-gather.1 = bf16[4,2,1536]{2,1,0:T(2,128)(2,1)S(1)} all-gather(bf16[1,2,1536]{2,1,0:T(2,128)(2,1)S(1)} %convert_bitcast_fusion), channel_id=2, replica_groups=mesh['row'=8,'col'=4] {'col'}, dimensions={0}, use_global_device_ids=true | all-gather | bytes 30720 | tf_op jit(solution)/shard_map/all_gather | solution.py:332
  22.3 2.0 %collective-permute-done.3.refs_5_ = bf16[1152,128]{1,0:T(8,128)(2,1)S(1)} collective-permute-done((bf16[1152,128]{1,0:T(8,128)(2,1)S(1)}, bf16[1152,128]{1,0:T(8,128)(2,1)S(1)}, u32[]{:S(2)}, u32[]{:S(2)}) %collective-permute-start.3) | collective-permute-done | bytes 294944 | tf_op jit(solution)/shard_map/ppermute | solution.py:307
  24.3 4.6 %collective-permute-start.5 = (bf16[1152,128]{1,0:T(8,128)(2,1)S(1)}, bf16[1152,128]{1,0:T(8,128)(2,1)S(1)}, u32[]{:S(2)}, u32[]{:S(2)}) collective-permute-start(bf16[1152,128]{1,0:T(8,128)(2,1)S(1)} %get-tuple-element.56), channel_id=1, source_target_pairs={{0,28},{4,24},{8,20},{12,16},{16,12},{20,8},{24,4},{28,0},{1,29},{... | collective-permute-start | bytes 884744 | tf_op jit(solution)/shard_map/ppermute | solution.py:307
  28.9 3.3 %collective-permute-done.2.refs_4_ = bf16[1152,128]{1,0:T(8,128)(2,1)S(1)} collective-permute-done((bf16[1152,128]{1,0:T(8,128)(2,1)S(1)}, bf16[1152,128]{1,0:T(8,128)(2,1)S(1)}, u32[]{:S(2)}, u32[]{:S(2)}) %collective-permute-start.2) | collective-permute-done | bytes 294944 | tf_op jit(solution)/shard_map/ppermute | solution.py:307
  32.2 0.0 collective-permute-start.6
  32.2 0.0 copy-done
  32.2 4.1 %recall.1 = (f32[3072,128]{1,0:T(8,128)S(1)}, f32[3072,128]{1,0:T(8,128)S(1)}) custom-call(s32[1]{0:T(128)} %bitcast.me_ref, f32[12]{0:T(128)S(1)} %copy-done, bf16[32,8,1536]{2,1,0:T(8,128)(2,1)} %q_ref.1, bf16[4,1536]{1,0:T(4,128)(2,1)S(1)} %get-tuple-element.98.key_ref, bf16[4,1536]{1,0:T(4,128)(2,1)S(1)} %get-tuple-element.97.value_ref), custom_call_target="tpu_custom_call" | custom-call | tf_op jit(solution)/shard_map/recall/pallas_call | solution.py:173
  36.3 0.0 collective-permute-done.refs_2_
  36.3 0.0 collective-permute-done.1.refs_3_
  36.4 3.4 %collective-permute-done.4.refs_6_ = bf16[1152,128]{1,0:T(8,128)(2,1)S(1)} collective-permute-done((bf16[1152,128]{1,0:T(8,128)(2,1)S(1)}, bf16[1152,128]{1,0:T(8,128)(2,1)S(1)}, u32[]{:S(2)}, u32[]{:S(2)}) %collective-permute-start.4) | collective-permute-done | bytes 294944 | tf_op jit(solution)/shard_map/ppermute | solution.py:307
  39.7 5.8 %collective-permute-done.5.refs_7_ = bf16[1152,128]{1,0:T(8,128)(2,1)S(1)} collective-permute-done((bf16[1152,128]{1,0:T(8,128)(2,1)S(1)}, bf16[1152,128]{1,0:T(8,128)(2,1)S(1)}, u32[]{:S(2)}, u32[]{:S(2)}) %collective-permute-start.5) | collective-permute-done | bytes 294944 | tf_op jit(solution)/shard_map/ppermute | solution.py:307
  45.5 0.0 collective-permute-done.6.refs_1_
  45.5 0.9 %attend.2 = (bf16[400,128]{1,0:T(8,128)(2,1)S(1)}, bf16[400,128]{1,0:T(8,128)(2,1)S(1)}) custom-call(bf16[1152,128]{1,0:T(8,128)(2,1)S(1)} %get-tuple-element.80.refs_0_, bf16[1152,128]{1,0:T(8,128)(2,1)S(1)} %collective-permute-done.6.refs_1_, bf16[1152,128]{1,0:T(8,128)(2,1)S(1)} %collective-permute-done.refs_2_, ...), custom_call_target="tpu_custom_call" | custom-call | tf_op jit(solution)/shard_map/attend/pallas_call | solution.py:231
  46.4 14.4 %collective-permute-start.9 = (bf16[400,128]{1,0:T(8,128)(2,1)S(1)}, bf16[400,128]{1,0:T(8,128)(2,1)S(1)}, u32[]{:S(2)}, u32[]{:S(2)}) collective-permute-start(bf16[400,128]{1,0:T(8,128)(2,1)S(1)} %get-tuple-element.89), channel_id=1, source_target_pairs={{0,16},{4,20},{8,24},{12,28},{16,0},{20,4},{24,8},{28,12},{1,17},{... | collective-permute-start | bytes 307208 | tf_op jit(solution)/shard_map/ppermute | solution.py:307
  60.8 0.0 collective-permute-start.10
  60.8 1.3 %attend.3 = (bf16[400,128]{1,0:T(8,128)(2,1)S(1)}, bf16[400,128]{1,0:T(8,128)(2,1)S(1)}, bf16[400,128]{1,0:T(8,128)(2,1)S(1)}, bf16[400,128]{1,0:T(8,128)(2,1)S(...) custom-call(bf16[1152,128]{1,0:T(8,128)(2,1)S(1)} %get-tuple-element.80.refs_0_, ...), custom_call_target="tpu_custom_call" | custom-call | tf_op jit(solution)/shard_map/attend/pallas_call | solution.py:231
  62.2 0.5 collective-permute-start.7
  62.7 1.1 %collective-permute-start.8 = (bf16[400,128]{1,0:T(8,128)(2,1)S(1)}, bf16[400,128]{1,0:T(8,128)(2,1)S(1)}, u32[]{:S(2)}, u32[]{:S(2)}) collective-permute-start(bf16[400,128]{1,0:T(8,128)(2,1)S(1)} %get-tuple-element.88), channel_id=1, source_target_pairs={{0,12},{4,8},{8,4},{12,0},{16,28},{20,24},{24,20},{28,16},{1,13},{... | collective-permute-start | bytes 307208 | tf_op jit(solution)/shard_map/ppermute | solution.py:307
  63.8 2.6 %collective-permute-start.11 = (bf16[400,128]{1,0:T(8,128)(2,1)S(1)}, bf16[400,128]{1,0:T(8,128)(2,1)S(1)}, u32[]{:S(2)}, u32[]{:S(2)}) collective-permute-start(bf16[400,128]{1,0:T(8,128)(2,1)S(1)} %get-tuple-element.91), channel_id=1, source_target_pairs={{0,24},{4,28},{8,16},{12,20},{16,8},{20,12},{24,0},{28,4},{1,25},{... | collective-permute-start | bytes 307208 | tf_op jit(solution)/shard_map/ppermute | solution.py:307
  66.4 2.3 %collective-permute-done.9.refs_2_ = bf16[400,128]{1,0:T(8,128)(2,1)S(1)} collective-permute-done((bf16[400,128]{1,0:T(8,128)(2,1)S(1)}, bf16[400,128]{1,0:T(8,128)(2,1)S(1)}, u32[]{:S(2)}, u32[]{:S(2)}) %collective-permute-start.9) | collective-permute-done | bytes 102432 | tf_op jit(solution)/shard_map/ppermute | solution.py:307
  68.7 0.0 collective-permute-start.12
  68.7 1.7 %collective-permute-done.10.refs_3_ = bf16[400,128]{1,0:T(8,128)(2,1)S(1)} collective-permute-done((bf16[400,128]{1,0:T(8,128)(2,1)S(1)}, bf16[400,128]{1,0:T(8,128)(2,1)S(1)}, u32[]{:S(2)}, u32[]{:S(2)}) %collective-permute-start.10) | collective-permute-done | bytes 102432 | tf_op jit(solution)/shard_map/ppermute | solution.py:307
  70.4 0.3 collective-permute-start.13
  70.7 5.8 %collective-permute-done.7.refs_0_ = bf16[400,128]{1,0:T(8,128)(2,1)S(1)} collective-permute-done((bf16[400,128]{1,0:T(8,128)(2,1)S(1)}, bf16[400,128]{1,0:T(8,128)(2,1)S(1)}, u32[]{:S(2)}, u32[]{:S(2)}) %collective-permute-start.7) | collective-permute-done | bytes 102432 | tf_op jit(solution)/shard_map/ppermute | solution.py:307
  76.5 0.7 collective-permute-done.8.refs_1_
  77.1 0.0 collective-permute-done.11.refs_4_
  77.2 0.0 collective-permute-done.12.refs_5_
  77.2 0.0 collective-permute-done.13.refs_6_
  77.2 1.9 %collect.1 = bf16[32,8,1536]{2,1,0:T(8,128)(2,1)} custom-call(s32[1]{0:T(128)} %bitcast.me_ref, f32[3072,128]{1,0:T(8,128)S(1)} %get-tuple-element.61.mem_ref, f32[3072,128]{1,0:T(8,128)S(1)} %get-tuple-element.62.lse_ref, bf16[400,128]{1,0:T(8,128)(2,1)S(1)} %collective-permute-done.7.refs_0_, bf16[400,128]{1,0:T(8,128)(2,1)S(1)} %collective-permute-done.8.refs_1_, ...), custom_call_target="tpu_custom_call" | custom-call | tf_op jit(solution)/shard_map/collect/pallas_call | solution.py:289
  (3 shorter events, 0.1 us)
Async XLA Ops:
  1.3 23.0 %collective-permute-start.3 = (bf16[1152,128]{1,0:T(8,128)(2,1)S(1)}, bf16[1152,128]{1,0:T(8,128)(2,1)S(1)}, u32[]{:S(2)}, u32[]{:S(2)}) collective-permute-start(bf16[1152,128]{1,0:T(8,128)(2,1)S(1)} %get-tuple-element.54), channel_id=1, source_target_pairs={{0,20},{4,16},{8,28},{12,24},{16,4},{20,0},{24,12},{28,8},{1,21},{... | collective-permute-start | bytes 884744 | tf_op jit(solution)/shard_map/ppermute | solution.py:307
  4.8 27.4 %copy-start = (f32[12]{0:T(128)S(1)}, f32[12]{0:T(128)}, u32[]{:S(2)}) copy-start(f32[12]{0:T(128)} %bias_ref.1) | copy-start | bytes 148
  4.8 27.4 %collective-permute-start.2 = (bf16[1152,128]{1,0:T(8,128)(2,1)S(1)}, bf16[1152,128]{1,0:T(8,128)(2,1)S(1)}, u32[]{:S(2)}, u32[]{:S(2)}) collective-permute-start(bf16[1152,128]{1,0:T(8,128)(2,1)S(1)} %get-tuple-element.50), channel_id=1, source_target_pairs={{0,16},{4,20},{8,24},{12,28},{16,0},{20,4},{24,8},{28,12},{1,17},{... | collective-permute-start | bytes 884744 | tf_op jit(solution)/shard_map/ppermute | solution.py:307
  7.4 29.0 %collective-permute-start = (bf16[1152,128]{1,0:T(8,128)(2,1)S(1)}, bf16[1152,128]{1,0:T(8,128)(2,1)S(1)}, u32[]{:S(2)}, u32[]{:S(2)}) collective-permute-start(bf16[1152,128]{1,0:T(8,128)(2,1)S(1)} %get-tuple-element.52), channel_id=1, source_target_pairs={{0,8},{4,12},{8,0},{12,4},{16,24},{20,28},{24,16},{28,20},{1,9},{5... | collective-permute-start | bytes 884744 | tf_op jit(solution)/shard_map/ppermute | solution.py:307
  9.0 27.3 %collective-permute-start.1 = (bf16[1152,128]{1,0:T(8,128)(2,1)S(1)}, bf16[1152,128]{1,0:T(8,128)(2,1)S(1)}, u32[]{:S(2)}, u32[]{:S(2)}) collective-permute-start(bf16[1152,128]{1,0:T(8,128)(2,1)S(1)} %get-tuple-element.53), channel_id=1, source_target_pairs={{0,12},{4,8},{8,4},{12,0},{16,28},{20,24},{24,20},{28,16},{1,13},{... | collective-permute-start | bytes 884744 | tf_op jit(solution)/shard_map/ppermute | solution.py:307
  9.0 30.7 %collective-permute-start.4 = (bf16[1152,128]{1,0:T(8,128)(2,1)S(1)}, bf16[1152,128]{1,0:T(8,128)(2,1)S(1)}, u32[]{:S(2)}, u32[]{:S(2)}) collective-permute-start(bf16[1152,128]{1,0:T(8,128)(2,1)S(1)} %get-tuple-element.55), channel_id=1, source_target_pairs={{0,24},{4,28},{8,16},{12,20},{16,8},{20,12},{24,0},{28,4},{1,25},{... | collective-permute-start | bytes 884744 | tf_op jit(solution)/shard_map/ppermute | solution.py:307
  24.3 21.3 %collective-permute-start.5 = (bf16[1152,128]{1,0:T(8,128)(2,1)S(1)}, bf16[1152,128]{1,0:T(8,128)(2,1)S(1)}, u32[]{:S(2)}, u32[]{:S(2)}) collective-permute-start(bf16[1152,128]{1,0:T(8,128)(2,1)S(1)} %get-tuple-element.56), channel_id=1, source_target_pairs={{0,28},{4,24},{8,20},{12,16},{16,12},{20,8},{24,4},{28,0},{1,29},{... | collective-permute-start | bytes 884744 | tf_op jit(solution)/shard_map/ppermute | solution.py:307
  32.2 13.3 %collective-permute-start.6 = (bf16[1152,128]{1,0:T(8,128)(2,1)S(1)}, bf16[1152,128]{1,0:T(8,128)(2,1)S(1)}, u32[]{:S(2)}, u32[]{:S(2)}) collective-permute-start(bf16[1152,128]{1,0:T(8,128)(2,1)S(1)} %get-tuple-element.57), channel_id=1, source_target_pairs={{0,4},{4,0},{8,12},{12,8},{16,20},{20,16},{24,28},{28,24},{1,5},{5... | collective-permute-start | bytes 884744 | tf_op jit(solution)/shard_map/ppermute | solution.py:307
  46.4 22.3 %collective-permute-start.9 = (bf16[400,128]{1,0:T(8,128)(2,1)S(1)}, bf16[400,128]{1,0:T(8,128)(2,1)S(1)}, u32[]{:S(2)}, u32[]{:S(2)}) collective-permute-start(bf16[400,128]{1,0:T(8,128)(2,1)S(1)} %get-tuple-element.89), channel_id=1, source_target_pairs={{0,16},{4,20},{8,24},{12,28},{16,0},{20,4},{24,8},{28,12},{1,17},{... | collective-permute-start | bytes 307208 | tf_op jit(solution)/shard_map/ppermute | solution.py:307
  60.8 9.6 %collective-permute-start.10 = (bf16[400,128]{1,0:T(8,128)(2,1)S(1)}, bf16[400,128]{1,0:T(8,128)(2,1)S(1)}, u32[]{:S(2)}, u32[]{:S(2)}) collective-permute-start(bf16[400,128]{1,0:T(8,128)(2,1)S(1)} %get-tuple-element.90), channel_id=1, source_target_pairs={{0,20},{4,16},{8,28},{12,24},{16,4},{20,0},{24,12},{28,8},{1,21},{... | collective-permute-start | bytes 307208 | tf_op jit(solution)/shard_map/ppermute | solution.py:307
  62.2 14.3 %collective-permute-start.7 = (bf16[400,128]{1,0:T(8,128)(2,1)S(1)}, bf16[400,128]{1,0:T(8,128)(2,1)S(1)}, u32[]{:S(2)}, u32[]{:S(2)}) collective-permute-start(bf16[400,128]{1,0:T(8,128)(2,1)S(1)} %get-tuple-element.87), channel_id=1, source_target_pairs={{0,8},{4,12},{8,0},{12,4},{16,24},{20,28},{24,16},{28,20},{1,9},{5... | collective-permute-start | bytes 307208 | tf_op jit(solution)/shard_map/ppermute | solution.py:307
  62.7 14.5 %collective-permute-start.8 = (bf16[400,128]{1,0:T(8,128)(2,1)S(1)}, bf16[400,128]{1,0:T(8,128)(2,1)S(1)}, u32[]{:S(2)}, u32[]{:S(2)}) collective-permute-start(bf16[400,128]{1,0:T(8,128)(2,1)S(1)} %get-tuple-element.88), channel_id=1, source_target_pairs={{0,12},{4,8},{8,4},{12,0},{16,28},{20,24},{24,20},{28,16},{1,13},{... | collective-permute-start | bytes 307208 | tf_op jit(solution)/shard_map/ppermute | solution.py:307
  63.8 13.4 %collective-permute-start.11 = (bf16[400,128]{1,0:T(8,128)(2,1)S(1)}, bf16[400,128]{1,0:T(8,128)(2,1)S(1)}, u32[]{:S(2)}, u32[]{:S(2)}) collective-permute-start(bf16[400,128]{1,0:T(8,128)(2,1)S(1)} %get-tuple-element.91), channel_id=1, source_target_pairs={{0,24},{4,28},{8,16},{12,20},{16,8},{20,12},{24,0},{28,4},{1,25},{... | collective-permute-start | bytes 307208 | tf_op jit(solution)/shard_map/ppermute | solution.py:307
  68.7 8.4 %collective-permute-start.12 = (bf16[400,128]{1,0:T(8,128)(2,1)S(1)}, bf16[400,128]{1,0:T(8,128)(2,1)S(1)}, u32[]{:S(2)}, u32[]{:S(2)}) collective-permute-start(bf16[400,128]{1,0:T(8,128)(2,1)S(1)} %get-tuple-element.92), channel_id=1, source_target_pairs={{0,28},{4,24},{8,20},{12,16},{16,12},{20,8},{24,4},{28,0},{1,29},{... | collective-permute-start | bytes 307208 | tf_op jit(solution)/shard_map/ppermute | solution.py:307
  70.4 6.8 %collective-permute-start.13 = (bf16[400,128]{1,0:T(8,128)(2,1)S(1)}, bf16[400,128]{1,0:T(8,128)(2,1)S(1)}, u32[]{:S(2)}, u32[]{:S(2)}) collective-permute-start(bf16[400,128]{1,0:T(8,128)(2,1)S(1)} %get-tuple-element.93), channel_id=1, source_target_pairs={{0,4},{4,0},{8,12},{12,8},{16,20},{20,16},{24,28},{28,24},{1,5},{5... | collective-permute-start | bytes 307208 | tf_op jit(solution)/shard_map/ppermute | solution.py:307

commit v4 on v3

--- a/solution.py
+++ b/solution.py
@@ -41,6 +41,16 @@
 
     def lane(self, me, kg):
         return pl.multiple_of(((me // self.col_groups) ^ kg) * self.width, 128)
+
+    def fold_lanes(self, lane, row_dev):
+        row = lax.broadcasted_iota(jnp.int32, lane.shape, 0) % row_dev
+        return lane - row // self.tail_rows * (self.head_dim // self.folds)
+
+    def fold(self, tail):
+        parts = [
+            tail[i * self.tail_rows : (i + 1) * self.tail_rows] for i in range(self.folds)
+        ]
+        return functools.reduce(lambda a, b: a + b, parts)
 
     def partners(self, kg):
         ks = range(kg * self.col_groups, (kg + 1) * self.col_groups)
@@ -142,9 +152,11 @@
     me, head_dim, row_dev = me_ref[0], dims.head_dim, dims.row_dev
     scale = LOG2E / math.sqrt(head_dim)
     ones = jnp.ones((dims.n_col, head_dim), jnp.bfloat16)
+    column = dims.fold_lanes(lax.broadcasted_iota(jnp.int32, (row_dev, head_dim), 1), row_dev)
     slot = 0
     for kg in range(dims.head_groups):
         lane = dims.lane(me, kg)
+        tails = [jnp.zeros((row_dev, head_dim), jnp.float32)] * dims.col_groups
         for j in range(dims.heads_g):
             at = pl.ds(pl.multiple_of(lane + j * head_dim, 128), head_dim)
             query = raw[:, :, at].reshape(dims.patches, head_dim)
@@ -163,16 +175,21 @@
                     to = dims.at(kg * dims.col_groups + kl, j * dims.cols_g + c)
                     patch = pl.ds(dims.column(me, kl, c), row_dev, stride=dims.col_dev)
                     out_ref[to : to + row_dev] = wide[slot, patch, :]
-                    lse_ref[to : to + row_dev] = wide_lse[slot, patch, :]
+                    pair = j * dims.cols_g + c
+                    tails[kl] = jnp.where(column == pair, wide_lse[slot, patch, :], tails[kl])
             slot = (slot + 1) % wide.shape[0]
+        for kl, tail in enumerate(tails):
+            to = (kg * dims.col_groups + kl) * dims.tail_rows
+            lse_ref[to : to + dims.tail_rows] = dims.fold(tail)
 
 
 def recall(dims, me, bias, queries, key, value):
     out = jax.ShapeDtypeStruct((dims.heads * dims.patches, dims.head_dim), jnp.float32)
+    tails = jax.ShapeDtypeStruct((dims.n_row * dims.tail_rows, dims.head_dim), jnp.float32)
     wide = pltpu.VMEM((4, dims.patches, dims.head_dim), jnp.float32)
     return pl.pallas_call(
         functools.partial(recall_kernel, dims),
-        out_shape=[out] * 2,
+        out_shape=[out, tails],
         in_specs=[SMEM] * 2 + [HBM] + [VMEM] * 2,
         out_specs=[VMEM] * 2,
         scratch_shapes=[
@@ -192,9 +209,7 @@
     count = len(ks) * row_dev
     scale = LOG2E / math.sqrt(head_dim)
     ones = jnp.ones((rows, head_dim), jnp.bfloat16)
-    lane = lax.broadcasted_iota(jnp.int32, (count, head_dim), 1)
-    row = lax.broadcasted_iota(jnp.int32, (count, head_dim), 0) % row_dev
-    lane = lane - row // dims.tail_rows * (head_dim // dims.folds)
+    lane = dims.fold_lanes(lax.broadcasted_iota(jnp.int32, (count, head_dim), 1), row_dev)
     tail = jnp.zeros((count, head_dim), jnp.float32)
 
     def gather(t, pair, sources):
@@ -219,10 +234,7 @@
         for i in range(len(ks)):
             outs[i][pair * row_dev : (pair + 1) * row_dev] = out[i * row_dev : (i + 1) * row_dev]
     for i in range(len(ks)):
-        folded = jnp.zeros((dims.tail_rows, head_dim), jnp.float32)
-        for fold in range(dims.folds):
-            at = i * row_dev + fold * dims.tail_rows
-            folded = folded + tail[at : at + dims.tail_rows]
+        folded = dims.fold(tail[i * row_dev : (i + 1) * row_dev])
         outs[i][dims.pairs * row_dev :] = folded.astype(jnp.bfloat16)
 
 
@@ -239,37 +251,53 @@
 
 
 def collect_kernel(dims, kgs, me_ref, mem_ref, lse_ref, *refs):
-    blocks = refs[: len(kgs) * dims.col_groups]
+    ks = [k for kg in kgs for k in dims.partners(kg)]
+    blocks = dict(zip(ks, refs))
     out, wide, done, sems = refs[-4:]
-    me, head_dim, row_dev = me_ref[0], dims.head_dim, dims.row_dev
-    shape = (head_dim, dims.pairs * head_dim)
-    row = lax.broadcasted_iota(jnp.int32, shape, 0)
-    pair_of = lax.broadcasted_iota(jnp.int32, shape, 1) // head_dim
+    me, head_dim, row_dev, size = me_ref[0], dims.head_dim, dims.row_dev, dims.tail_rows
+    span = head_dim // dims.folds
+
+    def one_hot(shape, match):
+        row = lax.broadcasted_iota(jnp.int32, shape, 0) % head_dim
+        return match(row, lax.broadcasted_iota(jnp.int32, shape, 1)).astype(jnp.bfloat16)
+
+    tails = jnp.concatenate([blocks[k][dims.pairs * row_dev :] for k in ks], axis=0)
+    join = one_hot(
+        (head_dim, head_dim),
+        lambda row, col: (row // span == col // span) & (row % span // PARTS == col % span),
+    )
+    col_lse = jnp.dot(tails, join, preferred_element_type=jnp.float32)
+    mem_lse = jnp.concatenate([lse_ref[k * size : (k + 1) * size] for k in ks], axis=0)
+    share = 1.0 / (1.0 + jnp.exp2(mem_lse - col_lse))
+    high = share.astype(jnp.bfloat16)
+    low = (share - high.astype(jnp.float32)).astype(jnp.bfloat16)
+    terms = jnp.concatenate([high, low], axis=1)
+    shares = []
+    for fold in range(dims.folds):
+        pick = one_hot(
+            (2 * head_dim, dims.pairs * head_dim),
+            lambda row, col: row - fold * span == col // head_dim,
+        )
+        shares.append(jnp.dot(terms, pick, preferred_element_type=jnp.float32))
+
     stores = []
     slot = 0
     for i, kg in enumerate(kgs):
-        mine = blocks[i * dims.col_groups : (i + 1) * dims.col_groups]
-        tails = jnp.concatenate([ref[dims.pairs * row_dev :] for ref in mine], axis=0)
-        lses = []
-        for fold in range(dims.folds):
-            first = fold * (head_dim // dims.folds)
-            pick = ((row >= first) & ((row - first) // PARTS == pair_of)).astype(jnp.bfloat16)
-            lses.append(jnp.dot(tails, pick, preferred_element_type=jnp.float32))
         lane = dims.lane(me, kg)
         for j in range(dims.heads_g):
-            for n, ref in enumerate(mine):
-                kl = dims.partners(kg)[n] % dims.col_groups
+            for k in dims.partners(kg):
                 for c in range(dims.cols_g):
                     pair = j * dims.cols_g + c
                     lanes = slice(pair * head_dim, (pair + 1) * head_dim)
-                    rows = slice(n * dims.tail_rows, (n + 1) * dims.tail_rows)
-                    lse = jnp.concatenate([part[rows, lanes] for part in lses], axis=0)
-                    at = dims.at(kg * dims.col_groups + kl, pair)
+                    rows = slice(ks.index(k) * size, (ks.index(k) + 1) * size)
+                    part = jnp.concatenate([fold[rows, lanes] for fold in shares], axis=0)
+                    at = dims.at(k, pair)
                     mem = mem_ref[at : at + row_dev]
-                    share = 1.0 / (1.0 + jnp.exp2(lse_ref[at : at + row_dev] - lse))
-                    col = ref[pair * row_dev : (pair + 1) * row_dev].astype(jnp.float32)
-                    to = pl.ds(dims.column(me, kl, c), row_dev, stride=dims.col_dev)
-                    wide[slot, to, :] = mem + share * (col - mem)
+                    col = blocks[k][pair * row_dev : (pair + 1) * row_dev].astype(jnp.float32)
+                    to = pl.ds(
+                        dims.column(me, k % dims.col_groups, c), row_dev, stride=dims.col_dev
+                    )
+                    wide[slot, to, :] = mem + part * (col - mem)
             done[i, j] = (
                 wide[slot].astype(jnp.bfloat16).reshape(row_dev, dims.col_dev, head_dim)
             )
@@ -321,6 +349,8 @@
     lead = dims.head_groups // 2
     waves = [kgs for kgs in ((lead,), tuple(kg for kg in order if kg != lead)) if kgs]
 
+    back_waves = [(lead, 0), tuple(kg for kg in order if kg not in (lead, 0))] if lead else [order]
+
     got, token = {}, me
     for kgs in waves:
         ks = [k for kg in kgs for k in dims.partners(kg)]
@@ -334,12 +364,16 @@
 
     got, mem, lse = lax.optimization_barrier(([got[k] for k in flat], mem, lse))
     home = {}
-    for kgs in waves:
+    for kgs in back_waves:
         ks = [k for kg in kgs for k in dims.partners(kg)]
         back = attend(dims, ks, [got[flat.index(k)] for k in range(n_row)])
         got, back = lax.optimization_barrier((got, list(back)))
         home.update(zip(ks, exchange(dims, ks, back)))
-    return collect(dims, order, me, mem, lse, [home[k] for k in flat])
+    out = None
+    for kgs in [(0, lead), back_waves[1]] if lead else [order]:
+        ks = [k for kg in kgs for k in dims.partners(kg)]
+        out = collect(dims, kgs, me, mem, lse, [home[k] for k in ks], out)
+    return out
 
 
 def solution(mesh):

time: 79.4 us -> 78.3 us (0.986)
  waiting for transfers between devices: 25 us -> 19.3 us
  starting transfers between devices: 32.9 us -> 36.9 us
    ppermute x14, waiting for transfers between devices: 25 us -> 19.3 us  [exchange(): lax.ppermute(block, 'row', [(i, i ^ k) for i in range(dims.n_row)])]
    ppermute x14, starting transfers between devices: 32.9 us -> 36.9 us  [exchange(): lax.ppermute(block, 'row', [(i, i ^ k) for i in range(dims.n_row)])]
    pallas_call x1 -> x2, Pallas kernels: 1.88 us -> 2.62 us  [collect(): pl.pallas_call(functools.partial(collect_kernel, dims, kgs), out_shape=ja...]
  transfers between devices with their start and end apart: 14 -> 14, of which waited for: 8 -> 5; matrix products, arithmetic and copies ran while one was open for 0% -> 0% of each run, Pallas kernels for 11% -> 13%
where the time goes in v4:
time: 78.3 us; the launch traced here: 77.9 us
  starting transfers between devices  36.9 us (47%)
  waiting for transfers between devices  19.3 us (25%)
  Pallas kernels  13.3 us (17%)
  blocking collectives  8.17 us (10%)
    ppermute x14, starting transfers between devices, exchange(): lax.ppermute(block, 'row', [(i, i ^ k) for i in range(dims.n_row)])  36.9 us
    ppermute x14, waiting for transfers between devices, exchange(): lax.ppermute(block, 'row', [(i, i ^ k) for i in range(dims.n_row)])  19.3 us
    all_gather x1, blocking collectives, per_device(): band = lax.all_gather(pooled[None], 'col', axis=0, tiled=True)  8.17 us
    pallas_call x1, Pallas kernels, recall(): pl.pallas_call(functools.partial(recall_kernel, dims), out_shape=[out, ta...  4.11 us
    pallas_call x2, Pallas kernels, spread(): pl.pallas_call(functools.partial(spread_kernel, dims, kgs), out_shape=[bl...  3.16 us
    pallas_call x2, Pallas kernels, collect(): pl.pallas_call(functools.partial(collect_kernel, dims, kgs), out_shape=ja...  2.62 us
    pallas_call x2, Pallas kernels, attend(): pl.pallas_call(functools.partial(attend_kernel, dims, ks), out_shape=[blo...  1.94 us
  transfers between devices with their start and end apart: 14, of which 5 were waited for; matrix products, arithmetic and copies ran while one was open for 0% of the time, Pallas kernels for 13%

profile of v4, /device:TPU:0, one launch (start us, length us, event | category | flops | bytes accessed | tf_op | source)
XLA Modules:
  0.0 77.9 jit_solution(6755907256266173637)
XLA Ops:
  0.0 1.2 %spread.2 = (bf16[1152,128]{1,0:T(8,128)(2,1)S(1)}, bf16[1152,128]{1,0:T(8,128)(2,1)S(1)}) custom-call(s32[1]{0:T(128)} %bitcast.me_ref, bf16[32,8,1536]{2,1,0:T(8,128)(2,1)} %q_ref.1, bf16[32,8,1536]{2,1,0:T(8,128)(2,1)} %k_ref.1, bf16[32,8,1536]{2,1,0:T(8,128)(2,1)} %v_ref.1), custom_call_target="tpu_custom_call" | custom-call | tf_op jit(solution)/shard_map/spread/pallas_call | solution.py:101
  1.3 0.0 copy-start
  1.3 4.1 %collective-permute-start.2 = (bf16[1152,128]{1,0:T(8,128)(2,1)S(1)}, bf16[1152,128]{1,0:T(8,128)(2,1)S(1)}, u32[]{:S(2)}, u32[]{:S(2)}) collective-permute-start(bf16[1152,128]{1,0:T(8,128)(2,1)S(1)} %get-tuple-element.50), channel_id=1, source_target_pairs={{0,16},{4,20},{8,24},{12,28},{16,0},{20,4},{24,8},{28,12},{1,17},{... | collective-permute-start | bytes 884744 | tf_op jit(solution)/shard_map/ppermute | solution.py:335
  5.4 1.9 %spread.3 = (bf16[1152,128]{1,0:T(8,128)(2,1)S(1)}, bf16[1152,128]{1,0:T(8,128)(2,1)S(1)}, bf16[1152,128]{1,0:T(8,128)(2,1)S(1)}, bf16[1152,128]{1,0:T(8,128)(2,...) custom-call(s32[1]{0:T(128)} %bitcast.me_ref, bf16[32,8,1536]{2,1,0:T(8,128)(2,1)} %q_ref.1, ...), custom_call_target="tpu_custom_call" | custom-call | tf_op jit(solution)/shard_map/spread/pallas_call | solution.py:101
  7.3 1.6 %collective-permute-start = (bf16[1152,128]{1,0:T(8,128)(2,1)S(1)}, bf16[1152,128]{1,0:T(8,128)(2,1)S(1)}, u32[]{:S(2)}, u32[]{:S(2)}) collective-permute-start(bf16[1152,128]{1,0:T(8,128)(2,1)S(1)} %get-tuple-element.52), channel_id=1, source_target_pairs={{0,8},{4,12},{8,0},{12,4},{16,24},{20,28},{24,16},{28,20},{1,9},{5... | collective-permute-start | bytes 884744 | tf_op jit(solution)/shard_map/ppermute | solution.py:335
  8.9 0.0 collective-permute-start.1
  8.9 0.2 collective-permute-start.3
  9.1 3.9 %collective-permute-start.4 = (bf16[1152,128]{1,0:T(8,128)(2,1)S(1)}, bf16[1152,128]{1,0:T(8,128)(2,1)S(1)}, u32[]{:S(2)}, u32[]{:S(2)}) collective-permute-start(bf16[1152,128]{1,0:T(8,128)(2,1)S(1)} %get-tuple-element.55), channel_id=1, source_target_pairs={{0,24},{4,28},{8,16},{12,20},{16,8},{20,12},{24,0},{28,4},{1,25},{... | collective-permute-start | bytes 884744 | tf_op jit(solution)/shard_map/ppermute | solution.py:335
  13.0 1.5 %pool.1 = f32[2,1536]{1,0:T(2,128)S(1)} custom-call(bf16[32,8,1536]{2,1,0:T(8,128)(2,1)} %k_ref.1, bf16[32,8,1536]{2,1,0:T(8,128)(2,1)} %v_ref.1), custom_call_target="tpu_custom_call" | custom-call | tf_op jit(solution)/shard_map/pool/pallas_call | solution.py:132
  14.6 8.2 %all-gather.1 = bf16[4,2,1536]{2,1,0:T(2,128)(2,1)S(1)} all-gather(bf16[1,2,1536]{2,1,0:T(2,128)(2,1)S(1)} %convert_bitcast_fusion), channel_id=2, replica_groups=mesh['row'=8,'col'=4] {'col'}, dimensions={0}, use_global_device_ids=true | all-gather | bytes 30720 | tf_op jit(solution)/shard_map/all_gather | solution.py:362
  22.8 6.0 %collective-permute-done.refs_2_ = bf16[1152,128]{1,0:T(8,128)(2,1)S(1)} collective-permute-done((bf16[1152,128]{1,0:T(8,128)(2,1)S(1)}, bf16[1152,128]{1,0:T(8,128)(2,1)S(1)}, u32[]{:S(2)}, u32[]{:S(2)}) %collective-permute-start) | collective-permute-done | bytes 294944 | tf_op jit(solution)/shard_map/ppermute | solution.py:335
  28.8 0.0 collective-permute-start.5
  28.8 4.1 %collective-permute-done.1.refs_3_ = bf16[1152,128]{1,0:T(8,128)(2,1)S(1)} collective-permute-done((bf16[1152,128]{1,0:T(8,128)(2,1)S(1)}, bf16[1152,128]{1,0:T(8,128)(2,1)S(1)}, u32[]{:S(2)}, u32[]{:S(2)}) %collective-permute-start.1) | collective-permute-done | bytes 294944 | tf_op jit(solution)/shard_map/ppermute | solution.py:335
  32.8 13.2 %collective-permute-start.6 = (bf16[1152,128]{1,0:T(8,128)(2,1)S(1)}, bf16[1152,128]{1,0:T(8,128)(2,1)S(1)}, u32[]{:S(2)}, u32[]{:S(2)}) collective-permute-start(bf16[1152,128]{1,0:T(8,128)(2,1)S(1)} %get-tuple-element.57), channel_id=1, source_target_pairs={{0,4},{4,0},{8,12},{12,8},{16,20},{20,16},{24,28},{28,24},{1,5},{5... | collective-permute-start | bytes 884744 | tf_op jit(solution)/shard_map/ppermute | solution.py:335
  46.1 0.0 copy-done
  46.1 4.1 %recall.1 = (f32[3072,128]{1,0:T(8,128)S(1)}, f32[128,128]{1,0:T(8,128)S(1)}) custom-call(s32[1]{0:T(128)} %bitcast.me_ref, f32[12]{0:T(128)S(1)} %copy-done, bf16[32,8,1536]{2,1,0:T(8,128)(2,1)} %q_ref.1, bf16[4,1536]{1,0:T(4,128)(2,1)S(1)} %get-tuple-element.98.key_ref, bf16[4,1536]{1,0:T(4,128)(2,1)S(1)} %get-tuple-element.97.value_ref), custom_call_target="tpu_custom_call" | custom-call | tf_op jit(solution)/shard_map/recall/pallas_call | solution.py:190
  50.2 0.0 collective-permute-done.2.refs_4_
  50.2 0.0 collective-permute-done.3.refs_5_
  50.2 0.0 collective-permute-done.4.refs_6_
  50.3 0.0 collective-permute-done.5.refs_7_
  50.3 0.0 collective-permute-done.6.refs_1_
  50.3 1.0 %attend.2 = (bf16[400,128]{1,0:T(8,128)(2,1)S(1)}, bf16[400,128]{1,0:T(8,128)(2,1)S(1)}, bf16[400,128]{1,0:T(8,128)(2,1)S(1)}, bf16[400,128]{1,0:T(8,128)(2,1)S(1)}) custom-call(bf16[1152,128]{1,0:T(8,128)(2,1)S(1)} %get-tuple-element.82.refs_0_, bf16[1152,128]{1,0:T(8,128)(2,1)S(1)} %collective-permute-done.6.refs_1_, ...), custom_call_target="tpu_custom_call" | custom-call | tf_op jit(solution)/shard_map/attend/pallas_call | solution.py:243
  51.3 0.1 collective-permute-start.11
  51.3 9.1 %collective-permute-start.12 = (bf16[400,128]{1,0:T(8,128)(2,1)S(1)}, bf16[400,128]{1,0:T(8,128)(2,1)S(1)}, u32[]{:S(2)}, u32[]{:S(2)}) collective-permute-start(bf16[400,128]{1,0:T(8,128)(2,1)S(1)} %get-tuple-element.93), channel_id=1, source_target_pairs={{0,16},{4,20},{8,24},{12,28},{16,0},{20,4},{24,8},{28,12},{1,17},{... | collective-permute-start | bytes 307208 | tf_op jit(solution)/shard_map/ppermute | solution.py:335
  60.4 1.0 %attend.3 = (bf16[400,128]{1,0:T(8,128)(2,1)S(1)}, bf16[400,128]{1,0:T(8,128)(2,1)S(1)}, bf16[400,128]{1,0:T(8,128)(2,1)S(1)}, bf16[400,128]{1,0:T(8,128)(2,1)S(1)}) custom-call(bf16[1152,128]{1,0:T(8,128)(2,1)S(1)} %get-tuple-element.82.refs_0_, bf16[1152,128]{1,0:T(8,128)(2,1)S(1)} %collective-permute-done.6.refs_1_, ...), custom_call_target="tpu_custom_call" | custom-call | tf_op jit(solution)/shard_map/attend/pallas_call | solution.py:243
  61.4 0.1 collective-permute-start.7
  61.5 0.5 collective-permute-start.13
  62.0 1.2 %collective-permute-start.8 = (bf16[400,128]{1,0:T(8,128)(2,1)S(1)}, bf16[400,128]{1,0:T(8,128)(2,1)S(1)}, u32[]{:S(2)}, u32[]{:S(2)}) collective-permute-start(bf16[400,128]{1,0:T(8,128)(2,1)S(1)} %get-tuple-element.88), channel_id=1, source_target_pairs={{0,12},{4,8},{8,4},{12,0},{16,28},{20,24},{24,20},{28,16},{1,13},{... | collective-permute-start | bytes 307208 | tf_op jit(solution)/shard_map/ppermute | solution.py:335
  63.2 0.0 collective-permute-done.11.refs_0_
  63.2 2.5 %collective-permute-start.9 = (bf16[400,128]{1,0:T(8,128)(2,1)S(1)}, bf16[400,128]{1,0:T(8,128)(2,1)S(1)}, u32[]{:S(2)}, u32[]{:S(2)}) collective-permute-start(bf16[400,128]{1,0:T(8,128)(2,1)S(1)} %get-tuple-element.89), channel_id=1, source_target_pairs={{0,24},{4,28},{8,16},{12,20},{16,8},{20,12},{24,0},{28,4},{1,25},{... | collective-permute-start | bytes 307208 | tf_op jit(solution)/shard_map/ppermute | solution.py:335
  65.6 0.7 collective-permute-done.12.refs_2_
  66.4 0.4 collective-permute-start.10
  66.8 3.5 %collective-permute-done.13.refs_3_ = bf16[400,128]{1,0:T(8,128)(2,1)S(1)} collective-permute-done((bf16[400,128]{1,0:T(8,128)(2,1)S(1)}, bf16[400,128]{1,0:T(8,128)(2,1)S(1)}, u32[]{:S(2)}, u32[]{:S(2)}) %collective-permute-start.13) | collective-permute-done | bytes 102432 | tf_op jit(solution)/shard_map/ppermute | solution.py:335
  70.2 1.3 %collect.2.refs_4_ = bf16[32,8,1536]{2,1,0:T(8,128)(2,1)} custom-call(s32[1]{0:T(128)} %bitcast.me_ref, f32[3072,128]{1,0:T(8,128)S(1)} %get-tuple-element.61.mem_ref, f32[128,128]{1,0:T(8,128)S(1)} %get-tuple-element.62.lse_ref, bf16[400,128]{1,0:T(8,128)(2,1)S(1)} %collective-permute-done.11.refs_0_, bf16[400,128]{1,0:T(8,128)(2,1)S(1)} %get-tuple-element.92.refs_1_, ...), custom_call_target="tpu_custom_call" | custom-call | tf_op jit(solution)/shard_map/collect/pallas_call | solution.py:317
  71.6 0.0 collective-permute-done.7.refs_0_
  71.6 5.0 %collective-permute-done.8.refs_1_ = bf16[400,128]{1,0:T(8,128)(2,1)S(1)} collective-permute-done((bf16[400,128]{1,0:T(8,128)(2,1)S(1)}, bf16[400,128]{1,0:T(8,128)(2,1)S(1)}, u32[]{:S(2)}, u32[]{:S(2)}) %collective-permute-start.8) | collective-permute-done | bytes 102432 | tf_op jit(solution)/shard_map/ppermute | solution.py:335
  76.6 0.0 collective-permute-done.9.refs_2_
  76.6 0.0 collective-permute-done.10.refs_3_
  76.6 1.3 %collect.3 = bf16[32,8,1536]{2,1,0:T(8,128)(2,1)} custom-call(s32[1]{0:T(128)} %bitcast.me_ref, f32[3072,128]{1,0:T(8,128)S(1)} %get-tuple-element.61.mem_ref, f32[128,128]{1,0:T(8,128)S(1)} %get-tuple-element.62.lse_ref, bf16[400,128]{1,0:T(8,128)(2,1)S(1)} %collective-permute-done.7.refs_0_, ...), custom_call_target="tpu_custom_call", output_to_operand_aliasing={{}: (7, {})} | custom-call | tf_op jit(solution)/shard_map/collect/pallas_call | solution.py:317
  (3 shorter events, 0.1 us)
Async XLA Ops:
  1.3 44.8 %copy-start = (f32[12]{0:T(128)S(1)}, f32[12]{0:T(128)}, u32[]{:S(2)}) copy-start(f32[12]{0:T(128)} %bias_ref.1) | copy-start | bytes 148
  1.3 49.0 %collective-permute-start.2 = (bf16[1152,128]{1,0:T(8,128)(2,1)S(1)}, bf16[1152,128]{1,0:T(8,128)(2,1)S(1)}, u32[]{:S(2)}, u32[]{:S(2)}) collective-permute-start(bf16[1152,128]{1,0:T(8,128)(2,1)S(1)} %get-tuple-element.50), channel_id=1, source_target_pairs={{0,16},{4,20},{8,24},{12,28},{16,0},{20,4},{24,8},{28,12},{1,17},{... | collective-permute-start | bytes 884744 | tf_op jit(solution)/shard_map/ppermute | solution.py:335
  7.3 21.5 %collective-permute-start = (bf16[1152,128]{1,0:T(8,128)(2,1)S(1)}, bf16[1152,128]{1,0:T(8,128)(2,1)S(1)}, u32[]{:S(2)}, u32[]{:S(2)}) collective-permute-start(bf16[1152,128]{1,0:T(8,128)(2,1)S(1)} %get-tuple-element.52), channel_id=1, source_target_pairs={{0,8},{4,12},{8,0},{12,4},{16,24},{20,28},{24,16},{28,20},{1,9},{5... | collective-permute-start | bytes 884744 | tf_op jit(solution)/shard_map/ppermute | solution.py:335
  8.9 23.9 %collective-permute-start.1 = (bf16[1152,128]{1,0:T(8,128)(2,1)S(1)}, bf16[1152,128]{1,0:T(8,128)(2,1)S(1)}, u32[]{:S(2)}, u32[]{:S(2)}) collective-permute-start(bf16[1152,128]{1,0:T(8,128)(2,1)S(1)} %get-tuple-element.53), channel_id=1, source_target_pairs={{0,12},{4,8},{8,4},{12,0},{16,28},{20,24},{24,20},{28,16},{1,13},{... | collective-permute-start | bytes 884744 | tf_op jit(solution)/shard_map/ppermute | solution.py:335
  8.9 41.3 %collective-permute-start.3 = (bf16[1152,128]{1,0:T(8,128)(2,1)S(1)}, bf16[1152,128]{1,0:T(8,128)(2,1)S(1)}, u32[]{:S(2)}, u32[]{:S(2)}) collective-permute-start(bf16[1152,128]{1,0:T(8,128)(2,1)S(1)} %get-tuple-element.54), channel_id=1, source_target_pairs={{0,20},{4,16},{8,28},{12,24},{16,4},{20,0},{24,12},{28,8},{1,21},{... | collective-permute-start | bytes 884744 | tf_op jit(solution)/shard_map/ppermute | solution.py:335
  9.1 41.1 %collective-permute-start.4 = (bf16[1152,128]{1,0:T(8,128)(2,1)S(1)}, bf16[1152,128]{1,0:T(8,128)(2,1)S(1)}, u32[]{:S(2)}, u32[]{:S(2)}) collective-permute-start(bf16[1152,128]{1,0:T(8,128)(2,1)S(1)} %get-tuple-element.55), channel_id=1, source_target_pairs={{0,24},{4,28},{8,16},{12,20},{16,8},{20,12},{24,0},{28,4},{1,25},{... | collective-permute-start | bytes 884744 | tf_op jit(solution)/shard_map/ppermute | solution.py:335
  28.8 21.5 %collective-permute-start.5 = (bf16[1152,128]{1,0:T(8,128)(2,1)S(1)}, bf16[1152,128]{1,0:T(8,128)(2,1)S(1)}, u32[]{:S(2)}, u32[]{:S(2)}) collective-permute-start(bf16[1152,128]{1,0:T(8,128)(2,1)S(1)} %get-tuple-element.56), channel_id=1, source_target_pairs={{0,28},{4,24},{8,20},{12,16},{16,12},{20,8},{24,4},{28,0},{1,29},{... | collective-permute-start | bytes 884744 | tf_op jit(solution)/shard_map/ppermute | solution.py:335
  32.8 17.4 %collective-permute-start.6 = (bf16[1152,128]{1,0:T(8,128)(2,1)S(1)}, bf16[1152,128]{1,0:T(8,128)(2,1)S(1)}, u32[]{:S(2)}, u32[]{:S(2)}) collective-permute-start(bf16[1152,128]{1,0:T(8,128)(2,1)S(1)} %get-tuple-element.57), channel_id=1, source_target_pairs={{0,4},{4,0},{8,12},{12,8},{16,20},{20,16},{24,28},{28,24},{1,5},{5... | collective-permute-start | bytes 884744 | tf_op jit(solution)/shard_map/ppermute | solution.py:335
  51.3 11.9 %collective-permute-start.11 = (bf16[400,128]{1,0:T(8,128)(2,1)S(1)}, bf16[400,128]{1,0:T(8,128)(2,1)S(1)}, u32[]{:S(2)}, u32[]{:S(2)}) collective-permute-start(bf16[400,128]{1,0:T(8,128)(2,1)S(1)} %get-tuple-element.91), channel_id=1, source_target_pairs={{0,4},{4,0},{8,12},{12,8},{16,20},{20,16},{24,28},{28,24},{1,5},{5... | collective-permute-start | bytes 307208 | tf_op jit(solution)/shard_map/ppermute | solution.py:335
  51.3 15.0 %collective-permute-start.12 = (bf16[400,128]{1,0:T(8,128)(2,1)S(1)}, bf16[400,128]{1,0:T(8,128)(2,1)S(1)}, u32[]{:S(2)}, u32[]{:S(2)}) collective-permute-start(bf16[400,128]{1,0:T(8,128)(2,1)S(1)} %get-tuple-element.93), channel_id=1, source_target_pairs={{0,16},{4,20},{8,24},{12,28},{16,0},{20,4},{24,8},{28,12},{1,17},{... | collective-permute-start | bytes 307208 | tf_op jit(solution)/shard_map/ppermute | solution.py:335
  61.4 10.2 %collective-permute-start.7 = (bf16[400,128]{1,0:T(8,128)(2,1)S(1)}, bf16[400,128]{1,0:T(8,128)(2,1)S(1)}, u32[]{:S(2)}, u32[]{:S(2)}) collective-permute-start(bf16[400,128]{1,0:T(8,128)(2,1)S(1)} %get-tuple-element.87), channel_id=1, source_target_pairs={{0,8},{4,12},{8,0},{12,4},{16,24},{20,28},{24,16},{28,20},{1,9},{5... | collective-permute-start | bytes 307208 | tf_op jit(solution)/shard_map/ppermute | solution.py:335
  61.5 8.8 %collective-permute-start.13 = (bf16[400,128]{1,0:T(8,128)(2,1)S(1)}, bf16[400,128]{1,0:T(8,128)(2,1)S(1)}, u32[]{:S(2)}, u32[]{:S(2)}) collective-permute-start(bf16[400,128]{1,0:T(8,128)(2,1)S(1)} %get-tuple-element.94), channel_id=1, source_target_pairs={{0,20},{4,16},{8,28},{12,24},{16,4},{20,0},{24,12},{28,8},{1,21},{... | collective-permute-start | bytes 307208 | tf_op jit(solution)/shard_map/ppermute | solution.py:335
  62.0 14.7 %collective-permute-start.8 = (bf16[400,128]{1,0:T(8,128)(2,1)S(1)}, bf16[400,128]{1,0:T(8,128)(2,1)S(1)}, u32[]{:S(2)}, u32[]{:S(2)}) collective-permute-start(bf16[400,128]{1,0:T(8,128)(2,1)S(1)} %get-tuple-element.88), channel_id=1, source_target_pairs={{0,12},{4,8},{8,4},{12,0},{16,28},{20,24},{24,20},{28,16},{1,13},{... | collective-permute-start | bytes 307208 | tf_op jit(solution)/shard_map/ppermute | solution.py:335
  63.2 13.4 %collective-permute-start.9 = (bf16[400,128]{1,0:T(8,128)(2,1)S(1)}, bf16[400,128]{1,0:T(8,128)(2,1)S(1)}, u32[]{:S(2)}, u32[]{:S(2)}) collective-permute-start(bf16[400,128]{1,0:T(8,128)(2,1)S(1)} %get-tuple-element.89), channel_id=1, source_target_pairs={{0,24},{4,28},{8,16},{12,20},{16,8},{20,12},{24,0},{28,4},{1,25},{... | collective-permute-start | bytes 307208 | tf_op jit(solution)/shard_map/ppermute | solution.py:335
  66.4 10.2 %collective-permute-start.10 = (bf16[400,128]{1,0:T(8,128)(2,1)S(1)}, bf16[400,128]{1,0:T(8,128)(2,1)S(1)}, u32[]{:S(2)}, u32[]{:S(2)}) collective-permute-start(bf16[400,128]{1,0:T(8,128)(2,1)S(1)} %get-tuple-element.90), channel_id=1, source_target_pairs={{0,28},{4,24},{8,20},{12,16},{16,12},{20,8},{24,4},{28,0},{1,29},{... | collective-permute-start | bytes 307208 | tf_op jit(solution)/shard_map/ppermute | solution.py:335

commit v5 on v4

--- a/solution.py
+++ b/solution.py
@@ -34,7 +34,6 @@
         self.width = self.heads_g * head_dim
         self.patches = row_dev * col_dev
         self.rows = n_row * row_dev
-        self.sent_rows = 3 * self.pairs * row_dev
         self.folds = 2 if 2 * PARTS * self.pairs <= head_dim and row_dev % 32 == 0 else 1
         self.tail_rows = row_dev // self.folds
         self.back_rows = self.pairs * row_dev + self.tail_rows
@@ -52,6 +51,12 @@
         ]
         return functools.reduce(lambda a, b: a + b, parts)
 
+    def pieces(self, k):
+        return ((1, 2), (0,)) if k >= self.n_row - self.col_groups else ((0, 1, 2),)
+
+    def row(self, kinds, kind, pair):
+        return (kinds.index(kind) * self.pairs + pair) * self.row_dev
+
     def partners(self, kg):
         ks = range(kg * self.col_groups, (kg + 1) * self.col_groups)
         return sorted(ks, reverse=kg == 0)
@@ -63,54 +68,68 @@
         return ((me % self.col_groups) ^ kl) * self.cols_g + c
 
 
-def spread_kernel(dims, kgs, me_ref, *refs):
-    args, outs, (raw, wide, sems) = refs[:3], refs[3:-3], refs[-3:]
+def spread_kernel(dims, parts, me_ref, *refs):
+    args, outs, raws, (wide, sems) = (
+        refs[:3],
+        refs[3 : -2 - len(parts)],
+        refs[-2 - len(parts) : -2],
+        refs[-2:],
+    )
     me, head_dim, row_dev = me_ref[0], dims.head_dim, dims.row_dev
     loads = {}
-    for i, kg in enumerate(kgs):
-        for t, arg in enumerate(args):
-            loads[i, t] = pltpu.make_async_copy(
-                arg.at[:, :, pl.ds(dims.lane(me, kg), dims.width)], raw.at[i, t], sems.at[i, t]
+    for i, (kg, kinds) in enumerate(parts):
+        for n, kind in enumerate(kinds):
+            loads[i, n] = pltpu.make_async_copy(
+                args[kind].at[:, :, pl.ds(dims.lane(me, kg), dims.width)],
+                raws[i].at[n],
+                sems.at[i, n],
             )
-            loads[i, t].start()
+            loads[i, n].start()
     slot = 0
-    for i in range(len(kgs)):
-        for t in range(3):
-            loads[i, t].wait()
+    for i, (kg, kinds) in enumerate(parts):
+        ks = dims.partners(kg)
+        mine, outs = outs[: len(ks)], outs[len(ks) :]
+        for n, kind in enumerate(kinds):
+            loads[i, n].wait()
             for j in range(dims.heads_g):
                 wide[slot] = (
-                    raw[i, t, :, :, j * head_dim : (j + 1) * head_dim]
+                    raws[i][n, :, :, j * head_dim : (j + 1) * head_dim]
                     .astype(jnp.float32)
                     .reshape(dims.patches, head_dim)
                 )
-                for n, k in enumerate(dims.partners(kgs[i])):
-                    kl = k % dims.col_groups
+                for k, out in zip(ks, mine):
                     for c in range(dims.cols_g):
-                        at = (t * dims.pairs + j * dims.cols_g + c) * row_dev
-                        outs[i * dims.col_groups + n][at : at + row_dev] = wide[
-                            slot,
-                            pl.ds(dims.column(me, kl, c), row_dev, stride=dims.col_dev),
-                            :,
-                        ].astype(jnp.bfloat16)
+                        patch = pl.ds(
+                            dims.column(me, k % dims.col_groups, c), row_dev, stride=dims.col_dev
+                        )
+                        at = dims.row(kinds, kind, j * dims.cols_g + c)
+                        out[at : at + row_dev] = wide[slot, patch, :].astype(jnp.bfloat16)
                 slot = (slot + 1) % wide.shape[0]
 
 
-def spread(dims, kgs, me, args):
-    block = jax.ShapeDtypeStruct((dims.sent_rows, dims.head_dim), jnp.bfloat16)
-    count = len(kgs) * dims.col_groups
-    return pl.pallas_call(
-        functools.partial(spread_kernel, dims, kgs),
-        out_shape=[block] * count,
+def spread(dims, parts, me, args):
+    keys = [(k, kinds) for kg, kinds in parts for k in dims.partners(kg)]
+    rows = dims.pairs * dims.row_dev
+    blocks = pl.pallas_call(
+        functools.partial(spread_kernel, dims, parts),
+        out_shape=[
+            jax.ShapeDtypeStruct((len(kinds) * rows, dims.head_dim), jnp.bfloat16)
+            for _, kinds in keys
+        ],
         in_specs=[SMEM] + [HBM] * 3,
-        out_specs=[VMEM] * count,
+        out_specs=[VMEM] * len(keys),
         scratch_shapes=[
-            pltpu.VMEM((len(kgs), 3, dims.row_dev, dims.col_dev, dims.width), jnp.bfloat16),
+            pltpu.VMEM((len(kinds), dims.row_dev, dims.col_dev, dims.width), jnp.bfloat16)
+            for _, kinds in parts
+        ]
+        + [
             pltpu.VMEM((4, dims.patches, dims.head_dim), jnp.float32),
-            pltpu.SemaphoreType.DMA((len(kgs), 3)),
+            pltpu.SemaphoreType.DMA((len(parts), 3)),
         ],
         compiler_params=PARAMS,
         name="spread",
     )(me, *[in_hbm(arg) for arg in args])
+    return dict(zip(keys, blocks))
 
 
 def pool_kernel(dims, k_ref, v_ref, out_ref, raw, sems):
@@ -203,8 +222,8 @@
     )(me, bias, in_hbm(queries), key, value)
 
 
-def attend_kernel(dims, ks, *refs):
-    ins, outs = refs[: dims.n_row], refs[dims.n_row :]
+def attend_kernel(dims, ks, keys, *refs):
+    ins, outs = dict(zip(keys, refs)), refs[len(keys) :]
     row_dev, head_dim, rows = dims.row_dev, dims.head_dim, dims.rows
     count = len(ks) * row_dev
     scale = LOG2E / math.sqrt(head_dim)
@@ -212,9 +231,13 @@
     lane = dims.fold_lanes(lax.broadcasted_iota(jnp.int32, (count, head_dim), 1), row_dev)
     tail = jnp.zeros((count, head_dim), jnp.float32)
 
-    def gather(t, pair, sources):
-        at = (t * dims.pairs + pair) * row_dev
-        return jnp.concatenate([ins[k][at : at + row_dev] for k in sources], axis=0)
+    def gather(kind, pair, sources):
+        parts = []
+        for k in sources:
+            kinds = [piece for piece in dims.pieces(k) if kind in piece][0]
+            at = dims.row(kinds, kind, pair)
+            parts.append(ins[k, kinds][at : at + row_dev])
+        return jnp.concatenate(parts, axis=0)
 
     for pair in range(dims.pairs):
         query = gather(0, pair, ks)
@@ -239,15 +262,21 @@
 
 
 def attend(dims, ks, blocks):
+    keys = [key for key in blocks if key[1] != (0,) or key[0] in ks]
     block = jax.ShapeDtypeStruct((dims.back_rows, dims.head_dim), jnp.bfloat16)
     return pl.pallas_call(
-        functools.partial(attend_kernel, dims, ks),
+        functools.partial(attend_kernel, dims, ks, keys),
         out_shape=[block] * len(ks),
-        in_specs=[VMEM] * dims.n_row,
+        in_specs=[VMEM] * len(keys),
         out_specs=[VMEM] * len(ks),
         compiler_params=PARAMS,
+        cost_estimate=pl.CostEstimate(
+            flops=6 * dims.pairs * dims.rows * dims.rows * dims.head_dim,
+            transcendentals=dims.pairs * dims.rows * dims.rows,
+            bytes_accessed=6 * dims.pairs * dims.rows * dims.head_dim,
+        ),
         name="attend",
-    )(*blocks)
+    )(*[blocks[key] for key in keys])
 
 
 def collect_kernel(dims, kgs, me_ref, mem_ref, lse_ref, *refs):
@@ -337,6 +366,11 @@
     ]
 
 
+def tied(blocks, *others):
+    values, others = lax.optimization_barrier((list(blocks.values()), others))
+    return (dict(zip(blocks, values)), *others)
+
+
 def per_device(queries, keys, values, memory_bias):
     row_dev, col_dev, model_width = queries.shape
     n_row, n_col = lax.axis_size("row"), lax.axis_size("col")
@@ -344,33 +378,45 @@
     dims = Dims(n_row, n_col, heads, model_width // heads, row_dev, col_dev)
     me = lax.axis_index("row").astype(jnp.int32).reshape(1)
     args = (queries, keys, values)
+    both, asked, every = (1, 2), (0,), (0, 1, 2)
+    last = dims.head_groups - 1
     order = (*range(1, dims.head_groups), 0)
-    flat = [k for kg in order for k in dims.partners(kg)]
-    lead = dims.head_groups // 2
-    waves = [kgs for kgs in ((lead,), tuple(kg for kg in order if kg != lead)) if kgs]
-
-    back_waves = [(lead, 0), tuple(kg for kg in order if kg not in (lead, 0))] if lead else [order]
-
+
+    def split(kg):
+        return both if kg == last else every
+
+    early = [kg for kg in order if kg not in (last, 0)]
+    waves = [
+        [(kg, every) for kg in early],
+        [(last, both)] + [(0, every)] * (last > 0),
+        [(last, asked)],
+    ]
+    waves = [parts for parts in waves if parts]
+    first = (*early[-1:], *([0] if last else []), *early[:-1])
     got, token = {}, me
-    for kgs in waves:
-        ks = [k for kg in kgs for k in dims.partners(kg)]
-        sent = list(spread(dims, kgs, token, args))
-        got.update(zip(ks, exchange(dims, ks, sent)))
-        token, _ = lax.optimization_barrier((me, sent[0]))
+    for parts in waves:
+        sent = spread(dims, parts, token, args)
+        token, _ = lax.optimization_barrier((me, list(sent.values())[0]))
+        got.update(zip(sent, exchange(dims, [k for k, _ in sent], sent.values())))
 
     pooled = pool(dims, keys, values)
     band = lax.all_gather(pooled[None], "col", axis=0, tiled=True)
     mem, lse = recall(dims, me, memory_bias, queries, band[:, 0], band[:, 1])
 
-    got, mem, lse = lax.optimization_barrier(([got[k] for k in flat], mem, lse))
+    held = [(k, split(kg)) for kg in order for k in dims.partners(kg)]
+    late = [(k, asked) for k in dims.partners(last)]
+    blocks, mem, lse = tied({key: got[key] for key in held}, mem, lse)
     home = {}
-    for kgs in back_waves:
-        ks = [k for kg in kgs for k in dims.partners(kg)]
-        back = attend(dims, ks, [got[flat.index(k)] for k in range(n_row)])
-        got, back = lax.optimization_barrier((got, list(back)))
-        home.update(zip(ks, exchange(dims, ks, back)))
+    ks = [k for kg in first for k in dims.partners(kg)]
+    back = list(attend(dims, ks, blocks))
+    tie = back
+    home.update(zip(ks, exchange(dims, ks, back)))
+    late_blocks, _ = tied({key: got[key] for key in late}, tie)
+    ks = [k for kg in order if kg not in first for k in dims.partners(kg)]
+    back = list(attend(dims, ks, {**blocks, **late_blocks}))
+    home.update(zip(ks, exchange(dims, ks, back)))
     out = None
-    for kgs in [(0, lead), back_waves[1]] if lead else [order]:
+    for kgs in ((*first,), (last,)):
         ks = [k for kg in kgs for k in dims.partners(kg)]
         out = collect(dims, kgs, me, mem, lse, [home[k] for k in ks], out)
     return out

time: 78.3 us -> 77.6 us (level)
  starting transfers between devices: 36.9 us -> 26.3 us
  waiting for transfers between devices: 19.3 us -> 28.1 us
  Pallas kernels: 13.3 us -> 14.6 us
    ppermute x14 -> x16, starting transfers between devices: 36.9 us -> 26.3 us  [exchange(): lax.ppermute(block, 'row', [(i, i ^ k) for i in range(dims.n_row)])]
    ppermute x14 -> x16, waiting for transfers between devices: 19.3 us -> 28.1 us  [exchange(): lax.ppermute(block, 'row', [(i, i ^ k) for i in range(dims.n_row)])]
    pallas_call x4 -> x5, Pallas kernels: 5.09 us -> 6.34 us  [the longest x3 4.12 us: spread(): pl.pallas_call(functools.partial(spread_kernel, dims, parts), out_shape=[...]
  transfers between devices with their start and end apart: 14 -> 16, of which waited for: 5 -> 6; matrix products, arithmetic and copies ran while one was open for 0% -> 0% of each run, Pallas kernels for 13% -> 15%
where the time goes in v5:
time: 77.6 us; the launch traced here: 77.3 us
  waiting for transfers between devices  28.1 us (36%)
  starting transfers between devices  26.3 us (34%)
  Pallas kernels  14.6 us (19%)
  blocking collectives  8.17 us (11%)
    ppermute x16, waiting for transfers between devices, exchange(): lax.ppermute(block, 'row', [(i, i ^ k) for i in range(dims.n_row)])  28.1 us
    ppermute x16, starting transfers between devices, exchange(): lax.ppermute(block, 'row', [(i, i ^ k) for i in range(dims.n_row)])  26.3 us
    all_gather x1, blocking collectives, per_device(): band = lax.all_gather(pooled[None], 'col', axis=0, tiled=True)  8.17 us
    pallas_call x3, Pallas kernels, spread(): pl.pallas_call(functools.partial(spread_kernel, dims, parts), out_shape=[...  4.12 us
    pallas_call x1, Pallas kernels, recall(): pl.pallas_call(functools.partial(recall_kernel, dims), out_shape=[out, ta...  4.12 us
    pallas_call x2, Pallas kernels, collect(): pl.pallas_call(functools.partial(collect_kernel, dims, kgs), out_shape=ja...  2.67 us
    pallas_call x2, Pallas kernels, attend(): pl.pallas_call(functools.partial(attend_kernel, dims, ks, keys), out_shap...  2.22 us
  transfers between devices with their start and end apart: 16, of which 6 were waited for; matrix products, arithmetic and copies ran while one was open for 0% of the time, Pallas kernels for 15%

profile of v5, /device:TPU:0, one launch (start us, length us, event | category | flops | bytes accessed | tf_op | source)
XLA Modules:
  0.0 77.3 jit_solution(12455997011124912371)
XLA Ops:
  0.0 1.6 %spread.3 = (bf16[1152,128]{1,0:T(8,128)(2,1)S(1)}, bf16[1152,128]{1,0:T(8,128)(2,1)S(1)}, bf16[1152,128]{1,0:T(8,128)(2,1)S(1)}, bf16[1152,128]{1,0:T(8,128)(2,1)S(1)}) custom-call(s32[1]{0:T(128)} %bitcast.me_ref, bf16[32,8,1536]{2,1,0:T(8,128)(2,1)} %refs_0_.5, bf16[32,8,1536]{2,1,0:T(8,128)(2,1)} %refs_1_.5, bf16[32,8,1536]{2,1,0:T(8,128)(2,1)} %refs_2_.5), custom_call_target="tpu_custom_call" | custom-call | tf_op jit(solution)/shard_map/spread/pallas_call | solution.py:113
  1.6 2.5 %collective-permute-start.1 = (bf16[1152,128]{1,0:T(8,128)(2,1)S(1)}, bf16[1152,128]{1,0:T(8,128)(2,1)S(1)}, u32[]{:S(2)}, u32[]{:S(2)}) collective-permute-start(bf16[1152,128]{1,0:T(8,128)(2,1)S(1)} %get-tuple-element.40), channel_id=1, source_target_pairs={{0,12},{4,8},{8,4},{12,0},{16,28},{20,24},{24,20},{28,16},{1,13},{... | collective-permute-start | bytes 884744 | tf_op jit(solution)/shard_map/ppermute | solution.py:364
  4.1 2.6 %collective-permute-start.2 = (bf16[1152,128]{1,0:T(8,128)(2,1)S(1)}, bf16[1152,128]{1,0:T(8,128)(2,1)S(1)}, u32[]{:S(2)}, u32[]{:S(2)}) collective-permute-start(bf16[1152,128]{1,0:T(8,128)(2,1)S(1)} %get-tuple-element.41), channel_id=1, source_target_pairs={{0,16},{4,20},{8,24},{12,28},{16,0},{20,4},{24,8},{28,12},{1,17},{... | collective-permute-start | bytes 884744 | tf_op jit(solution)/shard_map/ppermute | solution.py:364
  6.7 0.6 collective-permute-start
  7.3 1.5 %spread.4 = (bf16[768,128]{1,0:T(8,128)(2,1)S(1)}, bf16[768,128]{1,0:T(8,128)(2,1)S(1)}, bf16[1152,128]{1,0:T(8,128)(2,1)S(1)}, bf16[1152,128]{1,0:T(8,128)(2,1)S(1)}) custom-call(s32[1]{0:T(128)} %bitcast.me_ref, bf16[32,8,1536]{2,1,0:T(8,128)(2,1)} %refs_0_.5, bf16[32,8,1536]{2,1,0:T(8,128)(2,1)} %refs_1_.5, bf16[32,8,1536]{2,1,0:T(8,128)(2,1)} %refs_2_.5), custom_call_target="tpu_custom_call" | custom-call | tf_op jit(solution)/shard_map/spread/pallas_call | solution.py:113
  8.8 1.0 %collective-permute-start.5 = (bf16[768,128]{1,0:T(8,128)(2,1)S(1)}, bf16[768,128]{1,0:T(8,128)(2,1)S(1)}, u32[]{:S(2)}, u32[]{:S(2)}) collective-permute-start(bf16[768,128]{1,0:T(8,128)(2,1)S(1)} %get-tuple-element.45), channel_id=1, source_target_pairs={{0,28},{4,24},{8,20},{12,16},{16,12},{20,8},{24,4},{28,0},{1,29},{... | collective-permute-start | bytes 589832 | tf_op jit(solution)/shard_map/ppermute | solution.py:364
  9.8 2.4 %collective-permute-start.4 = (bf16[768,128]{1,0:T(8,128)(2,1)S(1)}, bf16[768,128]{1,0:T(8,128)(2,1)S(1)}, u32[]{:S(2)}, u32[]{:S(2)}) collective-permute-start(bf16[768,128]{1,0:T(8,128)(2,1)S(1)} %get-tuple-element.44), channel_id=1, source_target_pairs={{0,24},{4,28},{8,16},{12,20},{16,8},{20,12},{24,0},{28,4},{1,25},{... | collective-permute-start | bytes 589832 | tf_op jit(solution)/shard_map/ppermute | solution.py:364
  12.3 1.5 %pool.1 = f32[2,1536]{1,0:T(2,128)S(1)} custom-call(bf16[32,8,1536]{2,1,0:T(8,128)(2,1)} %refs_1_.5, bf16[32,8,1536]{2,1,0:T(8,128)(2,1)} %refs_2_.5), custom_call_target="tpu_custom_call" | custom-call | tf_op jit(solution)/shard_map/pool/pallas_call | solution.py:151
  13.8 0.0 copy-start
  13.8 8.2 %all-gather.1 = bf16[4,2,1536]{2,1,0:T(2,128)(2,1)S(1)} all-gather(bf16[1,2,1536]{2,1,0:T(2,128)(2,1)S(1)} %convert_bitcast_fusion), channel_id=2, replica_groups=mesh['row'=8,'col'=4] {'col'}, dimensions={0}, use_global_device_ids=true | all-gather | bytes 30720 | tf_op jit(solution)/shard_map/all_gather | solution.py:403
  22.0 1.1 %spread.5 = (bf16[384,128]{1,0:T(8,128)(2,1)S(1)}, bf16[384,128]{1,0:T(8,128)(2,1)S(1)}) custom-call(s32[1]{0:T(128)} %bitcast.me_ref, bf16[32,8,1536]{2,1,0:T(8,128)(2,1)} %refs_0_.5, bf16[32,8,1536]{2,1,0:T(8,128)(2,1)} %refs_1_.5, bf16[32,8,1536]{2,1,0:T(8,128)(2,1)} %refs_2_.5), custom_call_target="tpu_custom_call" | custom-call | tf_op jit(solution)/shard_map/spread/pallas_call | solution.py:113
  23.1 8.2 %collective-permute-done.5.refs_5_ = bf16[768,128]{1,0:T(8,128)(2,1)S(1)} collective-permute-done((bf16[768,128]{1,0:T(8,128)(2,1)S(1)}, bf16[768,128]{1,0:T(8,128)(2,1)S(1)}, u32[]{:S(2)}, u32[]{:S(2)}) %collective-permute-start.5) | collective-permute-done | bytes 196640 | tf_op jit(solution)/shard_map/ppermute | solution.py:364
  31.3 0.0 collective-permute-start.3
  31.3 4.5 %collective-permute-done.4.refs_4_ = bf16[768,128]{1,0:T(8,128)(2,1)S(1)} collective-permute-done((bf16[768,128]{1,0:T(8,128)(2,1)S(1)}, bf16[768,128]{1,0:T(8,128)(2,1)S(1)}, u32[]{:S(2)}, u32[]{:S(2)}) %collective-permute-start.4) | collective-permute-done | bytes 196640 | tf_op jit(solution)/shard_map/ppermute | solution.py:364
  35.8 0.0 collective-permute-start.6
  35.8 0.0 copy-done
  35.8 4.1 %recall.1 = (f32[3072,128]{1,0:T(8,128)S(1)}, f32[128,128]{1,0:T(8,128)S(1)}) custom-call(s32[1]{0:T(128)} %bitcast.me_ref, f32[12]{0:T(128)S(1)} %copy-done, bf16[32,8,1536]{2,1,0:T(8,128)(2,1)} %refs_0_.5, bf16[4,1536]{1,0:T(4,128)(2,1)S(1)} %get-tuple-element.76.key_ref, bf16[4,1536]{1,0:T(4,128)(2,1)S(1)} %get-tuple-element.75.value_ref), custom_call_target="tpu_custom_call" | custom-call | tf_op jit(solution)/shard_map/recall/pallas_call | solution.py:209
  39.9 0.0 collective-permute-done.1.refs_1_
  39.9 1.3 %collective-permute-start.7 = (bf16[384,128]{1,0:T(8,128)(2,1)S(1)}, bf16[384,128]{1,0:T(8,128)(2,1)S(1)}, u32[]{:S(2)}, u32[]{:S(2)}) collective-permute-start(bf16[384,128]{1,0:T(8,128)(2,1)S(1)} %get-tuple-element.61), channel_id=1, source_target_pairs={{0,24},{4,28},{8,16},{12,20},{16,8},{20,12},{24,0},{28,4},{1,25},{... | collective-permute-start | bytes 294920 | tf_op jit(solution)/shard_map/ppermute | solution.py:364
  41.3 0.0 collective-permute-done.2.refs_2_
  41.3 2.4 %collective-permute-start.8 = (bf16[384,128]{1,0:T(8,128)(2,1)S(1)}, bf16[384,128]{1,0:T(8,128)(2,1)S(1)}, u32[]{:S(2)}, u32[]{:S(2)}) collective-permute-start(bf16[384,128]{1,0:T(8,128)(2,1)S(1)} %get-tuple-element.62), channel_id=1, source_target_pairs={{0,28},{4,24},{8,20},{12,16},{16,12},{20,8},{24,4},{28,0},{1,29},{... | collective-permute-start | bytes 294920 | tf_op jit(solution)/shard_map/ppermute | solution.py:364
  43.7 10.7 %collective-permute-done.3.refs_3_ = bf16[1152,128]{1,0:T(8,128)(2,1)S(1)} collective-permute-done((bf16[1152,128]{1,0:T(8,128)(2,1)S(1)}, bf16[1152,128]{1,0:T(8,128)(2,1)S(1)}, u32[]{:S(2)}, u32[]{:S(2)}) %collective-permute-start.3) | collective-permute-done | bytes 294944 | tf_op jit(solution)/shard_map/ppermute | solution.py:364
  54.4 0.0 collective-permute-done.refs_0_
  54.4 0.0 collective-permute-done.6.refs_6_
  54.4 1.3 %attend.2 = (bf16[400,128]{1,0:T(8,128)(2,1)S(1)}, bf16[400,128]{1,0:T(8,128)(2,1)S(1)}, bf16[400,128]{1,0:T(8,128)(2,1)S(1)}, bf16[400,128]{1,0:T(8,128)(2,1)S(...) custom-call(bf16[1152,128]{1,0:T(8,128)(2,1)S(1)} %collective-permute-done.refs_0_, ...), custom_call_target="tpu_custom_call" | custom-call | flops 603979776 | bytes 2359296 | tf_op jit(solution)/shard_map/attend/pallas_call | solution.py:267
  55.7 2.1 %collective-permute-start.11 = (bf16[400,128]{1,0:T(8,128)(2,1)S(1)}, bf16[400,128]{1,0:T(8,128)(2,1)S(1)}, u32[]{:S(2)}, u32[]{:S(2)}) collective-permute-start(bf16[400,128]{1,0:T(8,128)(2,1)S(1)} %get-tuple-element.63), channel_id=1, source_target_pairs={{0,16},{4,20},{8,24},{12,28},{16,0},{20,4},{24,8},{28,12},{1,17},{... | collective-permute-start | bytes 307208 | tf_op jit(solution)/shard_map/ppermute | solution.py:364
  57.9 0.3 collective-permute-start.12
  58.2 0.7 collective-permute-start.13
  58.8 0.0 collective-permute-done.7.refs_8_
  58.8 1.0 %collective-permute-start.14 = (bf16[400,128]{1,0:T(8,128)(2,1)S(1)}, bf16[400,128]{1,0:T(8,128)(2,1)S(1)}, u32[]{:S(2)}, u32[]{:S(2)}) collective-permute-start(bf16[400,128]{1,0:T(8,128)(2,1)S(1)} %get-tuple-element.67), channel_id=1, source_target_pairs={{0,8},{4,12},{8,0},{12,4},{16,24},{20,28},{24,16},{28,20},{1,9},{5... | collective-permute-start | bytes 307208 | tf_op jit(solution)/shard_map/ppermute | solution.py:364
  59.8 0.0 collective-permute-done.8.refs_9_
  59.8 4.9 %collective-permute-start.15 = (bf16[400,128]{1,0:T(8,128)(2,1)S(1)}, bf16[400,128]{1,0:T(8,128)(2,1)S(1)}, u32[]{:S(2)}, u32[]{:S(2)}) collective-permute-start(bf16[400,128]{1,0:T(8,128)(2,1)S(1)} %get-tuple-element.68), channel_id=1, source_target_pairs={{0,12},{4,8},{8,4},{12,0},{16,28},{20,24},{24,20},{28,16},{1,13},{... | collective-permute-start | bytes 307208 | tf_op jit(solution)/shard_map/ppermute | solution.py:364
  64.7 0.9 %attend.3 = (bf16[400,128]{1,0:T(8,128)(2,1)S(1)}, bf16[400,128]{1,0:T(8,128)(2,1)S(1)}) custom-call(bf16[1152,128]{1,0:T(8,128)(2,1)S(1)} %collective-permute-done.refs_0_, bf16[1152,128]{1,0:T(8,128)(2,1)S(1)} %collective-permute-done.1.refs_1_, bf16[1152,128]{1,0:T(8,128)(2,1)S(1)} %collective-permute-done.2.refs_2_, ...), custom_call_target="tpu_custom_call" | custom-call | flops 603979776 | bytes 2359296 | tf_op jit(solution)/shard_map/attend/pallas_call | solution.py:267
  65.6 1.4 %collective-permute-done.11.refs_0_ = bf16[400,128]{1,0:T(8,128)(2,1)S(1)} collective-permute-done((bf16[400,128]{1,0:T(8,128)(2,1)S(1)}, bf16[400,128]{1,0:T(8,128)(2,1)S(1)}, u32[]{:S(2)}, u32[]{:S(2)}) %collective-permute-start.11) | collective-permute-done | bytes 102432 | tf_op jit(solution)/shard_map/ppermute | solution.py:364
  67.0 2.8 %collective-permute-start.9 = (bf16[400,128]{1,0:T(8,128)(2,1)S(1)}, bf16[400,128]{1,0:T(8,128)(2,1)S(1)}, u32[]{:S(2)}, u32[]{:S(2)}) collective-permute-start(bf16[400,128]{1,0:T(8,128)(2,1)S(1)} %get-tuple-element.71), channel_id=1, source_target_pairs={{0,24},{4,28},{8,16},{12,20},{16,8},{20,12},{24,0},{28,4},{1,25},{... | collective-permute-start | bytes 307208 | tf_op jit(solution)/shard_map/ppermute | solution.py:364
  69.8 0.0 collective-permute-done.12.refs_1_
  69.8 1.6 %collective-permute-start.10 = (bf16[400,128]{1,0:T(8,128)(2,1)S(1)}, bf16[400,128]{1,0:T(8,128)(2,1)S(1)}, u32[]{:S(2)}, u32[]{:S(2)}) collective-permute-start(bf16[400,128]{1,0:T(8,128)(2,1)S(1)} %get-tuple-element.72), channel_id=1, source_target_pairs={{0,28},{4,24},{8,20},{12,16},{16,12},{20,8},{24,4},{28,0},{1,29},{... | collective-permute-start | bytes 307208 | tf_op jit(solution)/shard_map/ppermute | solution.py:364
  71.4 0.0 collective-permute-done.13.refs_2_
  71.4 0.0 collective-permute-done.14.refs_4_
  71.4 0.0 collective-permute-done.15.refs_5_
  71.4 1.5 %collect.2.refs_2_ = bf16[32,8,1536]{2,1,0:T(8,128)(2,1)} custom-call(s32[1]{0:T(128)} %bitcast.me_ref, f32[3072,128]{1,0:T(8,128)S(1)} %get-tuple-element.50.mem_ref, f32[128,128]{1,0:T(8,128)S(1)} %get-tuple-element.51.lse_ref, bf16[400,128]{1,0:T(8,128)(2,1)S(1)} %collective-permute-done.11.refs_0_, bf16[400,128]{1,0:T(8,128)(2,1)S(1)} %collective-permute-done.12.refs_1_, ...), custom_call_target="tpu_custom_call" | custom-call | tf_op jit(solution)/shard_map/collect/pallas_call | solution.py:346
  73.0 0.6 collective-permute-done.9.refs_0_
  73.5 2.7 %collective-permute-done.10.refs_1_ = bf16[400,128]{1,0:T(8,128)(2,1)S(1)} collective-permute-done((bf16[400,128]{1,0:T(8,128)(2,1)S(1)}, bf16[400,128]{1,0:T(8,128)(2,1)S(1)}, u32[]{:S(2)}, u32[]{:S(2)}) %collective-permute-start.10) | collective-permute-done | bytes 102432 | tf_op jit(solution)/shard_map/ppermute | solution.py:364
  76.2 1.1 %collect.3 = bf16[32,8,1536]{2,1,0:T(8,128)(2,1)} custom-call(s32[1]{0:T(128)} %bitcast.me_ref, f32[3072,128]{1,0:T(8,128)S(1)} %get-tuple-element.50.mem_ref, f32[128,128]{1,0:T(8,128)S(1)} %get-tuple-element.51.lse_ref, bf16[400,128]{1,0:T(8,128)(2,1)S(1)} %collective-permute-done.9.refs_0_, ...), custom_call_target="tpu_custom_call", output_to_operand_aliasing={{}: (5, {})} | custom-call | tf_op jit(solution)/shard_map/collect/pallas_call | solution.py:346
  (3 shorter events, 0.1 us)
Async XLA Ops:
  1.6 38.3 %collective-permute-start.1 = (bf16[1152,128]{1,0:T(8,128)(2,1)S(1)}, bf16[1152,128]{1,0:T(8,128)(2,1)S(1)}, u32[]{:S(2)}, u32[]{:S(2)}) collective-permute-start(bf16[1152,128]{1,0:T(8,128)(2,1)S(1)} %get-tuple-element.40), channel_id=1, source_target_pairs={{0,12},{4,8},{8,4},{12,0},{16,28},{20,24},{24,20},{28,16},{1,13},{... | collective-permute-start | bytes 884744 | tf_op jit(solution)/shard_map/ppermute | solution.py:364
  4.1 37.2 %collective-permute-start.2 = (bf16[1152,128]{1,0:T(8,128)(2,1)S(1)}, bf16[1152,128]{1,0:T(8,128)(2,1)S(1)}, u32[]{:S(2)}, u32[]{:S(2)}) collective-permute-start(bf16[1152,128]{1,0:T(8,128)(2,1)S(1)} %get-tuple-element.41), channel_id=1, source_target_pairs={{0,16},{4,20},{8,24},{12,28},{16,0},{20,4},{24,8},{28,12},{1,17},{... | collective-permute-start | bytes 884744 | tf_op jit(solution)/shard_map/ppermute | solution.py:364
  6.7 47.7 %collective-permute-start = (bf16[1152,128]{1,0:T(8,128)(2,1)S(1)}, bf16[1152,128]{1,0:T(8,128)(2,1)S(1)}, u32[]{:S(2)}, u32[]{:S(2)}) collective-permute-start(bf16[1152,128]{1,0:T(8,128)(2,1)S(1)} %get-tuple-element.39), channel_id=1, source_target_pairs={{0,8},{4,12},{8,0},{12,4},{16,24},{20,28},{24,16},{28,20},{1,9},{5... | collective-permute-start | bytes 884744 | tf_op jit(solution)/shard_map/ppermute | solution.py:364
  8.8 22.5 %collective-permute-start.5 = (bf16[768,128]{1,0:T(8,128)(2,1)S(1)}, bf16[768,128]{1,0:T(8,128)(2,1)S(1)}, u32[]{:S(2)}, u32[]{:S(2)}) collective-permute-start(bf16[768,128]{1,0:T(8,128)(2,1)S(1)} %get-tuple-element.45), channel_id=1, source_target_pairs={{0,28},{4,24},{8,20},{12,16},{16,12},{20,8},{24,4},{28,0},{1,29},{... | collective-permute-start | bytes 589832 | tf_op jit(solution)/shard_map/ppermute | solution.py:364
  9.8 26.0 %collective-permute-start.4 = (bf16[768,128]{1,0:T(8,128)(2,1)S(1)}, bf16[768,128]{1,0:T(8,128)(2,1)S(1)}, u32[]{:S(2)}, u32[]{:S(2)}) collective-permute-start(bf16[768,128]{1,0:T(8,128)(2,1)S(1)} %get-tuple-element.44), channel_id=1, source_target_pairs={{0,24},{4,28},{8,16},{12,20},{16,8},{20,12},{24,0},{28,4},{1,25},{... | collective-permute-start | bytes 589832 | tf_op jit(solution)/shard_map/ppermute | solution.py:364
  13.8 22.0 %copy-start = (f32[12]{0:T(128)S(1)}, f32[12]{0:T(128)}, u32[]{:S(2)}) copy-start(f32[12]{0:T(128)} %bias_ref.1) | copy-start | bytes 148
  31.3 23.1 %collective-permute-start.3 = (bf16[1152,128]{1,0:T(8,128)(2,1)S(1)}, bf16[1152,128]{1,0:T(8,128)(2,1)S(1)}, u32[]{:S(2)}, u32[]{:S(2)}) collective-permute-start(bf16[1152,128]{1,0:T(8,128)(2,1)S(1)} %get-tuple-element.42), channel_id=1, source_target_pairs={{0,20},{4,16},{8,28},{12,24},{16,4},{20,0},{24,12},{28,8},{1,21},{... | collective-permute-start | bytes 884744 | tf_op jit(solution)/shard_map/ppermute | solution.py:364
  35.8 18.6 %collective-permute-start.6 = (bf16[1152,128]{1,0:T(8,128)(2,1)S(1)}, bf16[1152,128]{1,0:T(8,128)(2,1)S(1)}, u32[]{:S(2)}, u32[]{:S(2)}) collective-permute-start(bf16[1152,128]{1,0:T(8,128)(2,1)S(1)} %get-tuple-element.46), channel_id=1, source_target_pairs={{0,4},{4,0},{8,12},{12,8},{16,20},{20,16},{24,28},{28,24},{1,5},{5... | collective-permute-start | bytes 884744 | tf_op jit(solution)/shard_map/ppermute | solution.py:364
  39.9 18.9 %collective-permute-start.7 = (bf16[384,128]{1,0:T(8,128)(2,1)S(1)}, bf16[384,128]{1,0:T(8,128)(2,1)S(1)}, u32[]{:S(2)}, u32[]{:S(2)}) collective-permute-start(bf16[384,128]{1,0:T(8,128)(2,1)S(1)} %get-tuple-element.61), channel_id=1, source_target_pairs={{0,24},{4,28},{8,16},{12,20},{16,8},{20,12},{24,0},{28,4},{1,25},{... | collective-permute-start | bytes 294920 | tf_op jit(solution)/shard_map/ppermute | solution.py:364
  41.3 18.5 %collective-permute-start.8 = (bf16[384,128]{1,0:T(8,128)(2,1)S(1)}, bf16[384,128]{1,0:T(8,128)(2,1)S(1)}, u32[]{:S(2)}, u32[]{:S(2)}) collective-permute-start(bf16[384,128]{1,0:T(8,128)(2,1)S(1)} %get-tuple-element.62), channel_id=1, source_target_pairs={{0,28},{4,24},{8,20},{12,16},{16,12},{20,8},{24,4},{28,0},{1,29},{... | collective-permute-start | bytes 294920 | tf_op jit(solution)/shard_map/ppermute | solution.py:364
  55.7 11.3 %collective-permute-start.11 = (bf16[400,128]{1,0:T(8,128)(2,1)S(1)}, bf16[400,128]{1,0:T(8,128)(2,1)S(1)}, u32[]{:S(2)}, u32[]{:S(2)}) collective-permute-start(bf16[400,128]{1,0:T(8,128)(2,1)S(1)} %get-tuple-element.63), channel_id=1, source_target_pairs={{0,16},{4,20},{8,24},{12,28},{16,0},{20,4},{24,8},{28,12},{1,17},{... | collective-permute-start | bytes 307208 | tf_op jit(solution)/shard_map/ppermute | solution.py:364
  57.9 12.0 %collective-permute-start.12 = (bf16[400,128]{1,0:T(8,128)(2,1)S(1)}, bf16[400,128]{1,0:T(8,128)(2,1)S(1)}, u32[]{:S(2)}, u32[]{:S(2)}) collective-permute-start(bf16[400,128]{1,0:T(8,128)(2,1)S(1)} %get-tuple-element.64), channel_id=1, source_target_pairs={{0,20},{4,16},{8,28},{12,24},{16,4},{20,0},{24,12},{28,8},{1,21},{... | collective-permute-start | bytes 307208 | tf_op jit(solution)/shard_map/ppermute | solution.py:364
  58.2 13.2 %collective-permute-start.13 = (bf16[400,128]{1,0:T(8,128)(2,1)S(1)}, bf16[400,128]{1,0:T(8,128)(2,1)S(1)}, u32[]{:S(2)}, u32[]{:S(2)}) collective-permute-start(bf16[400,128]{1,0:T(8,128)(2,1)S(1)} %get-tuple-element.65), channel_id=1, source_target_pairs={{0,4},{4,0},{8,12},{12,8},{16,20},{20,16},{24,28},{28,24},{1,5},{5... | collective-permute-start | bytes 307208 | tf_op jit(solution)/shard_map/ppermute | solution.py:364
  58.8 12.6 %collective-permute-start.14 = (bf16[400,128]{1,0:T(8,128)(2,1)S(1)}, bf16[400,128]{1,0:T(8,128)(2,1)S(1)}, u32[]{:S(2)}, u32[]{:S(2)}) collective-permute-start(bf16[400,128]{1,0:T(8,128)(2,1)S(1)} %get-tuple-element.67), channel_id=1, source_target_pairs={{0,8},{4,12},{8,0},{12,4},{16,24},{20,28},{24,16},{28,20},{1,9},{5... | collective-permute-start | bytes 307208 | tf_op jit(solution)/shard_map/ppermute | solution.py:364
  59.8 11.6 %collective-permute-start.15 = (bf16[400,128]{1,0:T(8,128)(2,1)S(1)}, bf16[400,128]{1,0:T(8,128)(2,1)S(1)}, u32[]{:S(2)}, u32[]{:S(2)}) collective-permute-start(bf16[400,128]{1,0:T(8,128)(2,1)S(1)} %get-tuple-element.68), channel_id=1, source_target_pairs={{0,12},{4,8},{8,4},{12,0},{16,28},{20,24},{24,20},{28,16},{1,13},{... | collective-permute-start | bytes 307208 | tf_op jit(solution)/shard_map/ppermute | solution.py:364
  67.0 6.5 %collective-permute-start.9 = (bf16[400,128]{1,0:T(8,128)(2,1)S(1)}, bf16[400,128]{1,0:T(8,128)(2,1)S(1)}, u32[]{:S(2)}, u32[]{:S(2)}) collective-permute-start(bf16[400,128]{1,0:T(8,128)(2,1)S(1)} %get-tuple-element.71), channel_id=1, source_target_pairs={{0,24},{4,28},{8,16},{12,20},{16,8},{20,12},{24,0},{28,4},{1,25},{... | collective-permute-start | bytes 307208 | tf_op jit(solution)/shard_map/ppermute | solution.py:364
  69.8 6.3 %collective-permute-start.10 = (bf16[400,128]{1,0:T(8,128)(2,1)S(1)}, bf16[400,128]{1,0:T(8,128)(2,1)S(1)}, u32[]{:S(2)}, u32[]{:S(2)}) collective-permute-start(bf16[400,128]{1,0:T(8,128)(2,1)S(1)} %get-tuple-element.72), channel_id=1, source_target_pairs={{0,28},{4,24},{8,20},{12,16},{16,12},{20,8},{24,4},{28,0},{1,29},{... | collective-permute-start | bytes 307208 | tf_op jit(solution)/shard_map/ppermute | solution.py:364

commit v6 on v5

--- a/solution.py
+++ b/solution.py
@@ -394,14 +394,15 @@
     waves = [parts for parts in waves if parts]
     first = (*early[-1:], *([0] if last else []), *early[:-1])
     got, token = {}, me
-    for parts in waves:
+    for i, parts in enumerate(waves):
         sent = spread(dims, parts, token, args)
         token, _ = lax.optimization_barrier((me, list(sent.values())[0]))
         got.update(zip(sent, exchange(dims, [k for k, _ in sent], sent.values())))
-
-    pooled = pool(dims, keys, values)
-    band = lax.all_gather(pooled[None], "col", axis=0, tiled=True)
-    mem, lse = recall(dims, me, memory_bias, queries, band[:, 0], band[:, 1])
+        if i == 1:
+            pooled = pool(dims, keys, values)
+            band = lax.all_gather(pooled[None], "col", axis=0, tiled=True)
+            mem, lse = recall(dims, me, memory_bias, queries, band[:, 0], band[:, 1])
+            token, mem, lse = lax.optimization_barrier((token, mem, lse))
 
     held = [(k, split(kg)) for kg in order for k in dims.partners(kg)]
     late = [(k, asked) for k in dims.partners(last)]

time: 77.6 us -> 76.7 us (0.988)
  starting transfers between devices: 26.3 us -> 20.9 us
  waiting for transfers between devices: 28.1 us -> 32.5 us
    ppermute x16, starting transfers between devices: 26.3 us -> 20.9 us  [exchange(): lax.ppermute(block, 'row', [(i, i ^ k) for i in range(dims.n_row)])]
    ppermute x16, waiting for transfers between devices: 28.1 us -> 32.5 us  [exchange(): lax.ppermute(block, 'row', [(i, i ^ k) for i in range(dims.n_row)])]
  transfers between devices with their start and end apart: 16 -> 16, of which waited for: 6 -> 7; matrix products, arithmetic and copies ran while one was open for 0% -> 0% of each run, Pallas kernels for 15% -> 16%
where the time goes in v6:
time: 76.7 us; the launch traced here: 76.4 us
  waiting for transfers between devices  32.5 us (42%)
  starting transfers between devices  20.9 us (27%)
  Pallas kernels  14.7 us (19%)
  blocking collectives  8.17 us (11%)
    ppermute x16, waiting for transfers between devices, exchange(): lax.ppermute(block, 'row', [(i, i ^ k) for i in range(dims.n_row)])  32.5 us
    ppermute x16, starting transfers between devices, exchange(): lax.ppermute(block, 'row', [(i, i ^ k) for i in range(dims.n_row)])  20.9 us
    all_gather x1, blocking collectives, per_device(): band = lax.all_gather(pooled[None], 'col', axis=0, tiled=True)  8.17 us
    pallas_call x3, Pallas kernels, spread(): pl.pallas_call(functools.partial(spread_kernel, dims, parts), out_shape=[...  4.12 us
    pallas_call x1, Pallas kernels, recall(): pl.pallas_call(functools.partial(recall_kernel, dims), out_shape=[out, ta...  4.12 us
    pallas_call x2, Pallas kernels, collect(): pl.pallas_call(functools.partial(collect_kernel, dims, kgs), out_shape=ja...  2.68 us
    pallas_call x2, Pallas kernels, attend(): pl.pallas_call(functools.partial(attend_kernel, dims, ks, keys), out_shap...  2.24 us
  transfers between devices with their start and end apart: 16, of which 7 were waited for; matrix products, arithmetic and copies ran while one was open for 0% of the time, Pallas kernels for 16%

profile of v6, /device:TPU:0, one launch (start us, length us, event | category | flops | bytes accessed | tf_op | source)
XLA Modules:
  0.0 76.4 jit_solution(1966634808170967930)
XLA Ops:
  0.0 1.6 %spread.3 = (bf16[1152,128]{1,0:T(8,128)(2,1)S(1)}, bf16[1152,128]{1,0:T(8,128)(2,1)S(1)}, bf16[1152,128]{1,0:T(8,128)(2,1)S(1)}, bf16[1152,128]{1,0:T(8,128)(2,1)S(1)}) custom-call(s32[1]{0:T(128)} %bitcast.me_ref, bf16[32,8,1536]{2,1,0:T(8,128)(2,1)} %refs_0_.5, bf16[32,8,1536]{2,1,0:T(8,128)(2,1)} %refs_1_.5, bf16[32,8,1536]{2,1,0:T(8,128)(2,1)} %refs_2_.5), custom_call_target="tpu_custom_call" | custom-call | tf_op jit(solution)/shard_map/spread/pallas_call | solution.py:113
  1.6 2.5 %collective-permute-start.1 = (bf16[1152,128]{1,0:T(8,128)(2,1)S(1)}, bf16[1152,128]{1,0:T(8,128)(2,1)S(1)}, u32[]{:S(2)}, u32[]{:S(2)}) collective-permute-start(bf16[1152,128]{1,0:T(8,128)(2,1)S(1)} %get-tuple-element.43), channel_id=1, source_target_pairs={{0,12},{4,8},{8,4},{12,0},{16,28},{20,24},{24,20},{28,16},{1,13},{... | collective-permute-start | bytes 884744 | tf_op jit(solution)/shard_map/ppermute | solution.py:364
  4.1 2.6 %collective-permute-start.2 = (bf16[1152,128]{1,0:T(8,128)(2,1)S(1)}, bf16[1152,128]{1,0:T(8,128)(2,1)S(1)}, u32[]{:S(2)}, u32[]{:S(2)}) collective-permute-start(bf16[1152,128]{1,0:T(8,128)(2,1)S(1)} %get-tuple-element.44), channel_id=1, source_target_pairs={{0,16},{4,20},{8,24},{12,28},{16,0},{20,4},{24,8},{28,12},{1,17},{... | collective-permute-start | bytes 884744 | tf_op jit(solution)/shard_map/ppermute | solution.py:364
  6.7 0.0 copy-start
  6.7 0.6 collective-permute-start
  7.3 1.5 %spread.4 = (bf16[768,128]{1,0:T(8,128)(2,1)S(1)}, bf16[768,128]{1,0:T(8,128)(2,1)S(1)}, bf16[1152,128]{1,0:T(8,128)(2,1)S(1)}, bf16[1152,128]{1,0:T(8,128)(2,1)S(1)}) custom-call(s32[1]{0:T(128)} %bitcast.me_ref, bf16[32,8,1536]{2,1,0:T(8,128)(2,1)} %refs_0_.5, bf16[32,8,1536]{2,1,0:T(8,128)(2,1)} %refs_1_.5, bf16[32,8,1536]{2,1,0:T(8,128)(2,1)} %refs_2_.5), custom_call_target="tpu_custom_call" | custom-call | tf_op jit(solution)/shard_map/spread/pallas_call | solution.py:113
  8.8 1.0 %collective-permute-start.5 = (bf16[768,128]{1,0:T(8,128)(2,1)S(1)}, bf16[768,128]{1,0:T(8,128)(2,1)S(1)}, u32[]{:S(2)}, u32[]{:S(2)}) collective-permute-start(bf16[768,128]{1,0:T(8,128)(2,1)S(1)} %get-tuple-element.48), channel_id=1, source_target_pairs={{0,28},{4,24},{8,20},{12,16},{16,12},{20,8},{24,4},{28,0},{1,29},{... | collective-permute-start | bytes 589832 | tf_op jit(solution)/shard_map/ppermute | solution.py:364
  9.8 2.4 %collective-permute-start.4 = (bf16[768,128]{1,0:T(8,128)(2,1)S(1)}, bf16[768,128]{1,0:T(8,128)(2,1)S(1)}, u32[]{:S(2)}, u32[]{:S(2)}) collective-permute-start(bf16[768,128]{1,0:T(8,128)(2,1)S(1)} %get-tuple-element.47), channel_id=1, source_target_pairs={{0,24},{4,28},{8,16},{12,20},{16,8},{20,12},{24,0},{28,4},{1,25},{... | collective-permute-start | bytes 589832 | tf_op jit(solution)/shard_map/ppermute | solution.py:364
  12.3 1.5 %pool.1 = f32[2,1536]{1,0:T(2,128)S(1)} custom-call(bf16[32,8,1536]{2,1,0:T(8,128)(2,1)} %refs_1_.5, bf16[32,8,1536]{2,1,0:T(8,128)(2,1)} %refs_2_.5), custom_call_target="tpu_custom_call" | custom-call | tf_op jit(solution)/shard_map/pool/pallas_call | solution.py:151
  13.8 8.2 %all-gather.1 = bf16[4,2,1536]{2,1,0:T(2,128)(2,1)S(1)} all-gather(bf16[1,2,1536]{2,1,0:T(2,128)(2,1)S(1)} %convert_bitcast_fusion), channel_id=2, replica_groups=mesh['row'=8,'col'=4] {'col'}, dimensions={0}, use_global_device_ids=true | all-gather | bytes 30720 | tf_op jit(solution)/shard_map/all_gather | solution.py:403
  22.0 9.3 %collective-permute-done.5.refs_5_ = bf16[768,128]{1,0:T(8,128)(2,1)S(1)} collective-permute-done((bf16[768,128]{1,0:T(8,128)(2,1)S(1)}, bf16[768,128]{1,0:T(8,128)(2,1)S(1)}, u32[]{:S(2)}, u32[]{:S(2)}) %collective-permute-start.5) | collective-permute-done | bytes 196640 | tf_op jit(solution)/shard_map/ppermute | solution.py:364
  31.3 0.0 collective-permute-start.3
  31.3 4.5 %collective-permute-done.4.refs_4_ = bf16[768,128]{1,0:T(8,128)(2,1)S(1)} collective-permute-done((bf16[768,128]{1,0:T(8,128)(2,1)S(1)}, bf16[768,128]{1,0:T(8,128)(2,1)S(1)}, u32[]{:S(2)}, u32[]{:S(2)}) %collective-permute-start.4) | collective-permute-done | bytes 196640 | tf_op jit(solution)/shard_map/ppermute | solution.py:364
  35.8 0.0 collective-permute-start.6
  35.8 0.0 copy-done
  35.8 4.1 %recall.1 = (f32[3072,128]{1,0:T(8,128)S(1)}, f32[128,128]{1,0:T(8,128)S(1)}) custom-call(s32[1]{0:T(128)} %bitcast.me_ref, f32[12]{0:T(128)S(1)} %copy-done, bf16[32,8,1536]{2,1,0:T(8,128)(2,1)} %refs_0_.5, bf16[4,1536]{1,0:T(4,128)(2,1)S(1)} %get-tuple-element.82.key_ref, bf16[4,1536]{1,0:T(4,128)(2,1)S(1)} %get-tuple-element.81.value_ref), custom_call_target="tpu_custom_call" | custom-call | tf_op jit(solution)/shard_map/recall/pallas_call | solution.py:209
  39.9 1.1 %spread.5 = (bf16[384,128]{1,0:T(8,128)(2,1)S(1)}, bf16[384,128]{1,0:T(8,128)(2,1)S(1)}) custom-call(s32[1]{0:T(128)} %bitcast.me_ref, bf16[32,8,1536]{2,1,0:T(8,128)(2,1)} %refs_0_.5, bf16[32,8,1536]{2,1,0:T(8,128)(2,1)} %refs_1_.5, bf16[32,8,1536]{2,1,0:T(8,128)(2,1)} %refs_2_.5), custom_call_target="tpu_custom_call" | custom-call | tf_op jit(solution)/shard_map/spread/pallas_call | solution.py:113
  41.0 0.0 collective-permute-done.1.refs_1_
  41.0 1.3 %collective-permute-start.7 = (bf16[384,128]{1,0:T(8,128)(2,1)S(1)}, bf16[384,128]{1,0:T(8,128)(2,1)S(1)}, u32[]{:S(2)}, u32[]{:S(2)}) collective-permute-start(bf16[384,128]{1,0:T(8,128)(2,1)S(1)} %get-tuple-element.67), channel_id=1, source_target_pairs={{0,24},{4,28},{8,16},{12,20},{16,8},{20,12},{24,0},{28,4},{1,25},{... | collective-permute-start | bytes 294920 | tf_op jit(solution)/shard_map/ppermute | solution.py:364
  42.4 0.0 collective-permute-done.2.refs_2_
  42.4 2.4 %collective-permute-start.8 = (bf16[384,128]{1,0:T(8,128)(2,1)S(1)}, bf16[384,128]{1,0:T(8,128)(2,1)S(1)}, u32[]{:S(2)}, u32[]{:S(2)}) collective-permute-start(bf16[384,128]{1,0:T(8,128)(2,1)S(1)} %get-tuple-element.68), channel_id=1, source_target_pairs={{0,28},{4,24},{8,20},{12,16},{16,12},{20,8},{24,4},{28,0},{1,29},{... | collective-permute-start | bytes 294920 | tf_op jit(solution)/shard_map/ppermute | solution.py:364
  44.7 9.6 %collective-permute-done.3.refs_3_ = bf16[1152,128]{1,0:T(8,128)(2,1)S(1)} collective-permute-done((bf16[1152,128]{1,0:T(8,128)(2,1)S(1)}, bf16[1152,128]{1,0:T(8,128)(2,1)S(1)}, u32[]{:S(2)}, u32[]{:S(2)}) %collective-permute-start.3) | collective-permute-done | bytes 294944 | tf_op jit(solution)/shard_map/ppermute | solution.py:364
  54.4 0.0 collective-permute-done.refs_0_
  54.4 0.0 collective-permute-done.6.refs_6_
  54.4 1.4 %attend.2 = (bf16[400,128]{1,0:T(8,128)(2,1)S(1)}, bf16[400,128]{1,0:T(8,128)(2,1)S(1)}, bf16[400,128]{1,0:T(8,128)(2,1)S(1)}, bf16[400,128]{1,0:T(8,128)(2,1)S(...) custom-call(bf16[1152,128]{1,0:T(8,128)(2,1)S(1)} %collective-permute-done.refs_0_, ...), custom_call_target="tpu_custom_call" | custom-call | flops 603979776 | bytes 2359296 | tf_op jit(solution)/shard_map/attend/pallas_call | solution.py:267
  55.7 0.2 collective-permute-start.11
  55.9 2.5 %collective-permute-start.12 = (bf16[400,128]{1,0:T(8,128)(2,1)S(1)}, bf16[400,128]{1,0:T(8,128)(2,1)S(1)}, u32[]{:S(2)}, u32[]{:S(2)}) collective-permute-start(bf16[400,128]{1,0:T(8,128)(2,1)S(1)} %get-tuple-element.70), channel_id=1, source_target_pairs={{0,20},{4,16},{8,28},{12,24},{16,4},{20,0},{24,12},{28,8},{1,21},{... | collective-permute-start | bytes 307208 | tf_op jit(solution)/shard_map/ppermute | solution.py:364
  58.5 0.4 collective-permute-start.13
  58.9 0.0 collective-permute-done.7.refs_8_
  58.9 0.4 collective-permute-start.14
  59.2 0.0 collective-permute-done.8.refs_9_
  59.2 1.1 %collective-permute-start.15 = (bf16[400,128]{1,0:T(8,128)(2,1)S(1)}, bf16[400,128]{1,0:T(8,128)(2,1)S(1)}, u32[]{:S(2)}, u32[]{:S(2)}) collective-permute-start(bf16[400,128]{1,0:T(8,128)(2,1)S(1)} %get-tuple-element.74), channel_id=1, source_target_pairs={{0,12},{4,8},{8,4},{12,0},{16,28},{20,24},{24,20},{28,16},{1,13},{... | collective-permute-start | bytes 307208 | tf_op jit(solution)/shard_map/ppermute | solution.py:364
  60.4 0.9 %attend.3 = (bf16[400,128]{1,0:T(8,128)(2,1)S(1)}, bf16[400,128]{1,0:T(8,128)(2,1)S(1)}) custom-call(bf16[1152,128]{1,0:T(8,128)(2,1)S(1)} %collective-permute-done.refs_0_, bf16[1152,128]{1,0:T(8,128)(2,1)S(1)} %collective-permute-done.1.refs_1_, bf16[1152,128]{1,0:T(8,128)(2,1)S(1)} %collective-permute-done.2.refs_2_, ...), custom_call_target="tpu_custom_call" | custom-call | flops 603979776 | bytes 2359296 | tf_op jit(solution)/shard_map/attend/pallas_call | solution.py:267
  61.2 5.1 %collective-permute-done.11.refs_0_ = bf16[400,128]{1,0:T(8,128)(2,1)S(1)} collective-permute-done((bf16[400,128]{1,0:T(8,128)(2,1)S(1)}, bf16[400,128]{1,0:T(8,128)(2,1)S(1)}, u32[]{:S(2)}, u32[]{:S(2)}) %collective-permute-start.11) | collective-permute-done | bytes 102432 | tf_op jit(solution)/shard_map/ppermute | solution.py:364
  66.4 2.0 %collective-permute-start.9 = (bf16[400,128]{1,0:T(8,128)(2,1)S(1)}, bf16[400,128]{1,0:T(8,128)(2,1)S(1)}, u32[]{:S(2)}, u32[]{:S(2)}) collective-permute-start(bf16[400,128]{1,0:T(8,128)(2,1)S(1)} %get-tuple-element.77), channel_id=1, source_target_pairs={{0,24},{4,28},{8,16},{12,20},{16,8},{20,12},{24,0},{28,4},{1,25},{... | collective-permute-start | bytes 307208 | tf_op jit(solution)/shard_map/ppermute | solution.py:364
  68.3 0.1 collective-permute-done.12.refs_1_
  68.5 1.4 %collective-permute-start.10 = (bf16[400,128]{1,0:T(8,128)(2,1)S(1)}, bf16[400,128]{1,0:T(8,128)(2,1)S(1)}, u32[]{:S(2)}, u32[]{:S(2)}) collective-permute-start(bf16[400,128]{1,0:T(8,128)(2,1)S(1)} %get-tuple-element.78), channel_id=1, source_target_pairs={{0,28},{4,24},{8,20},{12,16},{16,12},{20,8},{24,4},{28,0},{1,29},{... | collective-permute-start | bytes 307208 | tf_op jit(solution)/shard_map/ppermute | solution.py:364
  69.9 0.0 collective-permute-done.13.refs_2_
  69.9 0.0 collective-permute-done.14.refs_4_
  69.9 0.0 collective-permute-done.15.refs_5_
  69.9 1.5 %collect.2.refs_2_ = bf16[32,8,1536]{2,1,0:T(8,128)(2,1)} custom-call(s32[1]{0:T(128)} %bitcast.me_ref, f32[3072,128]{1,0:T(8,128)S(1)} %get-tuple-element.56.mem_ref, f32[128,128]{1,0:T(8,128)S(1)} %get-tuple-element.57.lse_ref, bf16[400,128]{1,0:T(8,128)(2,1)S(1)} %collective-permute-done.11.refs_0_, bf16[400,128]{1,0:T(8,128)(2,1)S(1)} %collective-permute-done.12.refs_1_, ...), custom_call_target="tpu_custom_call" | custom-call | tf_op jit(solution)/shard_map/collect/pallas_call | solution.py:346
  71.5 1.6 %collective-permute-done.9.refs_0_ = bf16[400,128]{1,0:T(8,128)(2,1)S(1)} collective-permute-done((bf16[400,128]{1,0:T(8,128)(2,1)S(1)}, bf16[400,128]{1,0:T(8,128)(2,1)S(1)}, u32[]{:S(2)}, u32[]{:S(2)}) %collective-permute-start.9) | collective-permute-done | bytes 102432 | tf_op jit(solution)/shard_map/ppermute | solution.py:364
  73.1 2.2 %collective-permute-done.10.refs_1_ = bf16[400,128]{1,0:T(8,128)(2,1)S(1)} collective-permute-done((bf16[400,128]{1,0:T(8,128)(2,1)S(1)}, bf16[400,128]{1,0:T(8,128)(2,1)S(1)}, u32[]{:S(2)}, u32[]{:S(2)}) %collective-permute-start.10) | collective-permute-done | bytes 102432 | tf_op jit(solution)/shard_map/ppermute | solution.py:364
  75.3 1.1 %collect.3 = bf16[32,8,1536]{2,1,0:T(8,128)(2,1)} custom-call(s32[1]{0:T(128)} %bitcast.me_ref, f32[3072,128]{1,0:T(8,128)S(1)} %get-tuple-element.56.mem_ref, f32[128,128]{1,0:T(8,128)S(1)} %get-tuple-element.57.lse_ref, bf16[400,128]{1,0:T(8,128)(2,1)S(1)} %collective-permute-done.9.refs_0_, ...), custom_call_target="tpu_custom_call", output_to_operand_aliasing={{}: (5, {})} | custom-call | tf_op jit(solution)/shard_map/collect/pallas_call | solution.py:346
  (3 shorter events, 0.1 us)
Async XLA Ops:
  1.6 39.4 %collective-permute-start.1 = (bf16[1152,128]{1,0:T(8,128)(2,1)S(1)}, bf16[1152,128]{1,0:T(8,128)(2,1)S(1)}, u32[]{:S(2)}, u32[]{:S(2)}) collective-permute-start(bf16[1152,128]{1,0:T(8,128)(2,1)S(1)} %get-tuple-element.43), channel_id=1, source_target_pairs={{0,12},{4,8},{8,4},{12,0},{16,28},{20,24},{24,20},{28,16},{1,13},{... | collective-permute-start | bytes 884744 | tf_op jit(solution)/shard_map/ppermute | solution.py:364
  4.1 38.2 %collective-permute-start.2 = (bf16[1152,128]{1,0:T(8,128)(2,1)S(1)}, bf16[1152,128]{1,0:T(8,128)(2,1)S(1)}, u32[]{:S(2)}, u32[]{:S(2)}) collective-permute-start(bf16[1152,128]{1,0:T(8,128)(2,1)S(1)} %get-tuple-element.44), channel_id=1, source_target_pairs={{0,16},{4,20},{8,24},{12,28},{16,0},{20,4},{24,8},{28,12},{1,17},{... | collective-permute-start | bytes 884744 | tf_op jit(solution)/shard_map/ppermute | solution.py:364
  6.7 29.1 %copy-start = (f32[12]{0:T(128)S(1)}, f32[12]{0:T(128)}, u32[]{:S(2)}) copy-start(f32[12]{0:T(128)} %bias_ref.1) | copy-start | bytes 148
  6.7 47.7 %collective-permute-start = (bf16[1152,128]{1,0:T(8,128)(2,1)S(1)}, bf16[1152,128]{1,0:T(8,128)(2,1)S(1)}, u32[]{:S(2)}, u32[]{:S(2)}) collective-permute-start(bf16[1152,128]{1,0:T(8,128)(2,1)S(1)} %get-tuple-element.42), channel_id=1, source_target_pairs={{0,8},{4,12},{8,0},{12,4},{16,24},{20,28},{24,16},{28,20},{1,9},{5... | collective-permute-start | bytes 884744 | tf_op jit(solution)/shard_map/ppermute | solution.py:364
  8.8 22.5 %collective-permute-start.5 = (bf16[768,128]{1,0:T(8,128)(2,1)S(1)}, bf16[768,128]{1,0:T(8,128)(2,1)S(1)}, u32[]{:S(2)}, u32[]{:S(2)}) collective-permute-start(bf16[768,128]{1,0:T(8,128)(2,1)S(1)} %get-tuple-element.48), channel_id=1, source_target_pairs={{0,28},{4,24},{8,20},{12,16},{16,12},{20,8},{24,4},{28,0},{1,29},{... | collective-permute-start | bytes 589832 | tf_op jit(solution)/shard_map/ppermute | solution.py:364
  9.8 26.0 %collective-permute-start.4 = (bf16[768,128]{1,0:T(8,128)(2,1)S(1)}, bf16[768,128]{1,0:T(8,128)(2,1)S(1)}, u32[]{:S(2)}, u32[]{:S(2)}) collective-permute-start(bf16[768,128]{1,0:T(8,128)(2,1)S(1)} %get-tuple-element.47), channel_id=1, source_target_pairs={{0,24},{4,28},{8,16},{12,20},{16,8},{20,12},{24,0},{28,4},{1,25},{... | collective-permute-start | bytes 589832 | tf_op jit(solution)/shard_map/ppermute | solution.py:364
  31.3 23.1 %collective-permute-start.3 = (bf16[1152,128]{1,0:T(8,128)(2,1)S(1)}, bf16[1152,128]{1,0:T(8,128)(2,1)S(1)}, u32[]{:S(2)}, u32[]{:S(2)}) collective-permute-start(bf16[1152,128]{1,0:T(8,128)(2,1)S(1)} %get-tuple-element.45), channel_id=1, source_target_pairs={{0,20},{4,16},{8,28},{12,24},{16,4},{20,0},{24,12},{28,8},{1,21},{... | collective-permute-start | bytes 884744 | tf_op jit(solution)/shard_map/ppermute | solution.py:364
  35.8 18.6 %collective-permute-start.6 = (bf16[1152,128]{1,0:T(8,128)(2,1)S(1)}, bf16[1152,128]{1,0:T(8,128)(2,1)S(1)}, u32[]{:S(2)}, u32[]{:S(2)}) collective-permute-start(bf16[1152,128]{1,0:T(8,128)(2,1)S(1)} %get-tuple-element.49), channel_id=1, source_target_pairs={{0,4},{4,0},{8,12},{12,8},{16,20},{20,16},{24,28},{28,24},{1,5},{5... | collective-permute-start | bytes 884744 | tf_op jit(solution)/shard_map/ppermute | solution.py:364
  41.0 17.8 %collective-permute-start.7 = (bf16[384,128]{1,0:T(8,128)(2,1)S(1)}, bf16[384,128]{1,0:T(8,128)(2,1)S(1)}, u32[]{:S(2)}, u32[]{:S(2)}) collective-permute-start(bf16[384,128]{1,0:T(8,128)(2,1)S(1)} %get-tuple-element.67), channel_id=1, source_target_pairs={{0,24},{4,28},{8,16},{12,20},{16,8},{20,12},{24,0},{28,4},{1,25},{... | collective-permute-start | bytes 294920 | tf_op jit(solution)/shard_map/ppermute | solution.py:364
  42.4 16.9 %collective-permute-start.8 = (bf16[384,128]{1,0:T(8,128)(2,1)S(1)}, bf16[384,128]{1,0:T(8,128)(2,1)S(1)}, u32[]{:S(2)}, u32[]{:S(2)}) collective-permute-start(bf16[384,128]{1,0:T(8,128)(2,1)S(1)} %get-tuple-element.68), channel_id=1, source_target_pairs={{0,28},{4,24},{8,20},{12,16},{16,12},{20,8},{24,4},{28,0},{1,29},{... | collective-permute-start | bytes 294920 | tf_op jit(solution)/shard_map/ppermute | solution.py:364
  55.7 10.6 %collective-permute-start.11 = (bf16[400,128]{1,0:T(8,128)(2,1)S(1)}, bf16[400,128]{1,0:T(8,128)(2,1)S(1)}, u32[]{:S(2)}, u32[]{:S(2)}) collective-permute-start(bf16[400,128]{1,0:T(8,128)(2,1)S(1)} %get-tuple-element.69), channel_id=1, source_target_pairs={{0,16},{4,20},{8,24},{12,28},{16,0},{20,4},{24,8},{28,12},{1,17},{... | collective-permute-start | bytes 307208 | tf_op jit(solution)/shard_map/ppermute | solution.py:364
  55.9 12.5 %collective-permute-start.12 = (bf16[400,128]{1,0:T(8,128)(2,1)S(1)}, bf16[400,128]{1,0:T(8,128)(2,1)S(1)}, u32[]{:S(2)}, u32[]{:S(2)}) collective-permute-start(bf16[400,128]{1,0:T(8,128)(2,1)S(1)} %get-tuple-element.70), channel_id=1, source_target_pairs={{0,20},{4,16},{8,28},{12,24},{16,4},{20,0},{24,12},{28,8},{1,21},{... | collective-permute-start | bytes 307208 | tf_op jit(solution)/shard_map/ppermute | solution.py:364
  58.5 11.4 %collective-permute-start.13 = (bf16[400,128]{1,0:T(8,128)(2,1)S(1)}, bf16[400,128]{1,0:T(8,128)(2,1)S(1)}, u32[]{:S(2)}, u32[]{:S(2)}) collective-permute-start(bf16[400,128]{1,0:T(8,128)(2,1)S(1)} %get-tuple-element.71), channel_id=1, source_target_pairs={{0,4},{4,0},{8,12},{12,8},{16,20},{20,16},{24,28},{28,24},{1,5},{5... | collective-permute-start | bytes 307208 | tf_op jit(solution)/shard_map/ppermute | solution.py:364
  58.9 11.1 %collective-permute-start.14 = (bf16[400,128]{1,0:T(8,128)(2,1)S(1)}, bf16[400,128]{1,0:T(8,128)(2,1)S(1)}, u32[]{:S(2)}, u32[]{:S(2)}) collective-permute-start(bf16[400,128]{1,0:T(8,128)(2,1)S(1)} %get-tuple-element.73), channel_id=1, source_target_pairs={{0,8},{4,12},{8,0},{12,4},{16,24},{20,28},{24,16},{28,20},{1,9},{5... | collective-permute-start | bytes 307208 | tf_op jit(solution)/shard_map/ppermute | solution.py:364
  59.2 10.7 %collective-permute-start.15 = (bf16[400,128]{1,0:T(8,128)(2,1)S(1)}, bf16[400,128]{1,0:T(8,128)(2,1)S(1)}, u32[]{:S(2)}, u32[]{:S(2)}) collective-permute-start(bf16[400,128]{1,0:T(8,128)(2,1)S(1)} %get-tuple-element.74), channel_id=1, source_target_pairs={{0,12},{4,8},{8,4},{12,0},{16,28},{20,24},{24,20},{28,16},{1,13},{... | collective-permute-start | bytes 307208 | tf_op jit(solution)/shard_map/ppermute | solution.py:364
  66.4 6.7 %collective-permute-start.9 = (bf16[400,128]{1,0:T(8,128)(2,1)S(1)}, bf16[400,128]{1,0:T(8,128)(2,1)S(1)}, u32[]{:S(2)}, u32[]{:S(2)}) collective-permute-start(bf16[400,128]{1,0:T(8,128)(2,1)S(1)} %get-tuple-element.77), channel_id=1, source_target_pairs={{0,24},{4,28},{8,16},{12,20},{16,8},{20,12},{24,0},{28,4},{1,25},{... | collective-permute-start | bytes 307208 | tf_op jit(solution)/shard_map/ppermute | solution.py:364
  68.5 6.8 %collective-permute-start.10 = (bf16[400,128]{1,0:T(8,128)(2,1)S(1)}, bf16[400,128]{1,0:T(8,128)(2,1)S(1)}, u32[]{:S(2)}, u32[]{:S(2)}) collective-permute-start(bf16[400,128]{1,0:T(8,128)(2,1)S(1)} %get-tuple-element.78), channel_id=1, source_target_pairs={{0,28},{4,24},{8,20},{12,16},{16,12},{20,8},{24,4},{28,0},{1,29},{... | collective-permute-start | bytes 307208 | tf_op jit(solution)/shard_map/ppermute | solution.py:364

commit v7 on v6

--- a/solution.py
+++ b/solution.py
@@ -388,8 +388,8 @@
     early = [kg for kg in order if kg not in (last, 0)]
     waves = [
         [(kg, every) for kg in early],
-        [(last, both)] + [(0, every)] * (last > 0),
-        [(last, asked)],
+        [(last, both)],
+        [(last, asked)] + [(0, every)] * (last > 0),
     ]
     waves = [parts for parts in waves if parts]
     first = (*early[-1:], *([0] if last else []), *early[:-1])

time: 76.7 us -> 76.7 us (level)
  no operation moved by 1% of the time
where the time goes in v7:
time: 76.7 us; the launch traced here: 76.4 us
  waiting for transfers between devices  32.6 us (43%)
  starting transfers between devices  20.8 us (27%)
  Pallas kernels  14.7 us (19%)
  blocking collectives  8.17 us (11%)
    ppermute x16, waiting for transfers between devices, exchange(): lax.ppermute(block, 'row', [(i, i ^ k) for i in range(dims.n_row)])  32.6 us
    ppermute x16, starting transfers between devices, exchange(): lax.ppermute(block, 'row', [(i, i ^ k) for i in range(dims.n_row)])  20.8 us
    all_gather x1, blocking collectives, per_device(): band = lax.all_gather(pooled[None], 'col', axis=0, tiled=True)  8.17 us
    pallas_call x1, Pallas kernels, recall(): pl.pallas_call(functools.partial(recall_kernel, dims), out_shape=[out, ta...  4.12 us
    pallas_call x3, Pallas kernels, spread(): pl.pallas_call(functools.partial(spread_kernel, dims, parts), out_shape=[...  4.12 us
    pallas_call x2, Pallas kernels, collect(): pl.pallas_call(functools.partial(collect_kernel, dims, kgs), out_shape=ja...  2.67 us
    pallas_call x2, Pallas kernels, attend(): pl.pallas_call(functools.partial(attend_kernel, dims, ks, keys), out_shap...  2.23 us
  transfers between devices with their start and end apart: 16, of which 7 were waited for; matrix products, arithmetic and copies ran while one was open for 0% of the time, Pallas kernels for 16%

profile of v7, /device:TPU:0, one launch (start us, length us, event | category | flops | bytes accessed | tf_op | source)
XLA Modules:
  0.0 76.4 jit_solution(16257589145429938951)
XLA Ops:
  0.0 1.6 %spread.3 = (bf16[1152,128]{1,0:T(8,128)(2,1)S(1)}, bf16[1152,128]{1,0:T(8,128)(2,1)S(1)}, bf16[1152,128]{1,0:T(8,128)(2,1)S(1)}, bf16[1152,128]{1,0:T(8,128)(2,1)S(1)}) custom-call(s32[1]{0:T(128)} %bitcast.me_ref, bf16[32,8,1536]{2,1,0:T(8,128)(2,1)} %refs_0_.5, bf16[32,8,1536]{2,1,0:T(8,128)(2,1)} %refs_1_.5, bf16[32,8,1536]{2,1,0:T(8,128)(2,1)} %refs_2_.5), custom_call_target="tpu_custom_call" | custom-call | tf_op jit(solution)/shard_map/spread/pallas_call | solution.py:113
  1.6 2.5 %collective-permute-start.1 = (bf16[1152,128]{1,0:T(8,128)(2,1)S(1)}, bf16[1152,128]{1,0:T(8,128)(2,1)S(1)}, u32[]{:S(2)}, u32[]{:S(2)}) collective-permute-start(bf16[1152,128]{1,0:T(8,128)(2,1)S(1)} %get-tuple-element.43), channel_id=1, source_target_pairs={{0,12},{4,8},{8,4},{12,0},{16,28},{20,24},{24,20},{28,16},{1,13},{... | collective-permute-start | bytes 884744 | tf_op jit(solution)/shard_map/ppermute | solution.py:364
  4.1 2.6 %collective-permute-start.2 = (bf16[1152,128]{1,0:T(8,128)(2,1)S(1)}, bf16[1152,128]{1,0:T(8,128)(2,1)S(1)}, u32[]{:S(2)}, u32[]{:S(2)}) collective-permute-start(bf16[1152,128]{1,0:T(8,128)(2,1)S(1)} %get-tuple-element.44), channel_id=1, source_target_pairs={{0,16},{4,20},{8,24},{12,28},{16,0},{20,4},{24,8},{28,12},{1,17},{... | collective-permute-start | bytes 884744 | tf_op jit(solution)/shard_map/ppermute | solution.py:364
  6.7 0.0 copy-start
  6.7 0.6 collective-permute-start
  7.3 1.1 %spread.4 = (bf16[768,128]{1,0:T(8,128)(2,1)S(1)}, bf16[768,128]{1,0:T(8,128)(2,1)S(1)}) custom-call(s32[1]{0:T(128)} %bitcast.me_ref, bf16[32,8,1536]{2,1,0:T(8,128)(2,1)} %refs_0_.5, bf16[32,8,1536]{2,1,0:T(8,128)(2,1)} %refs_1_.5, bf16[32,8,1536]{2,1,0:T(8,128)(2,1)} %refs_2_.5), custom_call_target="tpu_custom_call" | custom-call | tf_op jit(solution)/shard_map/spread/pallas_call | solution.py:113
  8.5 1.0 %collective-permute-start.5 = (bf16[768,128]{1,0:T(8,128)(2,1)S(1)}, bf16[768,128]{1,0:T(8,128)(2,1)S(1)}, u32[]{:S(2)}, u32[]{:S(2)}) collective-permute-start(bf16[768,128]{1,0:T(8,128)(2,1)S(1)} %get-tuple-element.48), channel_id=1, source_target_pairs={{0,28},{4,24},{8,20},{12,16},{16,12},{20,8},{24,4},{28,0},{1,29},{... | collective-permute-start | bytes 589832 | tf_op jit(solution)/shard_map/ppermute | solution.py:364
  9.5 2.4 %collective-permute-start.4 = (bf16[768,128]{1,0:T(8,128)(2,1)S(1)}, bf16[768,128]{1,0:T(8,128)(2,1)S(1)}, u32[]{:S(2)}, u32[]{:S(2)}) collective-permute-start(bf16[768,128]{1,0:T(8,128)(2,1)S(1)} %get-tuple-element.47), channel_id=1, source_target_pairs={{0,24},{4,28},{8,16},{12,20},{16,8},{20,12},{24,0},{28,4},{1,25},{... | collective-permute-start | bytes 589832 | tf_op jit(solution)/shard_map/ppermute | solution.py:364
  11.9 1.5 %pool.1 = f32[2,1536]{1,0:T(2,128)S(1)} custom-call(bf16[32,8,1536]{2,1,0:T(8,128)(2,1)} %refs_1_.5, bf16[32,8,1536]{2,1,0:T(8,128)(2,1)} %refs_2_.5), custom_call_target="tpu_custom_call" | custom-call | tf_op jit(solution)/shard_map/pool/pallas_call | solution.py:151
  13.5 8.2 %all-gather.1 = bf16[4,2,1536]{2,1,0:T(2,128)(2,1)S(1)} all-gather(bf16[1,2,1536]{2,1,0:T(2,128)(2,1)S(1)} %convert_bitcast_fusion), channel_id=2, replica_groups=mesh['row'=8,'col'=4] {'col'}, dimensions={0}, use_global_device_ids=true | all-gather | bytes 30720 | tf_op jit(solution)/shard_map/all_gather | solution.py:403
  21.7 0.0 copy-done
  21.7 4.1 %recall.1 = (f32[3072,128]{1,0:T(8,128)S(1)}, f32[128,128]{1,0:T(8,128)S(1)}) custom-call(s32[1]{0:T(128)} %bitcast.me_ref, f32[12]{0:T(128)S(1)} %copy-done, bf16[32,8,1536]{2,1,0:T(8,128)(2,1)} %refs_0_.5, bf16[4,1536]{1,0:T(4,128)(2,1)S(1)} %get-tuple-element.82.key_ref, bf16[4,1536]{1,0:T(4,128)(2,1)S(1)} %get-tuple-element.81.value_ref), custom_call_target="tpu_custom_call" | custom-call | tf_op jit(solution)/shard_map/recall/pallas_call | solution.py:209
  25.8 1.4 %spread.5 = (bf16[384,128]{1,0:T(8,128)(2,1)S(1)}, bf16[384,128]{1,0:T(8,128)(2,1)S(1)}, bf16[1152,128]{1,0:T(8,128)(2,1)S(1)}, bf16[1152,128]{1,0:T(8,128)(2,1)S(1)}) custom-call(s32[1]{0:T(128)} %bitcast.me_ref, bf16[32,8,1536]{2,1,0:T(8,128)(2,1)} %refs_0_.5, bf16[32,8,1536]{2,1,0:T(8,128)(2,1)} %refs_1_.5, bf16[32,8,1536]{2,1,0:T(8,128)(2,1)} %refs_2_.5), custom_call_target="tpu_custom_call" | custom-call | tf_op jit(solution)/shard_map/spread/pallas_call | solution.py:113
  27.2 4.1 %collective-permute-done.5.refs_5_ = bf16[768,128]{1,0:T(8,128)(2,1)S(1)} collective-permute-done((bf16[768,128]{1,0:T(8,128)(2,1)S(1)}, bf16[768,128]{1,0:T(8,128)(2,1)S(1)}, u32[]{:S(2)}, u32[]{:S(2)}) %collective-permute-start.5) | collective-permute-done | bytes 196640 | tf_op jit(solution)/shard_map/ppermute | solution.py:364
  31.3 0.0 collective-permute-start.3
  31.3 4.5 %collective-permute-done.4.refs_4_ = bf16[768,128]{1,0:T(8,128)(2,1)S(1)} collective-permute-done((bf16[768,128]{1,0:T(8,128)(2,1)S(1)}, bf16[768,128]{1,0:T(8,128)(2,1)S(1)}, u32[]{:S(2)}, u32[]{:S(2)}) %collective-permute-start.4) | collective-permute-done | bytes 196640 | tf_op jit(solution)/shard_map/ppermute | solution.py:364
  35.8 0.0 collective-permute-start.6
  35.8 0.0 collective-permute-done.1.refs_1_
  35.8 1.3 %collective-permute-start.7 = (bf16[384,128]{1,0:T(8,128)(2,1)S(1)}, bf16[384,128]{1,0:T(8,128)(2,1)S(1)}, u32[]{:S(2)}, u32[]{:S(2)}) collective-permute-start(bf16[384,128]{1,0:T(8,128)(2,1)S(1)} %get-tuple-element.67), channel_id=1, source_target_pairs={{0,24},{4,28},{8,16},{12,20},{16,8},{20,12},{24,0},{28,4},{1,25},{... | collective-permute-start | bytes 294920 | tf_op jit(solution)/shard_map/ppermute | solution.py:364
  37.1 0.0 collective-permute-done.2.refs_2_
  37.1 2.4 %collective-permute-start.8 = (bf16[384,128]{1,0:T(8,128)(2,1)S(1)}, bf16[384,128]{1,0:T(8,128)(2,1)S(1)}, u32[]{:S(2)}, u32[]{:S(2)}) collective-permute-start(bf16[384,128]{1,0:T(8,128)(2,1)S(1)} %get-tuple-element.68), channel_id=1, source_target_pairs={{0,28},{4,24},{8,20},{12,16},{16,12},{20,8},{24,4},{28,0},{1,29},{... | collective-permute-start | bytes 294920 | tf_op jit(solution)/shard_map/ppermute | solution.py:364
  39.4 14.9 %collective-permute-done.3.refs_3_ = bf16[1152,128]{1,0:T(8,128)(2,1)S(1)} collective-permute-done((bf16[1152,128]{1,0:T(8,128)(2,1)S(1)}, bf16[1152,128]{1,0:T(8,128)(2,1)S(1)}, u32[]{:S(2)}, u32[]{:S(2)}) %collective-permute-start.3) | collective-permute-done | bytes 294944 | tf_op jit(solution)/shard_map/ppermute | solution.py:364
  54.4 0.0 collective-permute-done.refs_0_
  54.4 0.0 collective-permute-done.6.refs_6_
  54.4 1.4 %attend.2 = (bf16[400,128]{1,0:T(8,128)(2,1)S(1)}, bf16[400,128]{1,0:T(8,128)(2,1)S(1)}, bf16[400,128]{1,0:T(8,128)(2,1)S(1)}, bf16[400,128]{1,0:T(8,128)(2,1)S(...) custom-call(bf16[1152,128]{1,0:T(8,128)(2,1)S(1)} %collective-permute-done.refs_0_, ...), custom_call_target="tpu_custom_call" | custom-call | flops 603979776 | bytes 2359296 | tf_op jit(solution)/shard_map/attend/pallas_call | solution.py:267
  55.7 0.2 collective-permute-start.11
  55.9 2.5 %collective-permute-start.12 = (bf16[400,128]{1,0:T(8,128)(2,1)S(1)}, bf16[400,128]{1,0:T(8,128)(2,1)S(1)}, u32[]{:S(2)}, u32[]{:S(2)}) collective-permute-start(bf16[400,128]{1,0:T(8,128)(2,1)S(1)} %get-tuple-element.70), channel_id=1, source_target_pairs={{0,20},{4,16},{8,28},{12,24},{16,4},{20,0},{24,12},{28,8},{1,21},{... | collective-permute-start | bytes 307208 | tf_op jit(solution)/shard_map/ppermute | solution.py:364
  58.5 0.4 collective-permute-start.13
  58.9 0.0 collective-permute-done.7.refs_8_
  58.9 0.4 collective-permute-start.14
  59.2 0.0 collective-permute-done.8.refs_9_
  59.2 1.1 %collective-permute-start.15 = (bf16[400,128]{1,0:T(8,128)(2,1)S(1)}, bf16[400,128]{1,0:T(8,128)(2,1)S(1)}, u32[]{:S(2)}, u32[]{:S(2)}) collective-permute-start(bf16[400,128]{1,0:T(8,128)(2,1)S(1)} %get-tuple-element.74), channel_id=1, source_target_pairs={{0,12},{4,8},{8,4},{12,0},{16,28},{20,24},{24,20},{28,16},{1,13},{... | collective-permute-start | bytes 307208 | tf_op jit(solution)/shard_map/ppermute | solution.py:364
  60.4 0.9 %attend.3 = (bf16[400,128]{1,0:T(8,128)(2,1)S(1)}, bf16[400,128]{1,0:T(8,128)(2,1)S(1)}) custom-call(bf16[1152,128]{1,0:T(8,128)(2,1)S(1)} %collective-permute-done.refs_0_, bf16[1152,128]{1,0:T(8,128)(2,1)S(1)} %collective-permute-done.1.refs_1_, bf16[1152,128]{1,0:T(8,128)(2,1)S(1)} %collective-permute-done.2.refs_2_, ...), custom_call_target="tpu_custom_call" | custom-call | flops 603979776 | bytes 2359296 | tf_op jit(solution)/shard_map/attend/pallas_call | solution.py:267
  61.2 5.1 %collective-permute-done.11.refs_0_ = bf16[400,128]{1,0:T(8,128)(2,1)S(1)} collective-permute-done((bf16[400,128]{1,0:T(8,128)(2,1)S(1)}, bf16[400,128]{1,0:T(8,128)(2,1)S(1)}, u32[]{:S(2)}, u32[]{:S(2)}) %collective-permute-start.11) | collective-permute-done | bytes 102432 | tf_op jit(solution)/shard_map/ppermute | solution.py:364
  66.4 2.0 %collective-permute-start.9 = (bf16[400,128]{1,0:T(8,128)(2,1)S(1)}, bf16[400,128]{1,0:T(8,128)(2,1)S(1)}, u32[]{:S(2)}, u32[]{:S(2)}) collective-permute-start(bf16[400,128]{1,0:T(8,128)(2,1)S(1)} %get-tuple-element.77), channel_id=1, source_target_pairs={{0,24},{4,28},{8,16},{12,20},{16,8},{20,12},{24,0},{28,4},{1,25},{... | collective-permute-start | bytes 307208 | tf_op jit(solution)/shard_map/ppermute | solution.py:364
  68.3 0.1 collective-permute-done.12.refs_1_
  68.5 1.4 %collective-permute-start.10 = (bf16[400,128]{1,0:T(8,128)(2,1)S(1)}, bf16[400,128]{1,0:T(8,128)(2,1)S(1)}, u32[]{:S(2)}, u32[]{:S(2)}) collective-permute-start(bf16[400,128]{1,0:T(8,128)(2,1)S(1)} %get-tuple-element.78), channel_id=1, source_target_pairs={{0,28},{4,24},{8,20},{12,16},{16,12},{20,8},{24,4},{28,0},{1,29},{... | collective-permute-start | bytes 307208 | tf_op jit(solution)/shard_map/ppermute | solution.py:364
  69.9 0.0 collective-permute-done.13.refs_2_
  69.9 0.0 collective-permute-done.14.refs_4_
  69.9 0.0 collective-permute-done.15.refs_5_
  69.9 1.5 %collect.2.refs_2_ = bf16[32,8,1536]{2,1,0:T(8,128)(2,1)} custom-call(s32[1]{0:T(128)} %bitcast.me_ref, f32[3072,128]{1,0:T(8,128)S(1)} %get-tuple-element.57.mem_ref, f32[128,128]{1,0:T(8,128)S(1)} %get-tuple-element.58.lse_ref, bf16[400,128]{1,0:T(8,128)(2,1)S(1)} %collective-permute-done.11.refs_0_, bf16[400,128]{1,0:T(8,128)(2,1)S(1)} %collective-permute-done.12.refs_1_, ...), custom_call_target="tpu_custom_call" | custom-call | tf_op jit(solution)/shard_map/collect/pallas_call | solution.py:346
  71.5 1.6 %collective-permute-done.9.refs_0_ = bf16[400,128]{1,0:T(8,128)(2,1)S(1)} collective-permute-done((bf16[400,128]{1,0:T(8,128)(2,1)S(1)}, bf16[400,128]{1,0:T(8,128)(2,1)S(1)}, u32[]{:S(2)}, u32[]{:S(2)}) %collective-permute-start.9) | collective-permute-done | bytes 102432 | tf_op jit(solution)/shard_map/ppermute | solution.py:364
  73.0 2.2 %collective-permute-done.10.refs_1_ = bf16[400,128]{1,0:T(8,128)(2,1)S(1)} collective-permute-done((bf16[400,128]{1,0:T(8,128)(2,1)S(1)}, bf16[400,128]{1,0:T(8,128)(2,1)S(1)}, u32[]{:S(2)}, u32[]{:S(2)}) %collective-permute-start.10) | collective-permute-done | bytes 102432 | tf_op jit(solution)/shard_map/ppermute | solution.py:364
  75.3 1.1 %collect.3 = bf16[32,8,1536]{2,1,0:T(8,128)(2,1)} custom-call(s32[1]{0:T(128)} %bitcast.me_ref, f32[3072,128]{1,0:T(8,128)S(1)} %get-tuple-element.57.mem_ref, f32[128,128]{1,0:T(8,128)S(1)} %get-tuple-element.58.lse_ref, bf16[400,128]{1,0:T(8,128)(2,1)S(1)} %collective-permute-done.9.refs_0_, ...), custom_call_target="tpu_custom_call", output_to_operand_aliasing={{}: (5, {})} | custom-call | tf_op jit(solution)/shard_map/collect/pallas_call | solution.py:346
  (3 shorter events, 0.1 us)
Async XLA Ops:
  1.6 34.2 %collective-permute-start.1 = (bf16[1152,128]{1,0:T(8,128)(2,1)S(1)}, bf16[1152,128]{1,0:T(8,128)(2,1)S(1)}, u32[]{:S(2)}, u32[]{:S(2)}) collective-permute-start(bf16[1152,128]{1,0:T(8,128)(2,1)S(1)} %get-tuple-element.43), channel_id=1, source_target_pairs={{0,12},{4,8},{8,4},{12,0},{16,28},{20,24},{24,20},{28,16},{1,13},{... | collective-permute-start | bytes 884744 | tf_op jit(solution)/shard_map/ppermute | solution.py:364
  4.1 32.9 %collective-permute-start.2 = (bf16[1152,128]{1,0:T(8,128)(2,1)S(1)}, bf16[1152,128]{1,0:T(8,128)(2,1)S(1)}, u32[]{:S(2)}, u32[]{:S(2)}) collective-permute-start(bf16[1152,128]{1,0:T(8,128)(2,1)S(1)} %get-tuple-element.44), channel_id=1, source_target_pairs={{0,16},{4,20},{8,24},{12,28},{16,0},{20,4},{24,8},{28,12},{1,17},{... | collective-permute-start | bytes 884744 | tf_op jit(solution)/shard_map/ppermute | solution.py:364
  6.7 15.0 %copy-start = (f32[12]{0:T(128)S(1)}, f32[12]{0:T(128)}, u32[]{:S(2)}) copy-start(f32[12]{0:T(128)} %bias_ref.1) | copy-start | bytes 148
  6.7 47.7 %collective-permute-start = (bf16[1152,128]{1,0:T(8,128)(2,1)S(1)}, bf16[1152,128]{1,0:T(8,128)(2,1)S(1)}, u32[]{:S(2)}, u32[]{:S(2)}) collective-permute-start(bf16[1152,128]{1,0:T(8,128)(2,1)S(1)} %get-tuple-element.42), channel_id=1, source_target_pairs={{0,8},{4,12},{8,0},{12,4},{16,24},{20,28},{24,16},{28,20},{1,9},{5... | collective-permute-start | bytes 884744 | tf_op jit(solution)/shard_map/ppermute | solution.py:364
  8.5 22.8 %collective-permute-start.5 = (bf16[768,128]{1,0:T(8,128)(2,1)S(1)}, bf16[768,128]{1,0:T(8,128)(2,1)S(1)}, u32[]{:S(2)}, u32[]{:S(2)}) collective-permute-start(bf16[768,128]{1,0:T(8,128)(2,1)S(1)} %get-tuple-element.48), channel_id=1, source_target_pairs={{0,28},{4,24},{8,20},{12,16},{16,12},{20,8},{24,4},{28,0},{1,29},{... | collective-permute-start | bytes 589832 | tf_op jit(solution)/shard_map/ppermute | solution.py:364
  9.5 26.3 %collective-permute-start.4 = (bf16[768,128]{1,0:T(8,128)(2,1)S(1)}, bf16[768,128]{1,0:T(8,128)(2,1)S(1)}, u32[]{:S(2)}, u32[]{:S(2)}) collective-permute-start(bf16[768,128]{1,0:T(8,128)(2,1)S(1)} %get-tuple-element.47), channel_id=1, source_target_pairs={{0,24},{4,28},{8,16},{12,20},{16,8},{20,12},{24,0},{28,4},{1,25},{... | collective-permute-start | bytes 589832 | tf_op jit(solution)/shard_map/ppermute | solution.py:364
  31.3 23.1 %collective-permute-start.3 = (bf16[1152,128]{1,0:T(8,128)(2,1)S(1)}, bf16[1152,128]{1,0:T(8,128)(2,1)S(1)}, u32[]{:S(2)}, u32[]{:S(2)}) collective-permute-start(bf16[1152,128]{1,0:T(8,128)(2,1)S(1)} %get-tuple-element.45), channel_id=1, source_target_pairs={{0,20},{4,16},{8,28},{12,24},{16,4},{20,0},{24,12},{28,8},{1,21},{... | collective-permute-start | bytes 884744 | tf_op jit(solution)/shard_map/ppermute | solution.py:364
  35.8 18.6 %collective-permute-start.6 = (bf16[1152,128]{1,0:T(8,128)(2,1)S(1)}, bf16[1152,128]{1,0:T(8,128)(2,1)S(1)}, u32[]{:S(2)}, u32[]{:S(2)}) collective-permute-start(bf16[1152,128]{1,0:T(8,128)(2,1)S(1)} %get-tuple-element.53), channel_id=1, source_target_pairs={{0,4},{4,0},{8,12},{12,8},{16,20},{20,16},{24,28},{28,24},{1,5},{5... | collective-permute-start | bytes 884744 | tf_op jit(solution)/shard_map/ppermute | solution.py:364
  35.8 23.1 %collective-permute-start.7 = (bf16[384,128]{1,0:T(8,128)(2,1)S(1)}, bf16[384,128]{1,0:T(8,128)(2,1)S(1)}, u32[]{:S(2)}, u32[]{:S(2)}) collective-permute-start(bf16[384,128]{1,0:T(8,128)(2,1)S(1)} %get-tuple-element.67), channel_id=1, source_target_pairs={{0,24},{4,28},{8,16},{12,20},{16,8},{20,12},{24,0},{28,4},{1,25},{... | collective-permute-start | bytes 294920 | tf_op jit(solution)/shard_map/ppermute | solution.py:364
  37.1 22.2 %collective-permute-start.8 = (bf16[384,128]{1,0:T(8,128)(2,1)S(1)}, bf16[384,128]{1,0:T(8,128)(2,1)S(1)}, u32[]{:S(2)}, u32[]{:S(2)}) collective-permute-start(bf16[384,128]{1,0:T(8,128)(2,1)S(1)} %get-tuple-element.68), channel_id=1, source_target_pairs={{0,28},{4,24},{8,20},{12,16},{16,12},{20,8},{24,4},{28,0},{1,29},{... | collective-permute-start | bytes 294920 | tf_op jit(solution)/shard_map/ppermute | solution.py:364
  55.7 10.6 %collective-permute-start.11 = (bf16[400,128]{1,0:T(8,128)(2,1)S(1)}, bf16[400,128]{1,0:T(8,128)(2,1)S(1)}, u32[]{:S(2)}, u32[]{:S(2)}) collective-permute-start(bf16[400,128]{1,0:T(8,128)(2,1)S(1)} %get-tuple-element.69), channel_id=1, source_target_pairs={{0,16},{4,20},{8,24},{12,28},{16,0},{20,4},{24,8},{28,12},{1,17},{... | collective-permute-start | bytes 307208 | tf_op jit(solution)/shard_map/ppermute | solution.py:364
  55.9 12.5 %collective-permute-start.12 = (bf16[400,128]{1,0:T(8,128)(2,1)S(1)}, bf16[400,128]{1,0:T(8,128)(2,1)S(1)}, u32[]{:S(2)}, u32[]{:S(2)}) collective-permute-start(bf16[400,128]{1,0:T(8,128)(2,1)S(1)} %get-tuple-element.70), channel_id=1, source_target_pairs={{0,20},{4,16},{8,28},{12,24},{16,4},{20,0},{24,12},{28,8},{1,21},{... | collective-permute-start | bytes 307208 | tf_op jit(solution)/shard_map/ppermute | solution.py:364
  58.5 11.4 %collective-permute-start.13 = (bf16[400,128]{1,0:T(8,128)(2,1)S(1)}, bf16[400,128]{1,0:T(8,128)(2,1)S(1)}, u32[]{:S(2)}, u32[]{:S(2)}) collective-permute-start(bf16[400,128]{1,0:T(8,128)(2,1)S(1)} %get-tuple-element.71), channel_id=1, source_target_pairs={{0,4},{4,0},{8,12},{12,8},{16,20},{20,16},{24,28},{28,24},{1,5},{5... | collective-permute-start | bytes 307208 | tf_op jit(solution)/shard_map/ppermute | solution.py:364
  58.9 11.1 %collective-permute-start.14 = (bf16[400,128]{1,0:T(8,128)(2,1)S(1)}, bf16[400,128]{1,0:T(8,128)(2,1)S(1)}, u32[]{:S(2)}, u32[]{:S(2)}) collective-permute-start(bf16[400,128]{1,0:T(8,128)(2,1)S(1)} %get-tuple-element.73), channel_id=1, source_target_pairs={{0,8},{4,12},{8,0},{12,4},{16,24},{20,28},{24,16},{28,20},{1,9},{5... | collective-permute-start | bytes 307208 | tf_op jit(solution)/shard_map/ppermute | solution.py:364
  59.2 10.7 %collective-permute-start.15 = (bf16[400,128]{1,0:T(8,128)(2,1)S(1)}, bf16[400,128]{1,0:T(8,128)(2,1)S(1)}, u32[]{:S(2)}, u32[]{:S(2)}) collective-permute-start(bf16[400,128]{1,0:T(8,128)(2,1)S(1)} %get-tuple-element.74), channel_id=1, source_target_pairs={{0,12},{4,8},{8,4},{12,0},{16,28},{20,24},{24,20},{28,16},{1,13},{... | collective-permute-start | bytes 307208 | tf_op jit(solution)/shard_map/ppermute | solution.py:364
  66.4 6.7 %collective-permute-start.9 = (bf16[400,128]{1,0:T(8,128)(2,1)S(1)}, bf16[400,128]{1,0:T(8,128)(2,1)S(1)}, u32[]{:S(2)}, u32[]{:S(2)}) collective-permute-start(bf16[400,128]{1,0:T(8,128)(2,1)S(1)} %get-tuple-element.77), channel_id=1, source_target_pairs={{0,24},{4,28},{8,16},{12,20},{16,8},{20,12},{24,0},{28,4},{1,25},{... | collective-permute-start | bytes 307208 | tf_op jit(solution)/shard_map/ppermute | solution.py:364
  68.5 6.8 %collective-permute-start.10 = (bf16[400,128]{1,0:T(8,128)(2,1)S(1)}, bf16[400,128]{1,0:T(8,128)(2,1)S(1)}, u32[]{:S(2)}, u32[]{:S(2)}) collective-permute-start(bf16[400,128]{1,0:T(8,128)(2,1)S(1)} %get-tuple-element.78), channel_id=1, source_target_pairs={{0,28},{4,24},{8,20},{12,16},{16,12},{20,8},{24,4},{28,0},{1,29},{... | collective-permute-start | bytes 307208 | tf_op jit(solution)/shard_map/ppermute | solution.py:364

commit v8 on v6

--- a/solution.py
+++ b/solution.py
@@ -79,19 +79,21 @@
     loads = {}
     for i, (kg, kinds) in enumerate(parts):
         for n, kind in enumerate(kinds):
-            loads[i, n] = pltpu.make_async_copy(
-                args[kind].at[:, :, pl.ds(dims.lane(me, kg), dims.width)],
-                raws[i].at[n],
-                sems.at[i, n],
-            )
-            loads[i, n].start()
+            for j in range(dims.heads_g):
+                lane = pl.multiple_of(dims.lane(me, kg) + j * head_dim, 128)
+                loads[i, n, j] = pltpu.make_async_copy(
+                    args[kind].at[:, :, pl.ds(lane, head_dim)],
+                    raws[i].at[n, :, :, pl.ds(j * head_dim, head_dim)],
+                    sems.at[i, n, j],
+                )
+                loads[i, n, j].start()
     slot = 0
     for i, (kg, kinds) in enumerate(parts):
         ks = dims.partners(kg)
         mine, outs = outs[: len(ks)], outs[len(ks) :]
         for n, kind in enumerate(kinds):
-            loads[i, n].wait()
             for j in range(dims.heads_g):
+                loads[i, n, j].wait()
                 wide[slot] = (
                     raws[i][n, :, :, j * head_dim : (j + 1) * head_dim]
                     .astype(jnp.float32)
@@ -124,7 +126,7 @@
         ]
         + [
             pltpu.VMEM((4, dims.patches, dims.head_dim), jnp.float32),
-            pltpu.SemaphoreType.DMA((len(parts), 3)),
+            pltpu.SemaphoreType.DMA((len(parts), 3, dims.heads_g)),
         ],
         compiler_params=PARAMS,
         name="spread",

time: 76.7 us -> 76.8 us (level)
  no operation moved by 1% of the time
where the time goes in v8:
time: 76.8 us; the launch traced here: 76.5 us
  waiting for transfers between devices  32.5 us (42%)
  starting transfers between devices  20.9 us (27%)
  Pallas kernels  14.7 us (19%)
  blocking collectives  8.17 us (11%)
    ppermute x16, waiting for transfers between devices, exchange(): lax.ppermute(block, 'row', [(i, i ^ k) for i in range(dims.n_row)])  32.5 us
    ppermute x16, starting transfers between devices, exchange(): lax.ppermute(block, 'row', [(i, i ^ k) for i in range(dims.n_row)])  20.9 us
    all_gather x1, blocking collectives, per_device(): band = lax.all_gather(pooled[None], 'col', axis=0, tiled=True)  8.17 us
    pallas_call x3, Pallas kernels, spread(): pl.pallas_call(functools.partial(spread_kernel, dims, parts), out_shape=[...  4.2 us
    pallas_call x1, Pallas kernels, recall(): pl.pallas_call(functools.partial(recall_kernel, dims), out_shape=[out, ta...  4.11 us
    pallas_call x2, Pallas kernels, collect(): pl.pallas_call(functools.partial(collect_kernel, dims, kgs), out_shape=ja...  2.67 us
    pallas_call x2, Pallas kernels, attend(): pl.pallas_call(functools.partial(attend_kernel, dims, ks, keys), out_shap...  2.23 us
  transfers between devices with their start and end apart: 16, of which 7 were waited for; matrix products, arithmetic and copies ran while one was open for 0% of the time, Pallas kernels for 16%

profile of v8, /device:TPU:0, one launch (start us, length us, event | category | flops | bytes accessed | tf_op | source)
XLA Modules:
  0.0 76.5 jit_solution(10946617389193222883)
XLA Ops:
  0.0 1.6 %spread.3 = (bf16[1152,128]{1,0:T(8,128)(2,1)S(1)}, bf16[1152,128]{1,0:T(8,128)(2,1)S(1)}, bf16[1152,128]{1,0:T(8,128)(2,1)S(1)}, bf16[1152,128]{1,0:T(8,128)(2,1)S(1)}) custom-call(s32[1]{0:T(128)} %bitcast.me_ref, bf16[32,8,1536]{2,1,0:T(8,128)(2,1)} %refs_0_.5, bf16[32,8,1536]{2,1,0:T(8,128)(2,1)} %refs_1_.5, bf16[32,8,1536]{2,1,0:T(8,128)(2,1)} %refs_2_.5), custom_call_target="tpu_custom_call" | custom-call | tf_op jit(solution)/shard_map/spread/pallas_call | solution.py:115
  1.6 2.5 %collective-permute-start.1 = (bf16[1152,128]{1,0:T(8,128)(2,1)S(1)}, bf16[1152,128]{1,0:T(8,128)(2,1)S(1)}, u32[]{:S(2)}, u32[]{:S(2)}) collective-permute-start(bf16[1152,128]{1,0:T(8,128)(2,1)S(1)} %get-tuple-element.43), channel_id=1, source_target_pairs={{0,12},{4,8},{8,4},{12,0},{16,28},{20,24},{24,20},{28,16},{1,13},{... | collective-permute-start | bytes 884744 | tf_op jit(solution)/shard_map/ppermute | solution.py:366
  4.2 2.6 %collective-permute-start.2 = (bf16[1152,128]{1,0:T(8,128)(2,1)S(1)}, bf16[1152,128]{1,0:T(8,128)(2,1)S(1)}, u32[]{:S(2)}, u32[]{:S(2)}) collective-permute-start(bf16[1152,128]{1,0:T(8,128)(2,1)S(1)} %get-tuple-element.44), channel_id=1, source_target_pairs={{0,16},{4,20},{8,24},{12,28},{16,0},{20,4},{24,8},{28,12},{1,17},{... | collective-permute-start | bytes 884744 | tf_op jit(solution)/shard_map/ppermute | solution.py:366
  6.8 0.0 copy-start
  6.8 0.6 collective-permute-start
  7.4 1.5 %spread.4 = (bf16[768,128]{1,0:T(8,128)(2,1)S(1)}, bf16[768,128]{1,0:T(8,128)(2,1)S(1)}, bf16[1152,128]{1,0:T(8,128)(2,1)S(1)}, bf16[1152,128]{1,0:T(8,128)(2,1)S(1)}) custom-call(s32[1]{0:T(128)} %bitcast.me_ref, bf16[32,8,1536]{2,1,0:T(8,128)(2,1)} %refs_0_.5, bf16[32,8,1536]{2,1,0:T(8,128)(2,1)} %refs_1_.5, bf16[32,8,1536]{2,1,0:T(8,128)(2,1)} %refs_2_.5), custom_call_target="tpu_custom_call" | custom-call | tf_op jit(solution)/shard_map/spread/pallas_call | solution.py:115
  8.9 1.0 %collective-permute-start.5 = (bf16[768,128]{1,0:T(8,128)(2,1)S(1)}, bf16[768,128]{1,0:T(8,128)(2,1)S(1)}, u32[]{:S(2)}, u32[]{:S(2)}) collective-permute-start(bf16[768,128]{1,0:T(8,128)(2,1)S(1)} %get-tuple-element.48), channel_id=1, source_target_pairs={{0,28},{4,24},{8,20},{12,16},{16,12},{20,8},{24,4},{28,0},{1,29},{... | collective-permute-start | bytes 589832 | tf_op jit(solution)/shard_map/ppermute | solution.py:366
  9.9 2.4 %collective-permute-start.4 = (bf16[768,128]{1,0:T(8,128)(2,1)S(1)}, bf16[768,128]{1,0:T(8,128)(2,1)S(1)}, u32[]{:S(2)}, u32[]{:S(2)}) collective-permute-start(bf16[768,128]{1,0:T(8,128)(2,1)S(1)} %get-tuple-element.47), channel_id=1, source_target_pairs={{0,24},{4,28},{8,16},{12,20},{16,8},{20,12},{24,0},{28,4},{1,25},{... | collective-permute-start | bytes 589832 | tf_op jit(solution)/shard_map/ppermute | solution.py:366
  12.4 1.5 %pool.1 = f32[2,1536]{1,0:T(2,128)S(1)} custom-call(bf16[32,8,1536]{2,1,0:T(8,128)(2,1)} %refs_1_.5, bf16[32,8,1536]{2,1,0:T(8,128)(2,1)} %refs_2_.5), custom_call_target="tpu_custom_call" | custom-call | tf_op jit(solution)/shard_map/pool/pallas_call | solution.py:153
  13.9 8.2 %all-gather.1 = bf16[4,2,1536]{2,1,0:T(2,128)(2,1)S(1)} all-gather(bf16[1,2,1536]{2,1,0:T(2,128)(2,1)S(1)} %convert_bitcast_fusion), channel_id=2, replica_groups=mesh['row'=8,'col'=4] {'col'}, dimensions={0}, use_global_device_ids=true | all-gather | bytes 30720 | tf_op jit(solution)/shard_map/all_gather | solution.py:405
  22.1 9.3 %collective-permute-done.5.refs_5_ = bf16[768,128]{1,0:T(8,128)(2,1)S(1)} collective-permute-done((bf16[768,128]{1,0:T(8,128)(2,1)S(1)}, bf16[768,128]{1,0:T(8,128)(2,1)S(1)}, u32[]{:S(2)}, u32[]{:S(2)}) %collective-permute-start.5) | collective-permute-done | bytes 196640 | tf_op jit(solution)/shard_map/ppermute | solution.py:366
  31.4 0.0 collective-permute-start.3
  31.4 4.5 %collective-permute-done.4.refs_4_ = bf16[768,128]{1,0:T(8,128)(2,1)S(1)} collective-permute-done((bf16[768,128]{1,0:T(8,128)(2,1)S(1)}, bf16[768,128]{1,0:T(8,128)(2,1)S(1)}, u32[]{:S(2)}, u32[]{:S(2)}) %collective-permute-start.4) | collective-permute-done | bytes 196640 | tf_op jit(solution)/shard_map/ppermute | solution.py:366
  35.8 0.0 collective-permute-start.6
  35.9 0.0 copy-done
  35.9 4.1 %recall.1 = (f32[3072,128]{1,0:T(8,128)S(1)}, f32[128,128]{1,0:T(8,128)S(1)}) custom-call(s32[1]{0:T(128)} %bitcast.me_ref, f32[12]{0:T(128)S(1)} %copy-done, bf16[32,8,1536]{2,1,0:T(8,128)(2,1)} %refs_0_.5, bf16[4,1536]{1,0:T(4,128)(2,1)S(1)} %get-tuple-element.82.key_ref, bf16[4,1536]{1,0:T(4,128)(2,1)S(1)} %get-tuple-element.81.value_ref), custom_call_target="tpu_custom_call" | custom-call | tf_op jit(solution)/shard_map/recall/pallas_call | solution.py:211
  40.0 1.0 %spread.5 = (bf16[384,128]{1,0:T(8,128)(2,1)S(1)}, bf16[384,128]{1,0:T(8,128)(2,1)S(1)}) custom-call(s32[1]{0:T(128)} %bitcast.me_ref, bf16[32,8,1536]{2,1,0:T(8,128)(2,1)} %refs_0_.5, bf16[32,8,1536]{2,1,0:T(8,128)(2,1)} %refs_1_.5, bf16[32,8,1536]{2,1,0:T(8,128)(2,1)} %refs_2_.5), custom_call_target="tpu_custom_call" | custom-call | tf_op jit(solution)/shard_map/spread/pallas_call | solution.py:115
  41.0 0.0 collective-permute-done.1.refs_1_
  41.0 1.3 %collective-permute-start.7 = (bf16[384,128]{1,0:T(8,128)(2,1)S(1)}, bf16[384,128]{1,0:T(8,128)(2,1)S(1)}, u32[]{:S(2)}, u32[]{:S(2)}) collective-permute-start(bf16[384,128]{1,0:T(8,128)(2,1)S(1)} %get-tuple-element.67), channel_id=1, source_target_pairs={{0,24},{4,28},{8,16},{12,20},{16,8},{20,12},{24,0},{28,4},{1,25},{... | collective-permute-start | bytes 294920 | tf_op jit(solution)/shard_map/ppermute | solution.py:366
  42.4 0.0 collective-permute-done.2.refs_2_
  42.4 2.4 %collective-permute-start.8 = (bf16[384,128]{1,0:T(8,128)(2,1)S(1)}, bf16[384,128]{1,0:T(8,128)(2,1)S(1)}, u32[]{:S(2)}, u32[]{:S(2)}) collective-permute-start(bf16[384,128]{1,0:T(8,128)(2,1)S(1)} %get-tuple-element.68), channel_id=1, source_target_pairs={{0,28},{4,24},{8,20},{12,16},{16,12},{20,8},{24,4},{28,0},{1,29},{... | collective-permute-start | bytes 294920 | tf_op jit(solution)/shard_map/ppermute | solution.py:366
  44.8 9.7 %collective-permute-done.3.refs_3_ = bf16[1152,128]{1,0:T(8,128)(2,1)S(1)} collective-permute-done((bf16[1152,128]{1,0:T(8,128)(2,1)S(1)}, bf16[1152,128]{1,0:T(8,128)(2,1)S(1)}, u32[]{:S(2)}, u32[]{:S(2)}) %collective-permute-start.3) | collective-permute-done | bytes 294944 | tf_op jit(solution)/shard_map/ppermute | solution.py:366
  54.4 0.0 collective-permute-done.refs_0_
  54.4 0.0 collective-permute-done.6.refs_6_
  54.5 1.4 %attend.2 = (bf16[400,128]{1,0:T(8,128)(2,1)S(1)}, bf16[400,128]{1,0:T(8,128)(2,1)S(1)}, bf16[400,128]{1,0:T(8,128)(2,1)S(1)}, bf16[400,128]{1,0:T(8,128)(2,1)S(...) custom-call(bf16[1152,128]{1,0:T(8,128)(2,1)S(1)} %collective-permute-done.refs_0_, ...), custom_call_target="tpu_custom_call" | custom-call | flops 603979776 | bytes 2359296 | tf_op jit(solution)/shard_map/attend/pallas_call | solution.py:269
  55.8 0.2 collective-permute-start.11
  56.0 2.5 %collective-permute-start.12 = (bf16[400,128]{1,0:T(8,128)(2,1)S(1)}, bf16[400,128]{1,0:T(8,128)(2,1)S(1)}, u32[]{:S(2)}, u32[]{:S(2)}) collective-permute-start(bf16[400,128]{1,0:T(8,128)(2,1)S(1)} %get-tuple-element.70), channel_id=1, source_target_pairs={{0,20},{4,16},{8,28},{12,24},{16,4},{20,0},{24,12},{28,8},{1,21},{... | collective-permute-start | bytes 307208 | tf_op jit(solution)/shard_map/ppermute | solution.py:366
  58.6 0.4 collective-permute-start.13
  58.9 0.0 collective-permute-done.7.refs_8_
  58.9 0.4 collective-permute-start.14
  59.3 0.0 collective-permute-done.8.refs_9_
  59.3 1.1 %collective-permute-start.15 = (bf16[400,128]{1,0:T(8,128)(2,1)S(1)}, bf16[400,128]{1,0:T(8,128)(2,1)S(1)}, u32[]{:S(2)}, u32[]{:S(2)}) collective-permute-start(bf16[400,128]{1,0:T(8,128)(2,1)S(1)} %get-tuple-element.74), channel_id=1, source_target_pairs={{0,12},{4,8},{8,4},{12,0},{16,28},{20,24},{24,20},{28,16},{1,13},{... | collective-permute-start | bytes 307208 | tf_op jit(solution)/shard_map/ppermute | solution.py:366
  60.4 0.9 %attend.3 = (bf16[400,128]{1,0:T(8,128)(2,1)S(1)}, bf16[400,128]{1,0:T(8,128)(2,1)S(1)}) custom-call(bf16[1152,128]{1,0:T(8,128)(2,1)S(1)} %collective-permute-done.refs_0_, bf16[1152,128]{1,0:T(8,128)(2,1)S(1)} %collective-permute-done.1.refs_1_, bf16[1152,128]{1,0:T(8,128)(2,1)S(1)} %collective-permute-done.2.refs_2_, ...), custom_call_target="tpu_custom_call" | custom-call | flops 603979776 | bytes 2359296 | tf_op jit(solution)/shard_map/attend/pallas_call | solution.py:269
  61.3 5.1 %collective-permute-done.11.refs_0_ = bf16[400,128]{1,0:T(8,128)(2,1)S(1)} collective-permute-done((bf16[400,128]{1,0:T(8,128)(2,1)S(1)}, bf16[400,128]{1,0:T(8,128)(2,1)S(1)}, u32[]{:S(2)}, u32[]{:S(2)}) %collective-permute-start.11) | collective-permute-done | bytes 102432 | tf_op jit(solution)/shard_map/ppermute | solution.py:366
  66.5 2.0 %collective-permute-start.9 = (bf16[400,128]{1,0:T(8,128)(2,1)S(1)}, bf16[400,128]{1,0:T(8,128)(2,1)S(1)}, u32[]{:S(2)}, u32[]{:S(2)}) collective-permute-start(bf16[400,128]{1,0:T(8,128)(2,1)S(1)} %get-tuple-element.77), channel_id=1, source_target_pairs={{0,24},{4,28},{8,16},{12,20},{16,8},{20,12},{24,0},{28,4},{1,25},{... | collective-permute-start | bytes 307208 | tf_op jit(solution)/shard_map/ppermute | solution.py:366
  68.4 0.1 collective-permute-done.12.refs_1_
  68.6 1.4 %collective-permute-start.10 = (bf16[400,128]{1,0:T(8,128)(2,1)S(1)}, bf16[400,128]{1,0:T(8,128)(2,1)S(1)}, u32[]{:S(2)}, u32[]{:S(2)}) collective-permute-start(bf16[400,128]{1,0:T(8,128)(2,1)S(1)} %get-tuple-element.78), channel_id=1, source_target_pairs={{0,28},{4,24},{8,20},{12,16},{16,12},{20,8},{24,4},{28,0},{1,29},{... | collective-permute-start | bytes 307208 | tf_op jit(solution)/shard_map/ppermute | solution.py:366
  70.0 0.0 collective-permute-done.13.refs_2_
  70.0 0.0 collective-permute-done.14.refs_4_
  70.0 0.0 collective-permute-done.15.refs_5_
  70.0 1.5 %collect.2.refs_2_ = bf16[32,8,1536]{2,1,0:T(8,128)(2,1)} custom-call(s32[1]{0:T(128)} %bitcast.me_ref, f32[3072,128]{1,0:T(8,128)S(1)} %get-tuple-element.56.mem_ref, f32[128,128]{1,0:T(8,128)S(1)} %get-tuple-element.57.lse_ref, bf16[400,128]{1,0:T(8,128)(2,1)S(1)} %collective-permute-done.11.refs_0_, bf16[400,128]{1,0:T(8,128)(2,1)S(1)} %collective-permute-done.12.refs_1_, ...), custom_call_target="tpu_custom_call" | custom-call | tf_op jit(solution)/shard_map/collect/pallas_call | solution.py:348
  71.5 1.6 %collective-permute-done.9.refs_0_ = bf16[400,128]{1,0:T(8,128)(2,1)S(1)} collective-permute-done((bf16[400,128]{1,0:T(8,128)(2,1)S(1)}, bf16[400,128]{1,0:T(8,128)(2,1)S(1)}, u32[]{:S(2)}, u32[]{:S(2)}) %collective-permute-start.9) | collective-permute-done | bytes 102432 | tf_op jit(solution)/shard_map/ppermute | solution.py:366
  73.1 2.2 %collective-permute-done.10.refs_1_ = bf16[400,128]{1,0:T(8,128)(2,1)S(1)} collective-permute-done((bf16[400,128]{1,0:T(8,128)(2,1)S(1)}, bf16[400,128]{1,0:T(8,128)(2,1)S(1)}, u32[]{:S(2)}, u32[]{:S(2)}) %collective-permute-start.10) | collective-permute-done | bytes 102432 | tf_op jit(solution)/shard_map/ppermute | solution.py:366
  75.3 1.1 %collect.3 = bf16[32,8,1536]{2,1,0:T(8,128)(2,1)} custom-call(s32[1]{0:T(128)} %bitcast.me_ref, f32[3072,128]{1,0:T(8,128)S(1)} %get-tuple-element.56.mem_ref, f32[128,128]{1,0:T(8,128)S(1)} %get-tuple-element.57.lse_ref, bf16[400,128]{1,0:T(8,128)(2,1)S(1)} %collective-permute-done.9.refs_0_, ...), custom_call_target="tpu_custom_call", output_to_operand_aliasing={{}: (5, {})} | custom-call | tf_op jit(solution)/shard_map/collect/pallas_call | solution.py:348
  (3 shorter events, 0.1 us)
Async XLA Ops:
  1.6 39.4 %collective-permute-start.1 = (bf16[1152,128]{1,0:T(8,128)(2,1)S(1)}, bf16[1152,128]{1,0:T(8,128)(2,1)S(1)}, u32[]{:S(2)}, u32[]{:S(2)}) collective-permute-start(bf16[1152,128]{1,0:T(8,128)(2,1)S(1)} %get-tuple-element.43), channel_id=1, source_target_pairs={{0,12},{4,8},{8,4},{12,0},{16,28},{20,24},{24,20},{28,16},{1,13},{... | collective-permute-start | bytes 884744 | tf_op jit(solution)/shard_map/ppermute | solution.py:366
  4.2 38.2 %collective-permute-start.2 = (bf16[1152,128]{1,0:T(8,128)(2,1)S(1)}, bf16[1152,128]{1,0:T(8,128)(2,1)S(1)}, u32[]{:S(2)}, u32[]{:S(2)}) collective-permute-start(bf16[1152,128]{1,0:T(8,128)(2,1)S(1)} %get-tuple-element.44), channel_id=1, source_target_pairs={{0,16},{4,20},{8,24},{12,28},{16,0},{20,4},{24,8},{28,12},{1,17},{... | collective-permute-start | bytes 884744 | tf_op jit(solution)/shard_map/ppermute | solution.py:366
  6.8 29.1 %copy-start = (f32[12]{0:T(128)S(1)}, f32[12]{0:T(128)}, u32[]{:S(2)}) copy-start(f32[12]{0:T(128)} %bias_ref.1) | copy-start | bytes 148
  6.8 47.7 %collective-permute-start = (bf16[1152,128]{1,0:T(8,128)(2,1)S(1)}, bf16[1152,128]{1,0:T(8,128)(2,1)S(1)}, u32[]{:S(2)}, u32[]{:S(2)}) collective-permute-start(bf16[1152,128]{1,0:T(8,128)(2,1)S(1)} %get-tuple-element.42), channel_id=1, source_target_pairs={{0,8},{4,12},{8,0},{12,4},{16,24},{20,28},{24,16},{28,20},{1,9},{5... | collective-permute-start | bytes 884744 | tf_op jit(solution)/shard_map/ppermute | solution.py:366
  8.9 22.4 %collective-permute-start.5 = (bf16[768,128]{1,0:T(8,128)(2,1)S(1)}, bf16[768,128]{1,0:T(8,128)(2,1)S(1)}, u32[]{:S(2)}, u32[]{:S(2)}) collective-permute-start(bf16[768,128]{1,0:T(8,128)(2,1)S(1)} %get-tuple-element.48), channel_id=1, source_target_pairs={{0,28},{4,24},{8,20},{12,16},{16,12},{20,8},{24,4},{28,0},{1,29},{... | collective-permute-start | bytes 589832 | tf_op jit(solution)/shard_map/ppermute | solution.py:366
  9.9 25.9 %collective-permute-start.4 = (bf16[768,128]{1,0:T(8,128)(2,1)S(1)}, bf16[768,128]{1,0:T(8,128)(2,1)S(1)}, u32[]{:S(2)}, u32[]{:S(2)}) collective-permute-start(bf16[768,128]{1,0:T(8,128)(2,1)S(1)} %get-tuple-element.47), channel_id=1, source_target_pairs={{0,24},{4,28},{8,16},{12,20},{16,8},{20,12},{24,0},{28,4},{1,25},{... | collective-permute-start | bytes 589832 | tf_op jit(solution)/shard_map/ppermute | solution.py:366
  31.4 23.1 %collective-permute-start.3 = (bf16[1152,128]{1,0:T(8,128)(2,1)S(1)}, bf16[1152,128]{1,0:T(8,128)(2,1)S(1)}, u32[]{:S(2)}, u32[]{:S(2)}) collective-permute-start(bf16[1152,128]{1,0:T(8,128)(2,1)S(1)} %get-tuple-element.45), channel_id=1, source_target_pairs={{0,20},{4,16},{8,28},{12,24},{16,4},{20,0},{24,12},{28,8},{1,21},{... | collective-permute-start | bytes 884744 | tf_op jit(solution)/shard_map/ppermute | solution.py:366
  35.8 18.6 %collective-permute-start.6 = (bf16[1152,128]{1,0:T(8,128)(2,1)S(1)}, bf16[1152,128]{1,0:T(8,128)(2,1)S(1)}, u32[]{:S(2)}, u32[]{:S(2)}) collective-permute-start(bf16[1152,128]{1,0:T(8,128)(2,1)S(1)} %get-tuple-element.49), channel_id=1, source_target_pairs={{0,4},{4,0},{8,12},{12,8},{16,20},{20,16},{24,28},{28,24},{1,5},{5... | collective-permute-start | bytes 884744 | tf_op jit(solution)/shard_map/ppermute | solution.py:366
  41.0 17.9 %collective-permute-start.7 = (bf16[384,128]{1,0:T(8,128)(2,1)S(1)}, bf16[384,128]{1,0:T(8,128)(2,1)S(1)}, u32[]{:S(2)}, u32[]{:S(2)}) collective-permute-start(bf16[384,128]{1,0:T(8,128)(2,1)S(1)} %get-tuple-element.67), channel_id=1, source_target_pairs={{0,24},{4,28},{8,16},{12,20},{16,8},{20,12},{24,0},{28,4},{1,25},{... | collective-permute-start | bytes 294920 | tf_op jit(solution)/shard_map/ppermute | solution.py:366
  42.4 16.9 %collective-permute-start.8 = (bf16[384,128]{1,0:T(8,128)(2,1)S(1)}, bf16[384,128]{1,0:T(8,128)(2,1)S(1)}, u32[]{:S(2)}, u32[]{:S(2)}) collective-permute-start(bf16[384,128]{1,0:T(8,128)(2,1)S(1)} %get-tuple-element.68), channel_id=1, source_target_pairs={{0,28},{4,24},{8,20},{12,16},{16,12},{20,8},{24,4},{28,0},{1,29},{... | collective-permute-start | bytes 294920 | tf_op jit(solution)/shard_map/ppermute | solution.py:366
  55.8 10.6 %collective-permute-start.11 = (bf16[400,128]{1,0:T(8,128)(2,1)S(1)}, bf16[400,128]{1,0:T(8,128)(2,1)S(1)}, u32[]{:S(2)}, u32[]{:S(2)}) collective-permute-start(bf16[400,128]{1,0:T(8,128)(2,1)S(1)} %get-tuple-element.69), channel_id=1, source_target_pairs={{0,16},{4,20},{8,24},{12,28},{16,0},{20,4},{24,8},{28,12},{1,17},{... | collective-permute-start | bytes 307208 | tf_op jit(solution)/shard_map/ppermute | solution.py:366
  56.0 12.5 %collective-permute-start.12 = (bf16[400,128]{1,0:T(8,128)(2,1)S(1)}, bf16[400,128]{1,0:T(8,128)(2,1)S(1)}, u32[]{:S(2)}, u32[]{:S(2)}) collective-permute-start(bf16[400,128]{1,0:T(8,128)(2,1)S(1)} %get-tuple-element.70), channel_id=1, source_target_pairs={{0,20},{4,16},{8,28},{12,24},{16,4},{20,0},{24,12},{28,8},{1,21},{... | collective-permute-start | bytes 307208 | tf_op jit(solution)/shard_map/ppermute | solution.py:366
  58.6 11.4 %collective-permute-start.13 = (bf16[400,128]{1,0:T(8,128)(2,1)S(1)}, bf16[400,128]{1,0:T(8,128)(2,1)S(1)}, u32[]{:S(2)}, u32[]{:S(2)}) collective-permute-start(bf16[400,128]{1,0:T(8,128)(2,1)S(1)} %get-tuple-element.71), channel_id=1, source_target_pairs={{0,4},{4,0},{8,12},{12,8},{16,20},{20,16},{24,28},{28,24},{1,5},{5... | collective-permute-start | bytes 307208 | tf_op jit(solution)/shard_map/ppermute | solution.py:366
  58.9 11.1 %collective-permute-start.14 = (bf16[400,128]{1,0:T(8,128)(2,1)S(1)}, bf16[400,128]{1,0:T(8,128)(2,1)S(1)}, u32[]{:S(2)}, u32[]{:S(2)}) collective-permute-start(bf16[400,128]{1,0:T(8,128)(2,1)S(1)} %get-tuple-element.73), channel_id=1, source_target_pairs={{0,8},{4,12},{8,0},{12,4},{16,24},{20,28},{24,16},{28,20},{1,9},{5... | collective-permute-start | bytes 307208 | tf_op jit(solution)/shard_map/ppermute | solution.py:366
  59.3 10.7 %collective-permute-start.15 = (bf16[400,128]{1,0:T(8,128)(2,1)S(1)}, bf16[400,128]{1,0:T(8,128)(2,1)S(1)}, u32[]{:S(2)}, u32[]{:S(2)}) collective-permute-start(bf16[400,128]{1,0:T(8,128)(2,1)S(1)} %get-tuple-element.74), channel_id=1, source_target_pairs={{0,12},{4,8},{8,4},{12,0},{16,28},{20,24},{24,20},{28,16},{1,13},{... | collective-permute-start | bytes 307208 | tf_op jit(solution)/shard_map/ppermute | solution.py:366
  66.5 6.7 %collective-permute-start.9 = (bf16[400,128]{1,0:T(8,128)(2,1)S(1)}, bf16[400,128]{1,0:T(8,128)(2,1)S(1)}, u32[]{:S(2)}, u32[]{:S(2)}) collective-permute-start(bf16[400,128]{1,0:T(8,128)(2,1)S(1)} %get-tuple-element.77), channel_id=1, source_target_pairs={{0,24},{4,28},{8,16},{12,20},{16,8},{20,12},{24,0},{28,4},{1,25},{... | collective-permute-start | bytes 307208 | tf_op jit(solution)/shard_map/ppermute | solution.py:366
  68.6 6.8 %collective-permute-start.10 = (bf16[400,128]{1,0:T(8,128)(2,1)S(1)}, bf16[400,128]{1,0:T(8,128)(2,1)S(1)}, u32[]{:S(2)}, u32[]{:S(2)}) collective-permute-start(bf16[400,128]{1,0:T(8,128)(2,1)S(1)} %get-tuple-element.78), channel_id=1, source_target_pairs={{0,28},{4,24},{8,20},{12,16},{16,12},{20,8},{24,4},{28,0},{1,29},{... | collective-permute-start | bytes 307208 | tf_op jit(solution)/shard_map/ppermute | solution.py:366
